TPU v7x, 32 devices: a whole 2x2x4 slice. The times are simulated.
32 devices in a mesh: dp: 4 (over y, x), ctx: 8 (over z, core).
Axes of the slice: x: 2, y: 2, z: 4, core: 2. Of those that a mesh axis runs over, the one named last changes fastest.
Arguments:
- tokens: bfloat16 [4, 2048, 768], P('dp', 'ctx'), may hold values from -6 to 6
- segment_ids: int32 [4, 2048], P('dp', 'ctx'), may hold values from 0 to 7, never falling along the last dimension, each value on 1 to 1024 neighbouring positions
- live_blocks: int32 [4, 16, 16], P('dp'), may hold values 0 or 1
- norm1_gain: bfloat16 [768], P(('dp', 'ctx')), may hold values from 0.25 to 1.75
- norm1_bias: bfloat16 [768], P(('dp', 'ctx')), may hold values from -1.5 to 1.5
- qkv_weight: bfloat16 [768, 2304], P(('dp', 'ctx')), may hold values from -0.3125 to 0.3125
- qv_bias: bfloat16 [1536], P(('dp', 'ctx')), may hold values from -2.5 to 2.5
- out_weight: bfloat16 [768, 768], P(('dp', 'ctx')), may hold values from -1.25 to 1.25
- out_bias: bfloat16 [768], P(('dp', 'ctx')), may hold values from -1.5 to 1.5
- norm2_gain: bfloat16 [768], P(('dp', 'ctx')), may hold values from 0.25 to 1.75
- norm2_bias: bfloat16 [768], P(('dp', 'ctx')), may hold values from -1.5 to 1.5
- up_weight: bfloat16 [768, 3072], P(('dp', 'ctx')), may hold values from -0.21875 to 0.21875
- up_bias: bfloat16 [3072], P(('dp', 'ctx')), may hold values from -2.5 to 2.5
- down_weight: bfloat16 [3072, 768], P(('dp', 'ctx')), may hold values from -0.15625 to 0.15625
- down_bias: bfloat16 [768], P(('dp', 'ctx')), may hold values from -1.5 to 1.5
- grad_out: bfloat16 [4, 2048, 768], P('dp', 'ctx'), may hold values from -6 to 6
Outputs:
- output: bfloat16 [4, 2048, 768], P('dp', 'ctx')
- grad_tokens: float32 [4, 2048, 768], P('dp', 'ctx')
- grad_norm1_gain: float32 [768], P(('dp', 'ctx'))
- grad_norm1_bias: float32 [768], P(('dp', 'ctx'))
- grad_qkv_weight: float32 [768, 2304], P(('dp', 'ctx'))
- grad_qv_bias: float32 [1536], P(('dp', 'ctx'))
- grad_out_weight: float32 [768, 768], P(('dp', 'ctx'))
- grad_out_bias: float32 [768], P(('dp', 'ctx'))
- grad_norm2_gain: float32 [768], P(('dp', 'ctx'))
- grad_norm2_bias: float32 [768], P(('dp', 'ctx'))
- grad_up_weight: float32 [768, 3072], P(('dp', 'ctx'))
- grad_up_bias: float32 [3072], P(('dp', 'ctx'))
- grad_down_weight: float32 [3072, 768], P(('dp', 'ctx'))
- grad_down_bias: float32 [768], P(('dp', 'ctx'))
Inputs may be any that keep to these rules, and one draw needn't show every extreme that they name: `segment_ids`: segment numbers never fall along a sequence; a document holds 1 to 1024 positions and one holds exactly 1024.
All inputs are finite; a program needn't handle non-finite values. No bound on the sum of `live_blocks` on one device may be relied on, other than what follows from the above.
Results may differ from a plain program's by a relative error of at most 0.019.
Values may be sent and summed in bfloat16 or wider, within the bound.
No kernel may reach another device: no remote copies, remote signals or barrier semaphores. Data moves between devices by JAX's collectives and lax.ppermute only.
A program may use at most 192 MiB of HBM per device.

v0:
```python
import functools
import math

import jax
import jax.numpy as jnp
from jax import lax
from jax.experimental import pallas as pl
from jax.experimental.pallas import tpu as pltpu
from jax.sharding import Mesh, PartitionSpec as P

HEADS = 12
HEAD_DIM = 64
BLOCK = 128


NEG_FILL = -1e30
SCORE_SCALE = 0.125


def layer_norm(value_in, norm_gain, norm_shift):
    center = value_in - jnp.mean(value_in, axis=-1, keepdims=True)
    spread = jnp.mean(center * center, axis=-1, keepdims=True)
    return center * lax.rsqrt(spread + 1e-05) * norm_gain + norm_shift


def exact_gelu(value_in):
    return jax.nn.gelu(value_in, approximate=False)


def matmul_low(left_side, right_side):
    return jnp.dot(left_side, right_side, preferred_element_type=jnp.float32)


def inner_rows(left_side, right_side):
    return lax.dot_general(
        left_side, right_side, (((0,), (0,)), ((), ())), preferred_element_type=jnp.float32
    )


def times_transpose(left_side, right_side):
    return lax.dot_general(
        left_side, right_side, (((1,), (1,)), ((), ())), preferred_element_type=jnp.float32
    )


def sweep_blocks(count_rows, step_fn, carry_state):
    span_rows = math.gcd(count_rows, 512)
    return lax.fori_loop(
        0,
        count_rows // span_rows,
        lambda loop_index, loop_state: step_fn(loop_index * span_rows, span_rows, loop_state),
        carry_state,
    )


def allowed_pairs(live_table, query_pos, key_pos, query_seg, key_seg):
    block_slots = jnp.arange(live_table.shape[-1], dtype=jnp.int32)
    query_block = query_pos // BLOCK
    key_block = key_pos // BLOCK
    pick_query = (query_block[:, None] == block_slots[None, :]).astype(jnp.bfloat16)
    pick_key = (key_block[:, None] == block_slots[None, :]).astype(jnp.bfloat16)
    live_rows = jnp.einsum(
        "qa,sab->sqb", pick_query, live_table, preferred_element_type=jnp.float32
    )
    live_grid = jnp.einsum(
        "sqb,kb->sqk", live_rows.astype(jnp.bfloat16), pick_key, preferred_element_type=jnp.float32
    )
    same_block = query_block[:, None] == key_block[None, :]
    same_doc = query_seg[:, :, None] == key_seg[:, None, :]
    return same_doc & ((live_grid > 0.5) | same_block[None])


def pair_grads(
    live_table,
    query_heads,
    dout_heads,
    lse_heads,
    delta_heads,
    query_pos,
    query_seg,
    key_heads,
    value_heads,
    key_pos,
    key_seg,
):
    scores = (
        jnp.einsum("sqhd,skhd->shqk", query_heads, key_heads, preferred_element_type=jnp.float32)
        * SCORE_SCALE
    )
    permit = allowed_pairs(live_table, query_pos, key_pos, query_seg, key_seg)[:, None]
    attn_probs = jnp.where(permit, jnp.exp(scores - lse_heads[..., None]), 0.0)
    grad_prob = jnp.einsum(
        "sqhd,skhd->shqk", dout_heads, value_heads, preferred_element_type=jnp.float32
    )
    grad_score = (attn_probs * (grad_prob - delta_heads[..., None])).astype(jnp.bfloat16)
    grad_query = (
        jnp.einsum("shqk,skhd->sqhd", grad_score, key_heads, preferred_element_type=jnp.float32)
        * SCORE_SCALE
    )
    grad_key = (
        jnp.einsum("shqk,sqhd->skhd", grad_score, query_heads, preferred_element_type=jnp.float32)
        * SCORE_SCALE
    )
    grad_value = jnp.einsum(
        "shqk,sqhd->skhd",
        attn_probs.astype(jnp.bfloat16),
        dout_heads,
        preferred_element_type=jnp.float32,
    )
    return (grad_query, grad_key, grad_value)


def local(
    tokens,
    segment_ids,
    live_blocks,
    norm1_gain,
    norm1_bias,
    qkv_weight,
    qv_bias,
    out_weight,
    out_bias,
    norm2_gain,
    norm2_bias,
    up_weight,
    up_bias,
    down_weight,
    down_bias,
    grad_out,
):
    shards = (
        norm1_gain,
        norm1_bias,
        qkv_weight,
        qv_bias,
        out_weight,
        out_bias,
        norm2_gain,
        norm2_bias,
        up_weight,
        up_bias,
        down_weight,
        down_bias,
    )
    gathered = (
        lax.all_gather(shards[0], ("dp", "ctx"), axis=0, tiled=True),
        lax.all_gather(shards[1], ("dp", "ctx"), axis=0, tiled=True),
        lax.all_gather(shards[2], ("dp", "ctx"), axis=0, tiled=True),
        lax.all_gather(shards[3], ("dp", "ctx"), axis=0, tiled=True),
        lax.all_gather(shards[4], ("dp", "ctx"), axis=0, tiled=True),
        lax.all_gather(shards[5], ("dp", "ctx"), axis=0, tiled=True),
        lax.all_gather(shards[6], ("dp", "ctx"), axis=0, tiled=True),
        lax.all_gather(shards[7], ("dp", "ctx"), axis=0, tiled=True),
        lax.all_gather(shards[8], ("dp", "ctx"), axis=0, tiled=True),
        lax.all_gather(shards[9], ("dp", "ctx"), axis=0, tiled=True),
        lax.all_gather(shards[10], ("dp", "ctx"), axis=0, tiled=True),
        lax.all_gather(shards[11], ("dp", "ctx"), axis=0, tiled=True),
    )
    (
        gain_first,
        shift_first,
        full_qkv,
        bias_qv,
        full_out,
        bias_out,
        gain_second,
        shift_second,
        full_up,
        bias_up,
        full_down,
        bias_down,
    ) = gathered
    seq_count, tok_rows, model_width = tokens.shape
    head_count = HEADS
    head_size = HEAD_DIM
    flat_rows = seq_count * tok_rows
    query_pos = lax.axis_index("ctx") * tok_rows + jnp.arange(tok_rows, dtype=jnp.int32)
    live_table = live_blocks.astype(jnp.bfloat16)
    seg_low = segment_ids.astype(jnp.bfloat16)
    inputs_wide = tokens.reshape(flat_rows, model_width).astype(jnp.float32)
    normed_wide, norm_pull_one = jax.vjp(
        layer_norm, inputs_wide, gain_first.astype(jnp.float32), shift_first.astype(jnp.float32)
    )
    normed_one = normed_wide.astype(jnp.bfloat16)
    projected = matmul_low(normed_one, full_qkv)
    bias_wide = bias_qv.astype(jnp.float32)
    query_low = (projected[:, :model_width] + bias_wide[:model_width]).astype(jnp.bfloat16)
    key_low = projected[:, model_width : 2 * model_width].astype(jnp.bfloat16)
    value_low = (projected[:, 2 * model_width :] + bias_wide[model_width:]).astype(jnp.bfloat16)
    query_heads = query_low.reshape(seq_count, tok_rows, head_count, head_size)
    key_seq = key_low.reshape(seq_count, tok_rows, model_width)
    value_seq = value_low.reshape(seq_count, tok_rows, model_width)
    initial = (
        jnp.full((seq_count, head_count, tok_rows), NEG_FILL, jnp.float32),
        jnp.zeros((seq_count, head_count, tok_rows), jnp.float32),
        jnp.zeros((seq_count, tok_rows, head_count, head_size), jnp.float32),
    )
    key_part = lax.all_gather(key_seq, "ctx", axis=1, tiled=True)
    value_part = lax.all_gather(value_seq, "ctx", axis=1, tiled=True)
    seg_part = lax.all_gather(seg_low, "ctx", axis=1, tiled=True)

    def step_fn(offset, span_rows, inner_state):
        run_max, run_total, accum_out = inner_state
        key_heads = lax.dynamic_slice_in_dim(key_part, offset, span_rows, 1).reshape(
            seq_count, span_rows, head_count, head_size
        )
        value_heads = lax.dynamic_slice_in_dim(value_part, offset, span_rows, 1).reshape(
            seq_count, span_rows, head_count, head_size
        )
        key_seg = lax.dynamic_slice_in_dim(seg_part, offset, span_rows, 1)
        key_pos = offset + jnp.arange(span_rows, dtype=jnp.int32)
        scores = (
            jnp.einsum(
                "sqhd,skhd->shqk", query_heads, key_heads, preferred_element_type=jnp.float32
            )
            * SCORE_SCALE
        )
        permit = allowed_pairs(live_table, query_pos, key_pos, seg_low, key_seg)[:, None]
        scores = jnp.where(permit, scores, NEG_FILL)
        new_max = jnp.maximum(run_max, jnp.max(scores, axis=-1))
        exp_scores = jnp.where(permit, jnp.exp(scores - new_max[..., None]), 0.0)
        factor = jnp.exp(run_max - new_max)
        run_total = run_total * factor + jnp.sum(exp_scores, axis=-1)
        weighted = jnp.einsum(
            "shqk,skhd->sqhd",
            exp_scores.astype(jnp.bfloat16),
            value_heads,
            preferred_element_type=jnp.float32,
        )
        accum_out = accum_out * jnp.transpose(factor, (0, 2, 1))[..., None] + weighted
        return (new_max, run_total, accum_out)

    run_max, run_total, accum_out = sweep_blocks(key_part.shape[1], step_fn, initial)
    attn_wide = accum_out / jnp.transpose(run_total, (0, 2, 1))[..., None]
    lse_heads = run_max + jnp.log(run_total)
    attn_low = attn_wide.reshape(flat_rows, model_width).astype(jnp.bfloat16)
    hidden = inputs_wide + matmul_low(attn_low, full_out) + bias_out.astype(jnp.float32)
    normed_two_wide, norm_pull_two = jax.vjp(
        layer_norm, hidden, gain_second.astype(jnp.float32), shift_second.astype(jnp.float32)
    )
    normed_two = normed_two_wide.astype(jnp.bfloat16)
    before = matmul_low(normed_two, full_up) + bias_up.astype(jnp.float32)
    activated_wide, gelu_pull = jax.vjp(exact_gelu, before)
    activated = activated_wide.astype(jnp.bfloat16)
    output = (hidden + matmul_low(activated, full_down) + bias_down.astype(jnp.float32)).astype(
        jnp.bfloat16
    )
    back_params = (
        lax.all_gather(shards[0], ("dp", "ctx"), axis=0, tiled=True),
        lax.all_gather(shards[1], ("dp", "ctx"), axis=0, tiled=True),
        lax.all_gather(shards[2], ("dp", "ctx"), axis=0, tiled=True),
        lax.all_gather(shards[3], ("dp", "ctx"), axis=0, tiled=True),
        lax.all_gather(shards[4], ("dp", "ctx"), axis=0, tiled=True),
        lax.all_gather(shards[5], ("dp", "ctx"), axis=0, tiled=True),
        lax.all_gather(shards[6], ("dp", "ctx"), axis=0, tiled=True),
        lax.all_gather(shards[7], ("dp", "ctx"), axis=0, tiled=True),
        lax.all_gather(shards[8], ("dp", "ctx"), axis=0, tiled=True),
        lax.all_gather(shards[9], ("dp", "ctx"), axis=0, tiled=True),
        lax.all_gather(shards[10], ("dp", "ctx"), axis=0, tiled=True),
        lax.all_gather(shards[11], ("dp", "ctx"), axis=0, tiled=True),
    )
    back_qkv = back_params[2]
    back_out = back_params[4]
    back_up = back_params[8]
    back_down = back_params[10]
    grad_low = grad_out.reshape(flat_rows, model_width)
    grad_down = inner_rows(activated, grad_low)
    grad_bias_down = jnp.sum(grad_low.astype(jnp.float32), axis=0)
    grad_act = times_transpose(grad_low, back_down)
    grad_before = gelu_pull(grad_act)[0].astype(jnp.bfloat16)
    grad_up = inner_rows(normed_two, grad_before)
    grad_bias_up = jnp.sum(grad_before.astype(jnp.float32), axis=0)
    grad_normed_two = times_transpose(grad_before, back_up)
    grad_hidden_part, grad_gain_two, grad_shift_two = norm_pull_two(grad_normed_two)
    grad_hidden = grad_low.astype(jnp.float32) + grad_hidden_part
    grad_branch = grad_hidden.astype(jnp.bfloat16)
    grad_out_full = inner_rows(attn_low, grad_branch)
    grad_bias_out = jnp.sum(grad_branch.astype(jnp.float32), axis=0)
    grad_attn = times_transpose(grad_branch, back_out).astype(jnp.bfloat16)
    dout_heads = grad_attn.reshape(seq_count, tok_rows, head_count, head_size)
    delta_rows = jnp.sum(dout_heads.astype(jnp.float32) * attn_wide, axis=-1)
    delta_heads = jnp.transpose(delta_rows, (0, 2, 1))
    key_all, value_all, seg_all = (
        lax.all_gather(key_seq, "ctx", axis=1, tiled=True),
        lax.all_gather(value_seq, "ctx", axis=1, tiled=True),
        lax.all_gather(seg_low, "ctx", axis=1, tiled=True),
    )

    def key_step(offset, span_rows, inner_state):
        grad_query_acc, grad_key_all, grad_value_all = inner_state
        key_heads = lax.dynamic_slice_in_dim(key_all, offset, span_rows, 1).reshape(
            seq_count, span_rows, head_count, head_size
        )
        value_heads = lax.dynamic_slice_in_dim(value_all, offset, span_rows, 1).reshape(
            seq_count, span_rows, head_count, head_size
        )
        key_seg = lax.dynamic_slice_in_dim(seg_all, offset, span_rows, 1)
        key_pos = offset + jnp.arange(span_rows, dtype=jnp.int32)
        grad_query, grad_key, grad_value = pair_grads(
            live_table,
            query_heads,
            dout_heads,
            lse_heads,
            delta_heads,
            query_pos,
            seg_low,
            key_heads,
            value_heads,
            key_pos,
            key_seg,
        )
        grad_key_all = lax.dynamic_update_slice_in_dim(
            grad_key_all, grad_key.reshape(seq_count, span_rows, model_width), offset, 1
        )
        grad_value_all = lax.dynamic_update_slice_in_dim(
            grad_value_all, grad_value.reshape(seq_count, span_rows, model_width), offset, 1
        )
        return (grad_query_acc + grad_query, grad_key_all, grad_value_all)

    length_rows = key_all.shape[1]
    zero_query = jnp.zeros((seq_count, tok_rows, head_count, head_size), jnp.float32)
    zero_keys = jnp.zeros((seq_count, length_rows, model_width), jnp.float32)
    grad_query_heads, grad_key_all, grad_value_all = sweep_blocks(
        length_rows, key_step, (zero_query, zero_keys, zero_keys)
    )
    grad_key_seq, grad_value_seq = (
        lax.psum_scatter(
            grad_key_all.astype(jnp.bfloat16), "ctx", scatter_dimension=1, tiled=True
        ).astype(jnp.float32),
        lax.psum_scatter(
            grad_value_all.astype(jnp.bfloat16), "ctx", scatter_dimension=1, tiled=True
        ).astype(jnp.float32),
    )
    grad_query_low = grad_query_heads.reshape(flat_rows, model_width).astype(jnp.bfloat16)
    grad_key_low = grad_key_seq.reshape(flat_rows, model_width).astype(jnp.bfloat16)
    grad_value_low = grad_value_seq.reshape(flat_rows, model_width).astype(jnp.bfloat16)
    grad_proj_low = jnp.concatenate([grad_query_low, grad_key_low, grad_value_low], axis=1)
    grad_qkv_full = inner_rows(normed_one, grad_proj_low)
    grad_bias_qv = jnp.concatenate(
        [
            jnp.sum(grad_query_low.astype(jnp.float32), axis=0),
            jnp.sum(grad_value_low.astype(jnp.float32), axis=0),
        ]
    )
    grad_normed_one = times_transpose(grad_proj_low, back_qkv)
    grad_input_part, grad_gain_one, grad_shift_one = norm_pull_one(grad_normed_one)
    grad_tokens = (grad_hidden + grad_input_part).reshape(seq_count, tok_rows, model_width)
    summed = (
        lax.psum_scatter(grad_gain_one, ("dp", "ctx"), scatter_dimension=0, tiled=True),
        lax.psum_scatter(grad_shift_one, ("dp", "ctx"), scatter_dimension=0, tiled=True),
        lax.psum_scatter(grad_qkv_full.astype(jnp.bfloat16), ("dp", "ctx"), scatter_dimension=0, tiled=True).astype(jnp.float32),
        lax.psum_scatter(grad_bias_qv, ("dp", "ctx"), scatter_dimension=0, tiled=True),
        lax.psum_scatter(grad_out_full.astype(jnp.bfloat16), ("dp", "ctx"), scatter_dimension=0, tiled=True).astype(jnp.float32),
        lax.psum_scatter(grad_bias_out, ("dp", "ctx"), scatter_dimension=0, tiled=True),
        lax.psum_scatter(grad_gain_two, ("dp", "ctx"), scatter_dimension=0, tiled=True),
        lax.psum_scatter(grad_shift_two, ("dp", "ctx"), scatter_dimension=0, tiled=True),
        lax.psum_scatter(grad_up.astype(jnp.bfloat16), ("dp", "ctx"), scatter_dimension=0, tiled=True).astype(jnp.float32),
        lax.psum_scatter(grad_bias_up, ("dp", "ctx"), scatter_dimension=0, tiled=True),
        lax.psum_scatter(grad_down.astype(jnp.bfloat16), ("dp", "ctx"), scatter_dimension=0, tiled=True).astype(jnp.float32),
        lax.psum_scatter(grad_bias_down, ("dp", "ctx"), scatter_dimension=0, tiled=True),
    )
    return (
        output.reshape(seq_count, tok_rows, model_width),
        grad_tokens,
        summed[0],
        summed[1],
        summed[2],
        summed[3],
        summed[4],
        summed[5],
        summed[6],
        summed[7],
        summed[8],
        summed[9],
        summed[10],
        summed[11],
    )


NZ = 4
GROUP = HEADS // NZ
GW = GROUP * HEAD_DIM
CHUNK = 256


def pick(array, index, axis=0):
    return lax.dynamic_index_in_dim(array, index, axis, keepdims=False)


def shift(array, axis, size, hop):
    return lax.ppermute(array, axis, [(i, (i + hop) % size) for i in range(size)])


def swap(array, axis):
    return shift(array, axis, 2, 1)


def in_order(own, received, index, axis):
    first = jnp.where(index == 0, own, received)
    second = jnp.where(index == 0, received, own)
    return jnp.stack([first, second], axis=axis)


def z_pieces(block):
    return [block] + [shift(block, "z", NZ, j) for j in range(1, NZ)]


def z_order(pieces, z):
    return jnp.stack([lax.select_n((z - a) % NZ, *pieces) for a in range(NZ)])


def z_exchange(array, z):
    return [pick(array, z)] + [shift(pick(array, (z + j) % NZ), "z", NZ, j) for j in range(1, NZ)]


def xy_gather(line, y, x):
    a, b = line[: NZ // 2], line[NZ // 2 :]
    a = in_order(a, swap(a, "x"), x, 0)
    b = in_order(b, swap(b, "y"), y, 0)
    return (a, swap(a, "y"), y, 0), (b, swap(b, "x"), x, 1)


def add_up(kept, sent, name):
    return kept.astype(jnp.float32) + swap(sent, name).astype(jnp.float32)


def halve(array, name, index, wire):
    return add_up(pick(array, index), pick(array, 1 - index).astype(wire), name)


def after(value, event):
    flag = event[(slice(0, 1),) * event.ndim].reshape(()).astype(jnp.float32)
    return jnp.where(flag != flag, jnp.zeros_like(value), value)


def meet(*values):
    return lax.optimization_barrier(values)


def z_reduce(sent, z):
    edge = jnp.where(z == 0, sent[2], sent[0])
    edge = lax.ppermute(edge, "z", [(0, 1), (NZ - 1, NZ - 2)])
    far = (sent[1].astype(jnp.float32) + edge.astype(jnp.float32)).astype(sent[1].dtype)
    far = shift(far, "z", NZ, 2)
    up = lax.ppermute(sent[0], "z", [(0, 1), (1, 2), (2, 3)])
    down = lax.ppermute(sent[2], "z", [(1, 0), (2, 1), (3, 2)])
    return up, far, down


def norm_back(grad, gain, unit, scale):
    c = grad * gain
    return scale * (
        c - jnp.mean(c, axis=-1, keepdims=True) - unit * jnp.mean(c * unit, axis=-1, keepdims=True)
    )


def dot_nt(a, b):
    return lax.dot_general(a, b, (((1,), (1,)), ((), ())), preferred_element_type=jnp.float32)


def dot_tn(a, b):
    return lax.dot_general(a, b, (((0,), (0,)), ((), ())), preferred_element_type=jnp.float32)


def dot_nn(a, b):
    return lax.dot_general(a, b, (((1,), (0,)), ((), ())), preferred_element_type=jnp.float32)


def column_of(row):
    return jnp.transpose(jnp.broadcast_to(row, (8, row.shape[1])))[:, 0:1]


def query_row(may_ref, tile, block, seg_row, alive):
    per = CHUNK // BLOCK
    lane = lax.broadcasted_iota(jnp.int32, (1, CHUNK), 1)
    flag = jnp.full((1, CHUNK), may_ref[tile * per, block] * alive, jnp.int32)
    for b in range(1, per):
        flag = jnp.where(lane >= b * BLOCK, may_ref[tile * per + b, block] * alive, flag)
    return jnp.where(flag > 0, seg_row, -1.0)


def permit_of(may_ref, tile, chunk, seg_row, key_column, alive):
    per = CHUNK // BLOCK
    return jnp.concatenate(
        [
            key_column[b * BLOCK : (b + 1) * BLOCK]
            == query_row(may_ref, tile, chunk * per + b, seg_row, alive)
            for b in range(per)
        ],
        axis=0,
    )


def list_live(live, list_ref):
    count = jnp.int32(0)
    for number, flag in enumerate(live):
        list_ref[count] = number
        count = count + flag
    list_ref[count] = list_ref[jnp.maximum(count - 1, 0)]
    return count


def pair_at(list_ref, count, step):
    return (
        (list_ref[2 * step], jnp.int32(1)),
        (list_ref[2 * step + 1], (2 * step + 1 < count).astype(jnp.int32)),
    )


def whole_spec(shape):
    return pl.BlockSpec(shape, lambda *_: (0,) * len(shape))


def held(specs, arrays):
    return [
        pl.BlockSpec(memory_space=pltpu.VMEM) if tuple(spec.block_shape) == a.shape else spec
        for spec, a in zip(specs, arrays)
    ]


VMEM_MIB = {
    "unpack": 4, "pack": 4, "project": 14, "branch": 10, "feed": 28, "feed_weights": 24, "middle": 16,
    "inward": 16, "owners": 20, "finish": 10, "deliver": 6, "weave": 6,
}


WEIGHT = {'branch': 3, 'feed': 10, 'feed_weights': 3, 'middle': 3, 'inward': 3, 'owners': 3, 'finish': 10, 'deliver': 3, 'weave': 3}


def kernel_call(body, place, arrays, in_specs, outs, out_specs, grid, scratch, flops, name, more=()):
    prefetch = (place,) + tuple(more)
    moved = sum(a.size * a.dtype.itemsize for a in arrays)
    return pl.pallas_call(
        body,
        out_shape=tuple(jax.ShapeDtypeStruct(shape, dtype) for shape, dtype in outs),
        grid_spec=pltpu.PrefetchScalarGridSpec(
            num_scalar_prefetch=len(prefetch),
            grid=grid,
            in_specs=held(in_specs, arrays),
            out_specs=out_specs,
            scratch_shapes=scratch,
        ),
        compiler_params=pltpu.CompilerParams(vmem_limit_bytes=VMEM_MIB[name] << 20),
        cost_estimate=pl.CostEstimate(
            flops=int(flops * WEIGHT.get(name, 1)), bytes_accessed=int(moved * WEIGHT.get(name, 1)), transcendentals=0
        ),
        name=name,
    )(*prefetch, *arrays)


def lane_groups(lanes, size):
    lane = lax.broadcasted_iota(jnp.int32, (1, lanes), 1).astype(jnp.float32)
    group = jnp.floor((lane + 0.5) * (1.0 / size))
    return group, lane - group * size


def one_hot_rows(place_row, count):
    rows = lax.broadcasted_iota(jnp.int32, (count, place_row.shape[1]), 0).astype(jnp.float32)
    return (rows == place_row).astype(jnp.float32).astype(jnp.bfloat16)


VEC_ROWS = 16


def unpack_kernel(place_ref, packed_ref, vec_ref):
    devices = packed_ref.shape[0]
    width = vec_ref.shape[1]
    size = width // devices
    c = place_ref[1]
    device = lax.broadcasted_iota(jnp.int32, (devices, 1), 0)
    parity = lax.rem(device, 2)
    pair = lax.div(device, 2).astype(jnp.float32)
    device = device.astype(jnp.float32)
    vec_ref[...] = jnp.zeros(vec_ref.shape, jnp.float32)

    def spread(start, n, lanes, owner, keep):
        group, at = lane_groups(lanes, n)
        tiled = dot_nn(packed_ref[:, start : start + n], one_hot_rows(at, n))
        mine = (owner == group) if keep is None else (owner == group) & keep
        return jnp.sum(jnp.where(mine, tiled, 0.0), axis=0, keepdims=True)

    vec_ref[0:1] = spread(0, size, width, device, None)
    vec_ref[1:2] = spread(size, size, width, device, None)
    qv = spread(2 * size, 2 * size, 2 * width, device, None)
    vec_ref[2:3] = qv[:, :width]
    vec_ref[3:4] = qv[:, width:]
    vec_ref[4:5] = spread(4 * size, size, width, device, None)
    vec_ref[5:6] = spread(5 * size, size, width, device, None)
    vec_ref[6:7] = spread(6 * size, size, width, device, None)
    up = spread(7 * size, 4 * size, 2 * width, pair, parity == c)
    vec_ref[8:9] = up[:, :width]
    vec_ref[9:10] = up[:, width:]
    vec_ref[7:8] = spread(11 * size, size, width, device, None)


def pack_kernel(place_ref, grads_ref, mid_ref, qkv_ref, up_ref, packed_ref):
    devices = packed_ref.shape[0]
    width = grads_ref.shape[1]
    size = width // devices
    z, c = place_ref[0], place_ref[1]
    device = lax.broadcasted_iota(jnp.int32, (devices, 1), 0)
    parity = lax.rem(device, 2)
    pair = lax.div(device, 2).astype(jnp.float32)
    device = device.astype(jnp.float32)
    packed_ref[...] = jnp.zeros(packed_ref.shape, jnp.bfloat16)

    def gather(row, n, owner, keep):
        group, at = lane_groups(row.shape[1], n)
        mine = (owner == group) if keep is None else (owner == group) & keep
        return dot_nt(jnp.where(mine, row, 0.0).astype(jnp.bfloat16), one_hot_rows(at, n))

    def place_group(row):
        wide = jnp.concatenate([row] * NZ, axis=1)
        group, _ = lane_groups(wide.shape[1], GW)
        return jnp.where(group == z.astype(jnp.float32), wide, 0.0)

    qkv = qkv_ref[0:1]
    qv = jnp.concatenate([place_group(qkv[:, :GW]), place_group(qkv[:, 2 * GW :])], axis=1)
    parts = [
        gather(grads_ref[0:1], size, device, None),
        gather(grads_ref[1:2], size, device, None),
        gather(qv, 2 * size, device, None),
        gather(mid_ref[2:3], size, device, None),
        gather(mid_ref[0:1], size, device, None),
        gather(mid_ref[1:2], size, device, None),
        gather(up_ref[0:1], 4 * size, pair, parity == c),
        gather(mid_ref[3:4], size, device, None),
    ]
    packed_ref[:, 0 : 12 * size] = jnp.concatenate(parts, axis=1).astype(jnp.bfloat16)


def norm_rows(x):
    center = x - jnp.mean(x, axis=-1, keepdims=True)
    scale = lax.rsqrt(jnp.mean(center * center, axis=-1, keepdims=True) + 1e-05)
    return center * scale, scale


def project_kernel(place_ref, t0_ref, t1_ref, t2_ref, t3_ref, vec_ref, wz_ref, line_ref, n1_ref, q_ref, kv_ref):
    a = pl.program_id(0)
    z = place_ref[0]
    away = lax.rem(z - a + NZ, NZ)
    x = t0_ref[...].astype(jnp.float32)
    for j, ref in enumerate((t1_ref, t2_ref, t3_ref), 1):
        x = jnp.where(away == j, ref[...].astype(jnp.float32), x)
    line_ref[...] = x.astype(jnp.bfloat16)
    unit, _ = norm_rows(x)
    n1 = (unit * vec_ref[0:1] + vec_ref[1:2]).astype(jnp.bfloat16)
    n1_ref[...] = n1
    y = dot_nn(n1, wz_ref[...])
    q_bias, v_bias = vec_ref[2:3, 0:GW], vec_ref[3:4, 0:GW]
    for g in range(1, NZ):
        q_bias = jnp.where(z == g, vec_ref[2:3, g * GW : (g + 1) * GW], q_bias)
        v_bias = jnp.where(z == g, vec_ref[3:4, g * GW : (g + 1) * GW], v_bias)
    q = (y[:, :GW] + q_bias).astype(jnp.bfloat16)
    q_ref[...] = q * jnp.asarray(SCORE_SCALE, jnp.bfloat16)
    kv_ref[:, :GW] = y[:, GW : 2 * GW].astype(jnp.bfloat16)
    kv_ref[:, GW:] = (y[:, 2 * GW :] + v_bias).astype(jnp.bfloat16)


def project(place, pieces, vec, wz):
    rows, width = pieces[0].shape
    low = jnp.bfloat16
    tall = lambda w: pl.BlockSpec((rows, w), lambda a, *_: (a, 0))
    return kernel_call(
        project_kernel, place, (*pieces, vec, wz),
        [whole_spec((rows, width))] * NZ + [whole_spec(vec.shape), whole_spec(wz.shape)],
        [((NZ * rows, width), low), ((NZ * rows, width), low), ((NZ * rows, GW), low), ((NZ * rows, 2 * GW), low)],
        [tall(width), tall(width), tall(GW), tall(2 * GW)],
        (NZ,), [], 8 * NZ * rows * width * 3 * GW, "project",
    )


def branch_kernel(place_ref, a0_ref, a1_ref, a2_ref, a3_ref, wo_ref, own_ref, vec_ref, hidden_ref, n2_ref):
    z = place_ref[0]
    total = own_ref[...].astype(jnp.float32) + vec_ref[4:5]
    branch = None
    for j, ref in enumerate((a0_ref, a1_ref, a2_ref, a3_ref)):
        start = pl.multiple_of(lax.rem(z - j + NZ, NZ) * GW, GW)
        part = dot_nn(ref[...], wo_ref[pl.ds(start, GW), :])
        branch = part if branch is None else branch + part
    hidden = total + branch
    hidden_ref[...] = hidden
    unit, _ = norm_rows(hidden)
    n2_ref[...] = (unit * vec_ref[5:6] + vec_ref[6:7]).astype(jnp.bfloat16)


def branch_call(place, pieces, wo, own, vec):
    rows, width = own.shape
    arrays = (*pieces, wo, own, vec)
    return kernel_call(
        branch_kernel, place, arrays, [whole_spec(a.shape) for a in arrays],
        [((rows, width), jnp.float32), ((rows, width), jnp.bfloat16)],
        [whole_spec((rows, width))] * 2, (1,), [], 8 * rows * width * width, "branch",
    )


def feed_kernel(
    place_ref, na_ref, nb_ref, ga_ref, gb_ref, up_ref, down_ref, bias_ref,
    act_ref, grad_ref, out_ref, m_ref, sums_ref, bias_out_ref, n_s, g_s, out_s, m_s,
):
    k = pl.program_id(0)
    rows, width = na_ref.shape

    @pl.when(k == 0)
    def _():
        n_s[:rows], n_s[rows:] = na_ref[...], nb_ref[...]
        g_s[:rows], g_s[rows:] = ga_ref[...], gb_ref[...]
        out_s[...] = jnp.zeros(out_s.shape, jnp.float32)
        m_s[...] = jnp.zeros(m_s.shape, jnp.float32)

    up, down = up_ref[...].reshape(width, width), down_ref[...].reshape(width, width)
    v = dot_nn(n_s[...], up) + bias_ref[...]
    cdf = 0.5 * (1.0 + lax.erf(v * 0.7071067811865476))
    slope = cdf + v * (0.3989422804014327 * jnp.exp(-0.5 * v * v))
    act = (v * cdf).astype(jnp.bfloat16)
    act_ref[...] = act
    grad = dot_nt(g_s[...], down) * slope
    grad = grad.astype(jnp.bfloat16)
    grad_ref[...] = grad
    bias_out_ref[...] = jnp.sum(grad.astype(jnp.float32), axis=0, keepdims=True)
    out_s[...] += dot_nn(act, down)
    m_s[...] += dot_nt(grad, up)

    @pl.when(k == pl.num_programs(0) - 1)
    def _():
        out_ref[...] = out_s[:rows]
        m_ref[...] = m_s[:rows]
        sums_ref[0] = m_s[rows:].astype(jnp.bfloat16)
        sums_ref[1] = out_s[rows:].astype(jnp.bfloat16)


def feed(place, na, nb, ga, gb, both, bias):
    rows, width = na.shape
    chips, tall, _ = both.shape
    half = bias.shape[1]
    low, wide = jnp.bfloat16, jnp.float32
    one = whole_spec((rows, width))
    across = lambda r: pl.BlockSpec((r, width), lambda k, *_: (0, k))
    return kernel_call(
        feed_kernel, place, (na, nb, ga, gb, both, both, bias),
        [one] * 4 + [
            pl.BlockSpec((chips, tall // 4, width), lambda k, *_: (0, k, 0)),
            pl.BlockSpec((chips // 2, tall // 2, width), lambda k, *_: (k, 1, 0)),
            across(1),
        ],
        [
            ((2 * rows, half), low), ((2 * rows, half), low), ((rows, width), wide), ((rows, width), wide),
            ((2, rows, width), low), ((1, half), wide),
        ],
        [across(2 * rows), across(2 * rows), one, one, whole_spec((2, rows, width)), across(1)],
        (2,),
        [
            pltpu.VMEM((2 * rows, width), low), pltpu.VMEM((2 * rows, width), low),
            pltpu.VMEM((2 * rows, width), wide), pltpu.VMEM((2 * rows, width), wide),
        ],
        32 * rows * width * half, "feed",
    )


def feed_weights_kernel(
    place_ref, na_ref, nb_ref, ga_ref, gb_ref, act_ref, grad_ref, ak_ref, as_ref, bk_ref, bs_ref, n_s, a_s, g_s
):
    rows, width = na_ref.shape
    y, x = place_ref[2], place_ref[3]
    n_s[:, :rows], n_s[:, rows:] = jnp.transpose(na_ref[...]), jnp.transpose(nb_ref[...])
    g_s[:rows], g_s[rows:] = ga_ref[...], gb_ref[...]
    for k in range(0, act_ref.shape[1], width):
        a_s[k : k + width] = jnp.transpose(act_ref[:, k : k + width])
    tall = ak_ref.shape[2]
    quarter = tall // 4
    span = NZ * quarter

    def put(py, px, pz, row, value):
        count = value.shape[0]
        near, far = (ak_ref, as_ref) if pz < NZ // 2 else (bk_ref, bs_ref)
        index, mine = (px, py == y) if pz < NZ // 2 else (py, px == x)

        @pl.when(mine)
        def _():
            near[index, pz % (NZ // 2), row : row + count] = value

        @pl.when(jnp.logical_not(mine))
        def _():
            far[index, pz % (NZ // 2), row : row + count] = value

    def one_column(column, carry):
        py, px = lax.div(column, 2), lax.rem(column, 2)
        at = pl.multiple_of(column * span, span)
        up = dot_nn(n_s[pl.ds(at, span)], grad_ref[...]).astype(jnp.bfloat16)
        down = dot_nn(a_s[pl.ds(pl.multiple_of(2 * at, 2 * span), 2 * span)], g_s[...]).astype(jnp.bfloat16)
        for pz in range(NZ):
            here = slice(pz * quarter, (pz + 1) * quarter)
            put(py, px, pz, 0, up[here, :width])
            put(py, px, pz, quarter, up[here, width:])
            put(py, px, pz, 2 * quarter, down[2 * pz * quarter : 2 * (pz + 1) * quarter])
        return carry

    lax.fori_loop(0, 4, one_column, 0)


def feed_weights(place, na, nb, ga, gb, act, grad, tall):
    rows, width = na.shape
    low = jnp.bfloat16
    arrays = (na, nb, ga, gb, act, grad)
    shape = (2, NZ // 2, tall, width)
    return kernel_call(
        feed_weights_kernel, place, arrays, [whole_spec(a.shape) for a in arrays], [(shape, low)] * 4,
        [whole_spec(shape)] * 4, (1,),
        [
            pltpu.VMEM((width, 2 * rows), low), pltpu.VMEM((act.shape[1], 2 * rows), low),
            pltpu.VMEM((2 * rows, width), low),
        ],
        8 * rows * width * act.shape[1], "feed_weights",
    )


def middle_kernel(
    place_ref, m_ref, out_ref, sums_ref, hidden_ref, go_ref, vec_ref, wo_ref,
    output_ref, gh_ref, branch_ref, d0_ref, d1_ref, d2_ref, d3_ref, cols_ref,
):
    z = place_ref[0]
    hidden, go = hidden_ref[...], go_ref[...].astype(jnp.float32)
    output_ref[...] = (hidden + out_ref[...] + sums_ref[1].astype(jnp.float32) + vec_ref[7:8]).astype(
        jnp.bfloat16
    )
    m = m_ref[...] + sums_ref[0].astype(jnp.float32)
    unit, scale = norm_rows(hidden)
    grad_hidden = go + norm_back(m, vec_ref[5:6], unit, scale)
    gh_ref[...] = grad_hidden
    branch = grad_hidden.astype(jnp.bfloat16)
    branch_ref[...] = branch
    for j, ref in enumerate((d0_ref, d1_ref, d2_ref, d3_ref)):
        start = pl.multiple_of(lax.rem(z + j, NZ) * GW, GW)
        ref[...] = dot_nt(branch, wo_ref[pl.ds(start, GW), :]).astype(jnp.bfloat16)
    cols_ref[...] = jnp.zeros(cols_ref.shape, jnp.float32)
    cols_ref[0:1] = jnp.sum(m * unit, axis=0, keepdims=True)
    cols_ref[1:2] = jnp.sum(m, axis=0, keepdims=True)
    cols_ref[2:3] = jnp.sum(branch.astype(jnp.float32), axis=0, keepdims=True)
    cols_ref[3:4] = jnp.sum(go, axis=0, keepdims=True)


def middle(place, m, out, sums, hidden, go, vec, wo):
    rows, width = m.shape
    arrays = (m, out, sums, hidden, go, vec, wo)
    low, wide = jnp.bfloat16, jnp.float32
    outs = [((rows, width), low), ((rows, width), wide), ((rows, width), low)]
    outs += [((rows, GW), low)] * NZ + [((8, width), wide)]
    return kernel_call(
        middle_kernel, place, arrays, [whole_spec(a.shape) for a in arrays], outs,
        [whole_spec(shape) for shape, _ in outs], (1,), [], 8 * rows * width * width, "middle",
    )


def inward_kernel(
    place_ref, dq_ref, mine_ref, theirs_ref, line_ref, wz_ref, dqkv_ref, keep_ref, s1_ref, s2_ref, s3_ref,
    cols_ref, sums_ref,
):
    j = pl.program_id(0)
    rows = keep_ref.shape[0]
    at = pl.ds(pl.multiple_of(lax.rem(place_ref[0] + 1 + j, NZ) * rows, rows), rows)
    dkv = (mine_ref[at].astype(jnp.float32) + theirs_ref[at].astype(jnp.float32)).astype(jnp.bfloat16)
    dqkv = jnp.concatenate([dq_ref[at], dkv], axis=1)
    dqkv_ref[at] = dqkv
    m1 = dot_nt(dqkv, wz_ref[...])
    unit, _ = norm_rows(line_ref[at].astype(jnp.float32))

    @pl.when(j == 0)
    def _():
        cols_ref[...] = jnp.zeros(cols_ref.shape, jnp.float32)
        sums_ref[...] = jnp.zeros(sums_ref.shape, jnp.float32)

    cols_ref[0:1] += jnp.sum(m1 * unit, axis=0, keepdims=True)
    cols_ref[1:2] += jnp.sum(m1, axis=0, keepdims=True)
    sums_ref[0:1] += jnp.sum(dqkv.astype(jnp.float32), axis=0, keepdims=True)

    for number, ref in enumerate((s1_ref, s2_ref, s3_ref)):

        @pl.when(j == number)
        def _():
            ref[...] = m1.astype(jnp.bfloat16)

    @pl.when(j == pl.num_programs(0) - 1)
    def _():
        keep_ref[...] = m1


def inward(place, dq, mine, theirs, line, wz):
    total, width = line.shape
    rows = total // NZ
    low, wide = jnp.bfloat16, jnp.float32
    arrays = (dq, mine, theirs, line, wz)
    outs = [((total, 3 * GW), low), ((rows, width), wide)] + [((rows, width), low)] * (NZ - 1)
    outs += [((8, width), wide), ((8, 3 * GW), wide)]
    return kernel_call(
        inward_kernel, place, arrays, [whole_spec(a.shape) for a in arrays], outs,
        [whole_spec(shape) for shape, _ in outs], (NZ,), [], 8 * total * width * 3 * GW, "inward",
    )


def finish_kernel(place_ref, m_ref, r1_ref, r2_ref, r3_ref, own_ref, gh_ref, vec_ref, out_ref):
    m = m_ref[...]
    for ref in (r1_ref, r2_ref, r3_ref):
        m = m + ref[...].astype(jnp.float32)
    unit, scale = norm_rows(own_ref[...].astype(jnp.float32))
    out_ref[...] = gh_ref[...] + norm_back(m, vec_ref[0:1], unit, scale)


def finish(place, m, pieces, own, grad_hidden, vec):
    rows, width = own.shape
    arrays = (m, *pieces, own, grad_hidden, vec)
    return kernel_call(
        finish_kernel, place, arrays, [whole_spec(a.shape) for a in arrays],
        [((rows, width), jnp.float32)], [whole_spec((rows, width))], (1,), [], 100 * rows * width, "finish",
    )[0]


def owners_kernel(
    place_ref, a0_ref, a1_ref, a2_ref, a3_ref, branch_ref, n1_ref, dqkv_ref, cols_ref, mid_ref, sums_ref, up_ref,
    mine_ref, theirs_ref, wo_s, wz_s, vec_s,
):
    z, c = place_ref[0], place_ref[1]
    width = branch_ref.shape[1]
    for j, ref in enumerate((a0_ref, a1_ref, a2_ref, a3_ref)):
        start = pl.multiple_of(lax.rem(z - j + NZ, NZ) * GW, GW)
        wo_s[pl.ds(start, GW), :] = dot_tn(ref[...], branch_ref[...]).astype(jnp.bfloat16)
    wz_s[...] = dot_tn(n1_ref[...], dqkv_ref[...]).astype(jnp.bfloat16)
    pack_kernel(place_ref, cols_ref, mid_ref, sums_ref, up_ref, vec_s)
    chips, tall, span = mine_ref.shape
    devices = 2 * chips
    rows = width // devices
    first_row = lax.broadcasted_iota(jnp.int32, (tall - rows, span), 0) == 0
    for pair in range(chips):
        tails = []
        for core in range(2):
            row = vec_s[2 * pair + core : 2 * pair + core + 1].astype(jnp.float32)
            tails.append(jnp.where(first_row, jnp.broadcast_to(row, first_row.shape), 0.0).astype(jnp.bfloat16))
        mine_ref[pair, rows:] = jnp.where(c == 0, tails[0], tails[1])
        theirs_ref[pair, rows:] = jnp.where(c == 0, tails[1], tails[0])

    def one_chip(pair, carry):
        at = pl.ds(pl.multiple_of(pair * (2 * rows), 2 * rows), 2 * rows)
        both = jnp.concatenate([wo_s[at], wz_s[at]], axis=1)
        mine_ref[pair, :rows] = jnp.where(c == 0, both[:rows], both[rows:])
        theirs_ref[pair, :rows] = jnp.where(c == 0, both[rows:], both[:rows])
        return carry

    lax.fori_loop(0, chips, one_chip, 0)


def owners(place, pieces, branch, n1, dqkv, cols, mid, sums, up, devices, tall):
    width, span = n1.shape[1], n1.shape[1] + dqkv.shape[1]
    low = jnp.bfloat16
    arrays = (*pieces, branch, n1, dqkv, cols, mid, sums, up)
    shape = (devices // 2, tall, span)
    return kernel_call(
        owners_kernel, place, arrays, [whole_spec(a.shape) for a in arrays], [(shape, low), (shape, low)],
        [whole_spec(shape)] * 2, (1,),
        [pltpu.VMEM((width, width), low), pltpu.VMEM((width, dqkv.shape[1]), low), pltpu.VMEM((devices, span), low)],
        1 << 20, "owners",
    )


def deliver_kernel(place_ref, own_ref, p1_ref, p2_ref, p3_ref, qkv_ref, wo_ref, vec_ref):
    z = place_ref[0]
    rows, width = wo_ref.shape
    own = own_ref[...]
    pieces = [own] + [ref[...].astype(jnp.float32) for ref in (p1_ref, p2_ref, p3_ref)]
    for g in range(NZ):
        away = lax.rem(z - g + NZ, NZ)
        part = pieces[0]
        for j in range(1, NZ):
            part = jnp.where(away == j, pieces[j], part)
        for k in range(3):
            lanes = slice(k * width + g * GW, k * width + (g + 1) * GW)
            qkv_ref[:, lanes] = part[:rows, width + k * GW : width + (k + 1) * GW]
    total = pieces[0] + pieces[1] + pieces[2] + pieces[3]
    wo_ref[...] = total[:rows, :width]
    vec_ref[...] = total[rows:]


def weave_kernel(place_ref, mine_ref, theirs_ref, out_ref):
    c = place_ref[1]
    mine, theirs = mine_ref[...], theirs_ref[...].astype(jnp.float32)
    even, odd = jnp.where(c == 0, mine, theirs), jnp.where(c == 0, theirs, mine)
    half = mine.shape[1]
    units = half // 16
    for pair in range(16):
        here = slice(pair * units, (pair + 1) * units)
        out_ref[:, 2 * pair * units : (2 * pair + 1) * units] = even[:, here]
        out_ref[:, (2 * pair + 1) * units : (2 * pair + 2) * units] = odd[:, here]


def attend_kernel(
    act_ref, may_ref, place_ref, q_ref, mine_ref, theirs_ref, qseg_ref, kseg_ref, o_ref, low_ref, lse_ref,
    k_s, vt_s, col_s, m_s, l_s, acc_s, list_s,
):
    i = pl.program_id(0)
    chunks = kseg_ref.shape[0]

    @pl.when(i == 0)
    def _():
        for line, ref in enumerate((mine_ref, theirs_ref)):
            core = place_ref[1] if line == 0 else 1 - place_ref[1]
            for a in range(chunks // 2):
                rows = slice(a * CHUNK, (a + 1) * CHUNK)
                at = pl.ds(pl.multiple_of((2 * a + core) * CHUNK, CHUNK), CHUNK)
                for h in range(GROUP):
                    k_s[h, at] = ref[rows, HEAD_DIM * h : HEAD_DIM * (h + 1)]
                    vt_s[h, :, at] = jnp.transpose(ref[rows, GW + HEAD_DIM * h : GW + HEAD_DIM * (h + 1)])
        for j in range(chunks):
            col_s[j * CHUNK : (j + 1) * CHUNK] = column_of(kseg_ref[j : j + 1])

    m_s[...] = jnp.full(m_s.shape, NEG_FILL, jnp.float32)
    l_s[...] = jnp.zeros(l_s.shape, jnp.float32)
    acc_s[...] = jnp.zeros(acc_s.shape, jnp.float32)
    here = pl.ds(pl.multiple_of(i * CHUNK, CHUNK), CHUNK)
    q_heads = [q_ref[here, HEAD_DIM * h : HEAD_DIM * (h + 1)] for h in range(GROUP)]
    q_seg = qseg_ref[pl.ds(i, 1)]

    count = list_live([act_ref[i, j] for j in range(chunks)], list_s)

    def two_chunks(step, carry):
        heads, pair = range(GROUP), pair_at(list_s, count, step)
        at = [pl.ds(pl.multiple_of(j * CHUNK, CHUNK), CHUNK) for j, _ in pair]
        permit = [permit_of(may_ref, i, j, q_seg, col_s[at[u]], alive) for u, (j, alive) in enumerate(pair)]
        s = [[jnp.where(permit[u], dot_nt(k_s[h, at[u]], q_heads[h]), NEG_FILL) for u in range(2)] for h in heads]
        old = [m_s[h] for h in heads]
        top = [[jnp.max(part, axis=0, keepdims=True) for part in s[h]] for h in heads]
        new = [jnp.maximum(old[h], jnp.maximum(*top[h])) for h in heads]
        p = [[jnp.exp(part - new[h]) for part in s[h]] for h in heads]
        fade = [jnp.exp(old[h] - new[h]) for h in heads]
        for h in heads:
            l_s[h] = l_s[h] * fade[h] + sum(jnp.sum(part, axis=0, keepdims=True) for part in p[h])
            added = [dot_nn(vt_s[h, :, at[u]], p[h][u].astype(jnp.bfloat16)) for u in range(2)]
            acc_s[h] = acc_s[h] * fade[h] + (added[0] + added[1])
            m_s[h] = new[h]
        return carry

    lax.fori_loop(0, lax.div(count + 1, 2), two_chunks, 0)
    out = jnp.concatenate([jnp.transpose(acc_s[h] / l_s[h]) for h in range(GROUP)], axis=1)
    o_ref[...] = out
    low_ref[...] = out.astype(jnp.bfloat16)
    logs = [m_s[h] + jnp.log(l_s[h]) for h in range(GROUP)]
    lse_ref[...] = jnp.concatenate(logs + [logs[0]] * (8 - GROUP), axis=0)


def attend(active, may, place, q, mine, theirs, q_seg, k_seg):
    rows, keys = q.shape[0], 2 * mine.shape[0]
    tall = pl.BlockSpec((CHUNK, GW), lambda i, *_: (i, 0))
    return pl.pallas_call(
        attend_kernel,
        out_shape=(
            jax.ShapeDtypeStruct((rows, GW), jnp.float32),
            jax.ShapeDtypeStruct((rows, GW), jnp.bfloat16),
            jax.ShapeDtypeStruct((8, rows), jnp.float32),
        ),
        grid_spec=pltpu.PrefetchScalarGridSpec(
            num_scalar_prefetch=3,
            grid=(rows // CHUNK,),
            in_specs=held(
                [whole_spec(a.shape) for a in (q, mine, theirs, q_seg, k_seg)], (q, mine, theirs, q_seg, k_seg)
            ),
            out_specs=[tall, tall, pl.BlockSpec((8, CHUNK), lambda i, *_: (0, i))],
            scratch_shapes=[
                pltpu.VMEM((GROUP, keys, HEAD_DIM), jnp.bfloat16),
                pltpu.VMEM((GROUP, HEAD_DIM, keys), jnp.bfloat16),
                pltpu.VMEM((keys, 1), jnp.float32),
                pltpu.VMEM((GROUP, 1, CHUNK), jnp.float32),
                pltpu.VMEM((GROUP, 1, CHUNK), jnp.float32),
                pltpu.VMEM((GROUP, HEAD_DIM, CHUNK), jnp.float32),
                pltpu.SMEM((keys // CHUNK + 1,), jnp.int32),
            ],
        ),
        compiler_params=pltpu.CompilerParams(vmem_limit_bytes=18 << 20),
        cost_estimate=pl.CostEstimate(
            flops=int(48 * rows * keys * GW), bytes_accessed=16 * keys * GW, transcendentals=4 * rows * keys
        ),
        name="attend",
    )(active, may, place, q, mine, theirs, q_seg, k_seg)


def attend_back_kernel(first, *refs):
    (act_ref, may_ref, place_ref, q_ref, d0_ref, d1_ref, d2_ref, d3_ref, kv_ref, lse_ref, qseg_ref,
     kseg_ref, from_ref, *refs) = refs
    if first:
        dqt_ref, delta_ref, dkv_ref, list_s, q_s, do_s, dk_s, dv_s = refs
    else:
        old_ref, dq_ref, dkv_ref, list_s, q_s, do_s, dk_s, dv_s, dqt_ref = refs
        delta_ref = from_ref
    step = pl.program_id(0)
    rows = q_ref.shape[0]
    z, c = place_ref[0], place_ref[1]
    j = 2 * step + (1 - c if first else c)

    @pl.when(step == 0)
    def _():
        for r, ref in enumerate((d0_ref, d1_ref, d2_ref, d3_ref)):
            at = pl.ds(pl.multiple_of(lax.rem(z - r + NZ, NZ) * CHUNK, CHUNK), CHUNK)
            for h in range(GROUP):
                do_s[h, at] = ref[:, HEAD_DIM * h : HEAD_DIM * (h + 1)]
        ones = jnp.ones((8, HEAD_DIM), jnp.float32)
        for h in range(GROUP):
            lanes = slice(HEAD_DIM * h, HEAD_DIM * (h + 1))
            q_s[h] = q_ref[:, lanes]
            if first:
                both = do_s[h].astype(jnp.float32) * from_ref[:, lanes]
                delta_ref[h : h + 1] = lax.dot_general(
                    ones, both, (((1,), (1,)), ((), ())), precision=lax.Precision.HIGHEST,
                    preferred_element_type=jnp.float32,
                )[0:1]
        dqt_ref[...] = jnp.zeros(dqt_ref.shape, jnp.float32) if first else old_ref[...]
        if first:
            delta_ref[GROUP:] = jnp.zeros((8 - GROUP, rows), jnp.float32)

    dk_s[...] = jnp.zeros(dk_s.shape, jnp.float32)
    dv_s[...] = jnp.zeros(dv_s.shape, jnp.float32)
    here = pl.ds(pl.multiple_of(step * CHUNK, CHUNK), CHUNK)
    k_heads = [kv_ref[here, HEAD_DIM * h : HEAD_DIM * (h + 1)] for h in range(GROUP)]
    v_heads = [kv_ref[here, GW + HEAD_DIM * h : GW + HEAD_DIM * (h + 1)] for h in range(GROUP)]
    k_turned = [jnp.transpose(k) for k in k_heads]
    k_column = column_of(kseg_ref[pl.ds(j, 1)])

    count = list_live([act_ref[i, j] for i in range(rows // CHUNK)], list_s)

    def two_tiles(turn, carry):
        heads, pair, low = range(GROUP), pair_at(list_s, count, turn), jnp.bfloat16
        both = [(h, u) for h in heads for u in range(2)]
        at = [pl.ds(pl.multiple_of(i * CHUNK, CHUNK), CHUNK) for i, _ in pair]
        permit = [
            permit_of(may_ref, i, j, qseg_ref[pl.ds(i, 1)], k_column, alive) for i, alive in pair
        ]
        s = {(h, u): dot_nt(k_heads[h], q_s[h, at[u]]) for h, u in both}
        dp = {(h, u): dot_nt(v_heads[h], do_s[h, at[u]]) for h, u in both}
        p = {
            (h, u): jnp.where(permit[u], jnp.exp(s[h, u] - lse_ref[h : h + 1, at[u]]), 0.0) for h, u in both
        }
        ds = {(h, u): (p[h, u] * (dp[h, u] - delta_ref[h : h + 1, at[u]])).astype(low) for h, u in both}
        for h in heads:
            dv_s[h] += dot_nn(p[h, 0].astype(low), do_s[h, at[0]]) + dot_nn(p[h, 1].astype(low), do_s[h, at[1]])
            dk_s[h] += dot_nn(ds[h, 0], q_s[h, at[0]]) + dot_nn(ds[h, 1], q_s[h, at[1]])
            for u in range(2):
                dqt_ref[h, :, at[u]] += dot_nn(k_turned[h], ds[h, u])
        return carry

    lax.fori_loop(0, lax.div(count + 1, 2), two_tiles, 0)
    dkv_ref[...] = jnp.concatenate(
        [dk_s[h] for h in range(GROUP)] + [dv_s[h] for h in range(GROUP)], axis=1
    ).astype(jnp.bfloat16)
    if not first:

        @pl.when(step == pl.num_programs(0) - 1)
        def _():
            dq_ref[...] = jnp.concatenate(
                [jnp.transpose(dqt_ref[h] * SCORE_SCALE) for h in range(GROUP)], axis=1
            ).astype(jnp.bfloat16)


def attend_back(first, active, may, place, q, pieces, kv, lse, q_seg, k_seg, *carried):
    rows = q.shape[0]
    low, wide = jnp.bfloat16, jnp.float32
    tall = pl.BlockSpec((CHUNK, 2 * GW), lambda s, *_: (s, 0))
    turned = (GROUP, HEAD_DIM, rows)
    outs = [(turned, wide), ((8, rows), wide)] if first else [((rows, GW), low)]
    scratch = [pltpu.SMEM((rows // CHUNK + 1,), jnp.int32)] + [pltpu.VMEM((GROUP, rows, HEAD_DIM), low)] * 2 + [pltpu.VMEM((GROUP, CHUNK, HEAD_DIM), wide)] * 2
    if not first:
        scratch.append(pltpu.VMEM(turned, wide))
    return pl.pallas_call(
        functools.partial(attend_back_kernel, first),
        out_shape=tuple(jax.ShapeDtypeStruct(*o) for o in outs + [((rows, 2 * GW), low)]),
        grid_spec=pltpu.PrefetchScalarGridSpec(
            num_scalar_prefetch=3,
            grid=(rows // CHUNK,),
            in_specs=held(
                [
                    whole_spec((rows, GW)), *[whole_spec(p.shape) for p in pieces], whole_spec(kv.shape), whole_spec((8, rows)),
                    whole_spec(q_seg.shape), whole_spec(k_seg.shape), *[whole_spec(a.shape) for a in carried],
                ],
                (q, *pieces, kv, lse, q_seg, k_seg, *carried),
            ),
            out_specs=[whole_spec(shape) for shape, _ in outs] + [tall],
            scratch_shapes=scratch,
        ),
        compiler_params=pltpu.CompilerParams(vmem_limit_bytes=20 << 20),
        cost_estimate=pl.CostEstimate(
            flops=int(56 * rows * rows * GW), bytes_accessed=32 * rows * GW, transcendentals=4 * rows * rows
        ),
        name="attend_back_first" if first else "attend_back_last",
    )(active, may, place, q, *pieces, kv, lse, q_seg, k_seg, *carried)


def fast_local(
    tokens, segment_ids, live_blocks, norm1_gain, norm1_bias, qkv_weight, qv_bias, out_weight, out_bias,
    norm2_gain, norm2_bias, up_weight, up_bias, down_weight, down_bias, grad_out,
):
    y, x, z, c = (lax.axis_index(name) for name in ("y", "x", "z", "c"))
    place = jnp.stack([z, c, y, x]).astype(jnp.int32)
    wide, low = jnp.float32, jnp.bfloat16
    _, rows, width = tokens.shape
    own_rows, units = qkv_weight.shape[0], down_weight.shape[0]
    ff = up_weight.shape[1]
    half, pairs = ff // 2, ff // (2 * units)
    devices = width // own_rows
    seq_rows = rows * NZ
    keys = 2 * seq_rows
    blocks = keys // BLOCK
    per = CHUNK // BLOCK

    vectors = (norm1_gain, norm1_bias, qv_bias, out_bias, norm2_gain, norm2_bias, up_bias, down_bias)
    sizes = [v.shape[0] for v in vectors]
    cuts = [sum(sizes[:i]) for i in range(len(sizes) + 1)]
    span = width + 3 * GW
    tall = own_rows + 8
    parts = vectors + (segment_ids[0].astype(low),)
    extra = sum(
        jnp.pad(p, (start, span - start - p.shape[0])) for p, start in zip(parts, cuts)
    )
    extra = jnp.pad(extra[None], ((0, 7), (0, 0)))
    wz = qkv_weight.reshape(own_rows, 3, NZ, GW).transpose(2, 0, 1, 3).reshape(NZ, own_rows, 3 * GW)
    group1 = jnp.concatenate(
        [jnp.broadcast_to(out_weight[None], (NZ, own_rows, width)), wz], axis=2
    )
    group1 = jnp.concatenate([group1, jnp.broadcast_to(extra[None], (NZ, 8, span))], axis=1)
    pieces1 = z_exchange(group1, z)

    up_sets = up_weight.reshape(own_rows, pairs, 2, units).transpose(2, 0, 1, 3)
    up_sets = up_sets.reshape(2, own_rows, half)
    up_chip = in_order(pick(up_sets, c), swap(pick(up_sets, 1 - c), "c"), c, 0)
    up_chip = up_chip.reshape(2 * own_rows, half)
    group2 = jnp.concatenate([up_chip[:, :width], up_chip[:, width:], down_weight], axis=0)
    pieces2 = z_pieces(group2)

    own, pieces2[1], pieces2[3] = meet(tokens[0], pieces2[1], pieces2[3])
    line_pieces = z_pieces(own)
    group1 = z_order(pieces1, z)
    own_seg = group1[:, own_rows, cuts[-1] : cuts[-1] + rows].astype(wide)
    seg = in_order(own_seg, swap(own_seg, "c"), c, 1).reshape(keys // CHUNK, CHUNK)
    group1 = jnp.concatenate([in_order(*half) for half in xy_gather(group1, y, x)], axis=2)
    group1 = in_order(group1, swap(group1, "c"), c, 3)
    wo = group1[..., :own_rows, :width].reshape(width, width)
    wz = group1[..., :own_rows, width:].reshape(width, 3 * GW)
    packed = group1[..., own_rows, : cuts[-1]].reshape(devices, cuts[-1])
    vec = kernel_call(
        unpack_kernel, place, (packed,), [whole_spec(packed.shape)], [((VEC_ROWS, width), wide)],
        [whole_spec((VEC_ROWS, width))], (1,), [], 1 << 20, "unpack",
    )[0]
    group2, vec = meet(z_order(pieces2, z), vec)
    group2 = xy_gather(group2, y, x)

    own_blocks = seq_rows // BLOCK
    ids = jnp.arange(blocks, dtype=jnp.int32)
    own_ids = pick(ids.reshape(NZ, 2, rows // BLOCK), c, 1).reshape(own_blocks)
    own_live = pick(live_blocks[0].reshape(NZ, 2, rows // BLOCK, blocks), c, 1)
    own_live = own_live.reshape(own_blocks, blocks)
    seg_blocks = seg.reshape(blocks, BLOCK)
    own_seg_blocks = own_seg.reshape(own_blocks, BLOCK)
    may = (own_live > 0) | (own_ids[:, None] == ids[None, :])
    touch = (
        may
        & (own_seg_blocks[:, :1] <= seg_blocks[:, -1][None])
        & (seg_blocks[:, 0][None] <= own_seg_blocks[:, -1:])
    )
    active = jnp.any(touch.reshape(own_blocks // per, per, blocks // per, per), axis=(1, 3))
    active, may = active.astype(jnp.int32), may.astype(jnp.int32)

    line, n1, q, kv = project(place, line_pieces, vec, wz)
    kv_theirs = swap(kv, "c")
    att_wide, att_low, lse = attend(active, may, place, q, kv, kv_theirs, own_seg, seg)
    att = z_exchange(att_low.reshape(NZ, rows, GW), z)
    group2 = [in_order(own_half, after(other, att_low), at, axis) for own_half, other, at, axis in group2]
    group2 = jnp.concatenate(group2, axis=2)

    hidden, n2 = branch_call(place, att, wo, own, vec)
    go = grad_out[0]
    n2_theirs, go_theirs = swap(n2, "c"), swap(go, "c")
    up_bias_half = vec[8:10].reshape(1, half)
    chips = devices // 2
    group2 = group2.reshape(chips, 2 * units, width)
    activated, grad_before, out_part, m_part, sums, up_bias_part = feed(
        place, n2, n2_theirs, go, go_theirs, group2, up_bias_half
    )
    sums = swap(sums, "c")
    a_kept, a_sent, b_kept, b_sent = feed_weights(
        place, n2, n2_theirs, go, go_theirs, activated, grad_before, 2 * units
    )
    output, grad_hidden, grad_branch, *grad_att, mid = middle(
        place, m_part, out_part, sums, hidden, go, vec, wo
    )
    dout = [grad_att[0]] + [shift(grad_att[j], "z", NZ, j) for j in range(1, NZ)]
    a, b = add_up(a_kept, a_sent, "y"), add_up(b_kept, b_sent, "x")

    dq_part, delta, dkv_theirs = attend_back(
        True, active, may, place, q, dout, kv_theirs, lse, own_seg, seg, att_wide
    )
    a, b, dq_part = meet(a, b, dq_part)
    a, b = halve(a, "x", x, low), halve(b, "y", y, low)
    dq, dkv_mine = attend_back(
        False, active, may, place, q, dout, kv, lse, own_seg, seg, delta, dq_part
    )
    dqkv, m1_own, *m1_sent, cols, dqkv_sum = inward(place, dq, dkv_mine, swap(dkv_theirs, "c"), line, wz)
    a, b, m1_sent[0] = meet(a, b, m1_sent[0])
    group2 = jnp.concatenate([a, b], axis=0)
    m1_up, m1_far, m1_down = z_reduce(m1_sent, z)

    mine, theirs = owners(
        place, att, grad_branch, n1, dqkv, cols, mid, dqkv_sum, up_bias_part, devices, tall
    )
    group1 = (mine.astype(wide) + swap(theirs, "c").astype(wide)).astype(low)
    group1 = group1.reshape(2, 2, NZ, tall, span)
    a = halve(group1[:, :, :2], "y", y, low)
    b = halve(group1[:, :, 2:].swapaxes(0, 1), "x", x, low)
    a, b = halve(a, "x", x, low), halve(b, "y", y, low)
    a, b, m1_far, m1_down = meet(a, b, m1_far, m1_down)
    grad_tokens = finish(place, m1_own, (m1_up, m1_far, m1_down), own, grad_hidden, vec)
    group1 = jnp.concatenate([a, b], axis=0)
    pieces = z_exchange(group1.astype(low), z)
    arrays = (pick(group1, z), *pieces[1:])
    outs = [((own_rows, 3 * width), wide), ((own_rows, width), wide), ((tall - own_rows, span), wide)]
    grad_qkv, grad_wo, vec_sum = kernel_call(
        deliver_kernel, place, arrays, [whole_spec(a.shape) for a in arrays], outs,
        [whole_spec(shape) for shape, _ in outs], (1,), [], 1 << 20, "deliver",
    )
    v = [vec_sum[0, cuts[i] : cuts[i + 1]] for i in range(len(sizes))]

    group2_low = group2.astype(low)
    sent = [pick(group2_low, (z + j) % NZ) for j in range(1, NZ)]
    group2 = sum((piece.astype(wide) for piece in [shift(p, "z", NZ, j) for j, p in enumerate(sent, 1)]), pick(group2, z))
    grad_down = group2[units:]
    up_rows = jnp.concatenate([group2[: 2 * own_rows], group2[2 * own_rows : units]], axis=1)
    up_rows = up_rows.reshape(2, own_rows, half)
    arrays = (pick(up_rows, c), swap(pick(up_rows, 1 - c).astype(low), "c"))
    grad_up = kernel_call(
        weave_kernel, place, arrays, [whole_spec(a.shape) for a in arrays], [((own_rows, ff), wide)],
        [whole_spec((own_rows, ff))], (1,), [], 1 << 20, "weave",
    )[0]
    return (
        output[None], grad_tokens[None], v[0], v[1], grad_qkv, v[2], grad_wo, v[3],
        v[4], v[5], grad_up, v[6], grad_down, v[7],
    )


def build(body, mesh, dp, ctx):
    both = dp + ctx
    rows, vector, matrix = P(dp, ctx, None), P(both), P(both, None)
    return jax.shard_map(
        body,
        mesh=mesh,
        in_specs=(
            rows, P(dp, ctx), P(dp, None, None), vector, vector, matrix, vector, matrix, vector,
            vector, vector, matrix, vector, matrix, vector, rows,
        ),
        out_specs=(
            rows, rows, vector, vector, matrix, vector, matrix, vector, vector, vector, matrix,
            vector, matrix, vector,
        ),
        check_vma=False,
    )


def solution(mesh):
    if dict(mesh.shape) == {"dp": 4, "ctx": 2 * NZ}:
        grid = Mesh(mesh.devices.reshape(2, 2, NZ, 2), ("y", "x", "z", "c"))
        return build(fast_local, grid, ("y", "x"), ("z", "c"))
    return build(local, mesh, ("dp",), ("ctx",))
```

profile of v0, /device:TPU:0, one launch (start us, length us, event | category | flops | bytes accessed | tf_op | source)
XLA Modules:
  0.0 263.5 jit_solution(11522978910951432651)
XLA Ops:
  4.5 3.1 %collective-permute-start = (bf16[32,1344]{1,0:T(8,128)(2,1)S(1)}, bf16[32,1344]{1,0:T(8,128)(2,1)S(1)}, u32[]{:S(2)}, u32[]{:S(2)}) collective-permute-start(bf16[32,1344]{1,0:T(8,128)(2,1)S(1)} %get-tuple-element.184), channel_id=1, source_target_pairs={{0,2},{2,4},{4,6},{6,0},{1,3},{3,5},{5,7},{7,1},{8,10},{10,12},{12... | collective-permute-start | bytes 258056 | tf_op jit(solution)/shard_map/ppermute | solution.py:391
  7.6 2.6 collective-permute-start.1
  13.4 2.8 %collective-permute-done.1 = bf16[32,1344]{1,0:T(8,128)(2,1)S(1)} collective-permute-done((bf16[32,1344]{1,0:T(8,128)(2,1)S(1)}, bf16[32,1344]{1,0:T(8,128)(2,1)S(1)}, u32[]{:S(2)}, u32[]{:S(2)}) %collective-permute-start.1) | collective-permute-done | bytes 86048 | tf_op jit(solution)/shard_map/ppermute | solution.py:391
  16.5 1.6 collective-permute-start.11
  18.1 1.6 collective-permute-start.13
  20.4 2.2 collective-permute-start.5
  22.6 1.6 collective-permute-start.6
  26.3 9.9 %collective-permute-done.12 = bf16[2,2,32,1344]{3,2,1,0:T(8,128)(2,1)S(1)} collective-permute-done((bf16[2,2,32,1344]{3,2,1,0:T(8,128)(2,1)S(1)}, bf16[2,2,32,1344]{3,2,1,0:T(8,128)(2,1)S(1)}, u32[]{:S(2)}, u32[]{:S(2)}) %collective-permute-start.12) | collective-permute-done | bytes 344096 | tf_op jit(solution)/shard_map/ppermute | solution.py:391
  36.8 9.5 %collective-permute-done.14 = bf16[2,2,32,1344]{3,2,1,0:T(8,128)(2,1)S(1)} collective-permute-done((bf16[2,2,32,1344]{3,2,1,0:T(8,128)(2,1)S(1)}, bf16[2,2,32,1344]{3,2,1,0:T(8,128)(2,1)S(1)}, u32[]{:S(2)}, u32[]{:S(2)}) %collective-permute-start.14) | collective-permute-done | bytes 344096 | tf_op jit(solution)/shard_map/ppermute | solution.py:391
  48.6 2.1 collective-permute-start.7
  51.8 2.5 collective-permute-start.9
  55.7 1.4 select_bitcast_fusion.17
  58.8 1.8 select_bitcast_fusion.1
  65.3 13.6 %collective-permute-done.8.t2_ref = bf16[256,768]{1,0:T(8,128)(2,1)S(1)} collective-permute-done((bf16[256,768]{1,0:T(8,128)(2,1)S(1)}, bf16[256,768]{1,0:T(8,128)(2,1)S(1)}, u32[]{:S(2)}, u32[]{:S(2)}) %collective-permute-start.8) | collective-permute-done | bytes 393248 | tf_op jit(solution)/shard_map/ppermute | solution.py:391
  78.9 4.1 %project.1 = (bf16[1024,768]{1,0:T(8,128)(2,1)S(1)}, bf16[1024,768]{1,0:T(8,128)(2,1)S(1)}, bf16[1024,192]{1,0:T(8,128)(2,1)S(1)}, bf16[1024,384]{1,0:T(8,128)(2,1)S(1)}) custom-call(s32[4]{0:T(128)S(1)} %pad_add_fusion.1.place_ref.refs_2_, bf16[256,768]{1,0:T(8,128)(2,1)S(1)} %bitcast.235, bf16[256,768]{1,0:T(8,128)(2,1)S(1)} %collective-permute-done.7.t1_ref, ...), custom_call_target="tpu_custom_call" | custom-call | flops 3623878656 | bytes 2506752 | tf_op jit(solution)/shard_map/project/pallas_call | solution.py:533
  86.5 10.3 %attend.1 = (f32[1024,192]{1,0:T(8,128)S(1)}, bf16[1024,192]{1,0:T(8,128)(2,1)S(1)}, f32[8,1024]{1,0:T(8,128)S(1)}) custom-call(s32[4,8]{1,0:T(4,128)S(1)} %convert_element_type.157.act_ref.refs_0_, s32[8,16]{1,0:T(8,128)S(1)} %fusion.20.may_ref.refs_1_, s32[4]{0:T(128)S(1)} %pad_add_fusion.1.place_ref.refs_2_, ...), custom_call_target="tpu_custom_call" | custom-call | flops 19327352832 | bytes 6291456 | tf_op jit(solution)/shard_map/attend/pallas_call | solution.py:1050
  96.8 9.0 %collective-permute-start.17 = (bf16[256,192]{1,0:T(8,128)(2,1)S(1)}, bf16[256,192]{1,0:T(8,128)(2,1)S(1)}, u32[]{:S(2)}, u32[]{:S(2)}) collective-permute-start(bf16[256,192]{1,0:T(8,128)(2,1)S(1)} %get-tuple-element.173), channel_id=1, source_target_pairs={{0,2},{2,4},{4,6},{6,0},{1,3},{3,5},{5,7},{7,1},{8,10},{10,12},{12... | collective-permute-start | bytes 294920 | tf_op jit(solution)/shard_map/ppermute | solution.py:391
  105.8 1.9 collective-permute-start.18
  111.5 5.1 %collective-permute-done.18.a2_ref = bf16[256,192]{1,0:T(8,128)(2,1)S(1)} collective-permute-done((bf16[256,192]{1,0:T(8,128)(2,1)S(1)}, bf16[256,192]{1,0:T(8,128)(2,1)S(1)}, u32[]{:S(2)}, u32[]{:S(2)}) %collective-permute-start.18) | collective-permute-done | bytes 98336 | tf_op jit(solution)/shard_map/ppermute | solution.py:391
  119.8 7.0 %feed.1 = (bf16[512,1536]{1,0:T(8,128)(2,1)S(1)}, bf16[512,1536]{1,0:T(8,128)(2,1)S(1)}, f32[256,768]{1,0:T(8,128)S(1)}, f32[256,768]{1,0:T(8,128)S(1)}, bf16[2,...) custom-call(s32[4]{0:T(128)S(1)} %pad_add_fusion.1.place_ref.refs_2_, bf16[256,768]{1,0:T(8,128)(2,1)S(1)} %get-tuple-element.80.na_ref, ...), custom_call_target="tpu_custom_call" | custom-call | flops 96636764160 | bytes 110161920 | tf_op jit(solution)/shard_map/feed/pallas_call | solution.py:533
  127.0 6.1 %feed_weights.1 = (bf16[2,2,192,768]{3,2,1,0:T(8,128)(2,1)S(1)}, bf16[2,2,192,768]{3,2,1,0:T(8,128)(2,1)S(1)}, bf16[2,2,192,768]{3,2,1,0:T(8,128)(2,1)S(1)}, bf16[2,2,192,768]{3,2,1,0:T(8,128)(2,1)}) custom-call(s32[4]{0:T(128)S(1)} %pad_add_fusion.1.place_ref.refs_2_, bf16[256,768]{1,0:T(8,128)(2,1)S(1)} %get-tuple-element.80.na_ref, ...), custom_call_target="tpu_custom_call" | custom-call | flops 7247757312 | bytes 14155776 | tf_op jit(solution)/shard_map/feed_weights/pallas_call | solution.py:533
  133.1 2.7 %collective-permute-start.31 = (bf16[2,2,192,768]{3,2,1,0:T(8,128)(2,1)}, bf16[2,2,192,768]{3,2,1,0:T(8,128)(2,1)}, u32[]{:S(2)}, u32[]{:S(2)}) collective-permute-start(bf16[2,2,192,768]{3,2,1,0:T(8,128)(2,1)} %get-tuple-element.99), channel_id=1, source_target_pairs={{0,8},{8,0},{1,9},{9,1},{2,10},{10,2},{3,11},{11,3},{4,12},{12,4},... | collective-permute-start | bytes 3538952 | tf_op jit(solution)/shard_map/ppermute | solution.py:391
  135.8 2.4 middle.1
  140.5 2.9 %collective-permute-start.27 = (bf16[256,192]{1,0:T(8,128)(2,1)}, bf16[256,192]{1,0:T(8,128)(2,1)S(1)}, u32[]{:S(2)}, u32[]{:S(2)}) collective-permute-start(bf16[256,192]{1,0:T(8,128)(2,1)} %get-tuple-element.88), channel_id=1, source_target_pairs={{0,2},{2,4},{4,6},{6,0},{1,3},{3,5},{5,7},{7,1},{8,10},{10,12},{12... | collective-permute-start | bytes 294920 | tf_op jit(solution)/shard_map/ppermute | solution.py:391
  145.7 2.4 collective-permute-start.30
  149.0 4.5 %collective-permute-done.28.refs_6_ = bf16[256,192]{1,0:T(8,128)(2,1)S(1)} collective-permute-done((bf16[256,192]{1,0:T(8,128)(2,1)S(1)}, bf16[256,192]{1,0:T(8,128)(2,1)S(1)}, u32[]{:S(2)}, u32[]{:S(2)}) %collective-permute-start.28) | collective-permute-done | bytes 98336 | tf_op jit(solution)/shard_map/ppermute | solution.py:391
  157.8 8.8 %attend_back_first.1 = (f32[3,64,1024]{2,1,0:T(8,128)S(1)}, f32[8,1024]{1,0:T(8,128)S(1)}, bf16[1024,384]{1,0:T(8,128)(2,1)S(1)}) custom-call(s32[4,8]{1,0:T(4,128)S(1)} %convert_element_type.157.act_ref.refs_0_, s32[8,16]{1,0:T(8,128)S(1)} %fusion.20.may_ref.refs_1_, s32[4]{0:T(128)S(1)} %pad_add_fusion.1.place_ref.refs_2_, ...), custom_call_target="tpu_custom_call" | custom-call | flops 11274289152 | bytes 6291456 | tf_op jit(solution)/shard_map/attend_back_first/pallas_call | solution.py:1167
  166.7 1.5 convert_add_fusion
  168.2 5.8 %collective-permute-done.30 = bf16[2,2,192,768]{3,2,1,0:T(8,128)(2,1)S(1)} collective-permute-done((bf16[2,2,192,768]{3,2,1,0:T(8,128)(2,1)}, bf16[2,2,192,768]{3,2,1,0:T(8,128)(2,1)S(1)}, u32[]{:S(2)}, u32[]{:S(2)}) %collective-permute-start.30) | collective-permute-done | bytes 1179680 | tf_op jit(solution)/shard_map/ppermute | solution.py:391
  174.3 1.8 collective-permute-start.34
  176.5 7.8 %attend_back_last.1 = (bf16[1024,192]{1,0:T(8,128)(2,1)S(1)}, bf16[1024,384]{1,0:T(8,128)(2,1)S(1)}) custom-call(s32[4,8]{1,0:T(4,128)S(1)} %convert_element_type.157.act_ref.refs_0_, s32[8,16]{1,0:T(8,128)S(1)} %fusion.20.may_ref.refs_1_, s32[4]{0:T(128)S(1)} %pad_add_fusion.1.place_ref.refs_2_, bf16[1024,192]{1,0:T(8,128)(2,1)S(1)} %copy-done.34, ...), custom_call_target="tpu_custom_call" | custom-call | flops 11274289152 | bytes 6291456 | tf_op jit(solution)/shard_map/attend_back_last/pallas_call | solution.py:1167
  184.4 4.0 %inward.1 = (bf16[1024,576]{1,0:T(8,128)(2,1)S(1)}, f32[256,768]{1,0:T(8,128)S(1)}, bf16[256,768]{1,0:T(8,128)(2,1)S(1)}, bf16[256,768]{1,0:T(8,128)(2,1)S(1)}, ...) custom-call(s32[4]{0:T(128)S(1)} %pad_add_fusion.1.place_ref.refs_2_, ...), custom_call_target="tpu_custom_call" | custom-call | flops 10871635968 | bytes 13271040 | tf_op jit(solution)/shard_map/inward/pallas_call | solution.py:533
  192.4 2.1 collective-permute-start.47
  200.6 3.1 %owners.1 = (bf16[16,32,1344]{2,1,0:T(8,128)(2,1)S(1)}, bf16[16,32,1344]{2,1,0:T(8,128)(2,1)S(1)}) custom-call(s32[4]{0:T(128)S(1)} %pad_add_fusion.1.place_ref.refs_2_, bf16[256,192]{1,0:T(8,128)(2,1)S(1)} %copy-done.9, bf16[256,192]{1,0:T(8,128)(2,1)S(1)} %copy-done.19, bf16[256,192]{1,0:T(8,128)(2,1)S(1)} %copy-done.21, bf16[256,192]{1,0:T(8,128)(2,1)S(1)} %copy-done.23, ...), custom_call_target="tpu_custom_call" | custom-call | flops 3145728 | bytes 10838016 | tf_op jit(solution)/shard_map/owners/pallas_call | solution.py:533
  205.2 9.7 %collective-permute-start.35 = (bf16[256,768]{1,0:T(8,128)(2,1)S(1)}, bf16[256,768]{1,0:T(8,128)(2,1)S(1)}, u32[]{:S(2)}, u32[]{:S(2)}) collective-permute-start(bf16[256,768]{1,0:T(8,128)(2,1)S(1)} %get-tuple-element.110), channel_id=1, source_target_pairs={{0,2},{2,4},{4,6},{1,3},{3,5},{5,7},{8,10},{10,12},{12,14},{9,11},... | collective-permute-start | bytes 1179656 | tf_op jit(solution)/shard_map/ppermute | solution.py:445
  214.9 8.6 %collective-permute-start.41 = (bf16[256,768]{1,0:T(8,128)(2,1)S(1)}, bf16[256,768]{1,0:T(8,128)(2,1)S(1)}, u32[]{:S(2)}, u32[]{:S(2)}) collective-permute-start(bf16[256,768]{1,0:T(8,128)(2,1)S(1)} %broadcast_select_fusion.2), channel_id=1, source_target_pairs={{0,2},{6,4},{1,3},{7,5},{8,10},{14,12},{9,11},{15,13},{16,18},{22,... | collective-permute-start | bytes 1179656 | tf_op jit(solution)/shard_map/ppermute | solution.py:442
  223.5 1.5 fusion.3
  226.4 1.5 weave.1
  229.7 2.2 collective-permute-start.42
  233.2 5.7 %collective-permute-done.39 = bf16[2,2,32,1344]{3,2,1,0:T(8,128)(2,1)S(1)} collective-permute-done((bf16[2,2,32,1344]{3,2,1,0:T(8,128)(2,1)S(1)}, bf16[2,2,32,1344]{3,2,1,0:T(8,128)(2,1)S(1)}, u32[]{:S(2)}, u32[]{:S(2)}) %collective-permute-start.39) | collective-permute-done | bytes 344096 | tf_op jit(solution)/shard_map/ppermute | solution.py:391
  239.0 1.7 collective-permute-start.40
  240.8 2.1 collective-permute-done.37
  243.0 4.4 %collective-permute-start.38 = (bf16[2,32,1344]{2,1,0:T(8,128)(2,1)S(1)}, bf16[2,32,1344]{2,1,0:T(8,128)(2,1)S(1)}, u32[]{:S(2)}, u32[]{:S(2)}) collective-permute-start(bf16[2,32,1344]{2,1,0:T(8,128)(2,1)S(1)} %fusion.4), channel_id=1, source_target_pairs={{0,8},{8,0},{1,9},{9,1},{2,10},{10,2},{3,11},{11,3},{4,12},{12,4},... | collective-permute-start | bytes 516104 | tf_op jit(solution)/shard_map/ppermute | solution.py:391
  247.4 3.4 %collective-permute-done.38 = bf16[2,32,1344]{2,1,0:T(8,128)(2,1)S(1)} collective-permute-done((bf16[2,32,1344]{2,1,0:T(8,128)(2,1)S(1)}, bf16[2,32,1344]{2,1,0:T(8,128)(2,1)S(1)}, u32[]{:S(2)}, u32[]{:S(2)}) %collective-permute-start.38) | collective-permute-done | bytes 172064 | tf_op jit(solution)/shard_map/ppermute | solution.py:391
  251.2 2.1 collective-permute-start.45
  253.3 1.7 collective-permute-start.46
  255.0 2.1 finish.1
  258.4 2.0 collective-permute-done.45.p2_ref
  (294 shorter events, 62.3 us)
Async XLA Ops:
  4.5 8.9 %collective-permute-start = (bf16[32,1344]{1,0:T(8,128)(2,1)S(1)}, bf16[32,1344]{1,0:T(8,128)(2,1)S(1)}, u32[]{:S(2)}, u32[]{:S(2)}) collective-permute-start(bf16[32,1344]{1,0:T(8,128)(2,1)S(1)} %get-tuple-element.184), channel_id=1, source_target_pairs={{0,2},{2,4},{4,6},{6,0},{1,3},{3,5},{5,7},{7,1},{8,10},{10,12},{12... | collective-permute-start | bytes 258056 | tf_op jit(solution)/shard_map/ppermute | solution.py:391
  7.6 8.6 %collective-permute-start.1 = (bf16[32,1344]{1,0:T(8,128)(2,1)S(1)}, bf16[32,1344]{1,0:T(8,128)(2,1)S(1)}, u32[]{:S(2)}, u32[]{:S(2)}) collective-permute-start(bf16[32,1344]{1,0:T(8,128)(2,1)S(1)} %get-tuple-element.183), channel_id=1, source_target_pairs={{0,4},{2,6},{4,0},{6,2},{1,5},{3,7},{5,1},{7,3},{8,12},{10,14},{12... | collective-permute-start | bytes 258056 | tf_op jit(solution)/shard_map/ppermute | solution.py:391
  10.2 6.2 %collective-permute-start.2 = (bf16[32,1344]{1,0:T(8,128)(2,1)S(1)}, bf16[32,1344]{1,0:T(8,128)(2,1)S(1)}, u32[]{:S(2)}, u32[]{:S(2)}) collective-permute-start(bf16[32,1344]{1,0:T(8,128)(2,1)S(1)} %get-tuple-element.182), channel_id=1, source_target_pairs={{0,6},{2,0},{4,2},{6,4},{1,7},{3,1},{5,3},{7,5},{8,14},{10,8},{12,... | collective-permute-start | bytes 258056 | tf_op jit(solution)/shard_map/ppermute | solution.py:391
  16.5 8.5 %collective-permute-start.11 = (bf16[2,32,1344]{2,1,0:T(8,128)(2,1)S(1)}, bf16[2,32,1344]{2,1,0:T(8,128)(2,1)S(1)}, u32[]{:S(2)}, u32[]{:S(2)}) collective-permute-start(bf16[2,32,1344]{2,1,0:T(8,128)(2,1)S(1)} %pad_maximum_fusion.10), channel_id=1, source_target_pairs={{0,8},{8,0},{1,9},{9,1},{2,10},{10,2},{3,11},{11,3},{4,12},{12,4},... | collective-permute-start | bytes 516104 | tf_op jit(solution)/shard_map/ppermute | solution.py:391
  18.1 7.0 %collective-permute-start.13 = (bf16[2,32,1344]{2,1,0:T(8,128)(2,1)S(1)}, bf16[2,32,1344]{2,1,0:T(8,128)(2,1)S(1)}, u32[]{:S(2)}, u32[]{:S(2)}) collective-permute-start(bf16[2,32,1344]{2,1,0:T(8,128)(2,1)S(1)} %pad_maximum_fusion.11), channel_id=1, source_target_pairs={{0,16},{16,0},{1,17},{17,1},{2,18},{18,2},{3,19},{19,3},{4,20},{20... | collective-permute-start | bytes 516104 | tf_op jit(solution)/shard_map/ppermute | solution.py:391
  20.4 28.1 %collective-permute-start.5 = (bf16[192,768]{1,0:T(8,128)(2,1)}, bf16[192,768]{1,0:T(8,128)(2,1)}, u32[]{:S(2)}, u32[]{:S(2)}) collective-permute-start(bf16[192,768]{1,0:T(8,128)(2,1)} %pad_maximum_fusion.8), channel_id=1, source_target_pairs={{0,2},{2,4},{4,6},{6,0},{1,3},{3,5},{5,7},{7,1},{8,10},{10,12},{12... | collective-permute-start | bytes 884744 | tf_op jit(solution)/shard_map/ppermute | solution.py:391
  22.6 25.9 %collective-permute-start.6 = (bf16[192,768]{1,0:T(8,128)(2,1)}, bf16[192,768]{1,0:T(8,128)(2,1)}, u32[]{:S(2)}, u32[]{:S(2)}) collective-permute-start(bf16[192,768]{1,0:T(8,128)(2,1)} %pad_maximum_fusion.8), channel_id=1, source_target_pairs={{0,6},{2,0},{4,2},{6,4},{1,7},{3,1},{5,3},{7,5},{8,14},{10,8},{12,... | collective-permute-start | bytes 884744 | tf_op jit(solution)/shard_map/ppermute | solution.py:391
  24.3 30.1 %collective-permute-start.10 = (bf16[192,768]{1,0:T(8,128)(2,1)}, bf16[192,768]{1,0:T(8,128)(2,1)}, u32[]{:S(2)}, u32[]{:S(2)}) collective-permute-start(bf16[192,768]{1,0:T(8,128)(2,1)} %pad_maximum_fusion.8), channel_id=1, source_target_pairs={{0,4},{2,6},{4,0},{6,2},{1,5},{3,7},{5,1},{7,3},{8,12},{10,14},{12... | collective-permute-start | bytes 884744 | tf_op jit(solution)/shard_map/ppermute | solution.py:391
  25.1 22.8 %collective-permute-start.3 = (f32[4,256]{1,0:T(4,128)S(1)}, f32[4,256]{1,0:T(4,128)S(1)}, u32[]{:S(2)}, u32[]{:S(2)}) collective-permute-start(f32[4,256]{1,0:T(4,128)S(1)} %bitcast.238), channel_id=1, source_target_pairs={{0,1},{1,0},{2,3},{3,2},{4,5},{5,4},{6,7},{7,6},{8,9},{9,8},{10,11... | collective-permute-start | bytes 12296 | tf_op jit(solution)/shard_map/ppermute | solution.py:391
  25.3 10.9 %collective-permute-start.12 = (bf16[2,2,32,1344]{3,2,1,0:T(8,128)(2,1)S(1)}, bf16[2,2,32,1344]{3,2,1,0:T(8,128)(2,1)S(1)}, u32[]{:S(2)}, u32[]{:S(2)}) collective-permute-start(bf16[2,2,32,1344]{3,2,1,0:T(8,128)(2,1)S(1)} %pad_maximum_fusion.6), channel_id=1, source_target_pairs={{0,16},{16,0},{1,17},{17,1},{2,18},{18,2},{3,19},{19,3},{4,20},{20... | collective-permute-start | bytes 1032200 | tf_op jit(solution)/shard_map/ppermute | solution.py:391
  36.2 10.1 %collective-permute-start.14 = (bf16[2,2,32,1344]{3,2,1,0:T(8,128)(2,1)S(1)}, bf16[2,2,32,1344]{3,2,1,0:T(8,128)(2,1)S(1)}, u32[]{:S(2)}, u32[]{:S(2)}) collective-permute-start(bf16[2,2,32,1344]{3,2,1,0:T(8,128)(2,1)S(1)} %pad_maximum_fusion.7), channel_id=1, source_target_pairs={{0,8},{8,0},{1,9},{9,1},{2,10},{10,2},{3,11},{11,3},{4,12},{12,4},... | collective-permute-start | bytes 1032200 | tf_op jit(solution)/shard_map/ppermute | solution.py:391
  47.8 10.5 %collective-permute-start.15 = (bf16[2,2,4,32,1344]{4,3,2,1,0:T(8,128)(2,1)}, bf16[2,2,4,32,1344]{4,3,2,1,0:T(8,128)(2,1)}, u32[]{:S(2)}, u32[]{:S(2)}) collective-permute-start(bf16[2,2,4,32,1344]{4,3,2,1,0:T(8,128)(2,1)} %maximum_maximum_fusion.1), channel_id=1, source_target_pairs={{0,1},{1,0},{2,3},{3,2},{4,5},{5,4},{6,7},{7,6},{8,9},{9,8},{10,11... | collective-permute-start | bytes 4128776 | tf_op jit(solution)/shard_map/ppermute | solution.py:391
  48.6 16.7 %collective-permute-start.7 = (bf16[256,768]{1,0:T(8,128)(2,1)S(1)}, bf16[256,768]{1,0:T(8,128)(2,1)S(1)}, u32[]{:S(2)}, u32[]{:S(2)}) collective-permute-start(bf16[256,768]{1,0:T(8,128)(2,1)S(1)} %bitcast.232), channel_id=1, source_target_pairs={{0,2},{2,4},{4,6},{6,0},{1,3},{3,5},{5,7},{7,1},{8,10},{10,12},{12... | collective-permute-start | bytes 1179656 | tf_op jit(solution)/shard_map/ppermute | solution.py:391
  50.7 28.2 %collective-permute-start.8 = (bf16[256,768]{1,0:T(8,128)(2,1)S(1)}, bf16[256,768]{1,0:T(8,128)(2,1)S(1)}, u32[]{:S(2)}, u32[]{:S(2)}) collective-permute-start(bf16[256,768]{1,0:T(8,128)(2,1)S(1)} %bitcast.233), channel_id=1, source_target_pairs={{0,4},{2,6},{4,0},{6,2},{1,5},{3,7},{5,1},{7,3},{8,12},{10,14},{12... | collective-permute-start | bytes 1179656 | tf_op jit(solution)/shard_map/ppermute | solution.py:391
  51.8 27.1 %collective-permute-start.9 = (bf16[256,768]{1,0:T(8,128)(2,1)S(1)}, bf16[256,768]{1,0:T(8,128)(2,1)S(1)}, u32[]{:S(2)}, u32[]{:S(2)}) collective-permute-start(bf16[256,768]{1,0:T(8,128)(2,1)S(1)} %bitcast.234), channel_id=1, source_target_pairs={{0,6},{2,0},{4,2},{6,4},{1,7},{3,1},{5,3},{7,5},{8,14},{10,8},{12,... | collective-permute-start | bytes 1179656 | tf_op jit(solution)/shard_map/ppermute | solution.py:391
  64.0 20.2 %collective-permute-start.22 = (bf16[2,192,768]{2,1,0:T(8,128)(2,1)S(1)}, bf16[2,192,768]{2,1,0:T(8,128)(2,1)S(1)}, u32[]{:S(2)}, u32[]{:S(2)}) collective-permute-start(bf16[2,192,768]{2,1,0:T(8,128)(2,1)S(1)} %get-tuple-element.155), channel_id=1, source_target_pairs={{0,8},{8,0},{1,9},{9,1},{2,10},{10,2},{3,11},{11,3},{4,12},{12,4},... | collective-permute-start | bytes 1769480 | tf_op jit(solution)/shard_map/ppermute | solution.py:391
  64.6 19.6 %collective-permute-start.24 = (bf16[2,192,768]{2,1,0:T(8,128)(2,1)S(1)}, bf16[2,192,768]{2,1,0:T(8,128)(2,1)S(1)}, u32[]{:S(2)}, u32[]{:S(2)}) collective-permute-start(bf16[2,192,768]{2,1,0:T(8,128)(2,1)S(1)} %get-tuple-element.156), channel_id=1, source_target_pairs={{0,16},{16,0},{1,17},{17,1},{2,18},{18,2},{3,19},{19,3},{4,20},{20... | collective-permute-start | bytes 1769480 | tf_op jit(solution)/shard_map/ppermute | solution.py:391
  84.2 2.3 collective-permute-start.16
  84.5 33.6 %collective-permute-start.23 = (bf16[2,2,192,768]{3,2,1,0:T(8,128)(2,1)S(1)}, bf16[2,2,192,768]{3,2,1,0:T(8,128)(2,1)S(1)}, u32[]{:S(2)}, u32[]{:S(2)}) collective-permute-start(bf16[2,2,192,768]{3,2,1,0:T(8,128)(2,1)S(1)} %pad_maximum_fusion.2), channel_id=1, source_target_pairs={{0,16},{16,0},{1,17},{17,1},{2,18},{18,2},{3,19},{19,3},{4,20},{20... | collective-permute-start | bytes 3538952 | tf_op jit(solution)/shard_map/ppermute | solution.py:391
  85.2 33.1 %collective-permute-start.25 = (bf16[2,2,192,768]{3,2,1,0:T(8,128)(2,1)S(1)}, bf16[2,2,192,768]{3,2,1,0:T(8,128)(2,1)S(1)}, u32[]{:S(2)}, u32[]{:S(2)}) collective-permute-start(bf16[2,2,192,768]{3,2,1,0:T(8,128)(2,1)S(1)} %pad_maximum_fusion.3), channel_id=1, source_target_pairs={{0,8},{8,0},{1,9},{9,1},{2,10},{10,2},{3,11},{11,3},{4,12},{12,4},... | collective-permute-start | bytes 3538952 | tf_op jit(solution)/shard_map/ppermute | solution.py:391
  96.8 14.7 %collective-permute-start.17 = (bf16[256,192]{1,0:T(8,128)(2,1)S(1)}, bf16[256,192]{1,0:T(8,128)(2,1)S(1)}, u32[]{:S(2)}, u32[]{:S(2)}) collective-permute-start(bf16[256,192]{1,0:T(8,128)(2,1)S(1)} %get-tuple-element.173), channel_id=1, source_target_pairs={{0,2},{2,4},{4,6},{6,0},{1,3},{3,5},{5,7},{7,1},{8,10},{10,12},{12... | collective-permute-start | bytes 294920 | tf_op jit(solution)/shard_map/ppermute | solution.py:391
  105.8 10.8 %collective-permute-start.18 = (bf16[256,192]{1,0:T(8,128)(2,1)S(1)}, bf16[256,192]{1,0:T(8,128)(2,1)S(1)}, u32[]{:S(2)}, u32[]{:S(2)}) collective-permute-start(bf16[256,192]{1,0:T(8,128)(2,1)S(1)} %get-tuple-element.172), channel_id=1, source_target_pairs={{0,4},{2,6},{4,0},{6,2},{1,5},{3,7},{5,1},{7,3},{8,12},{10,14},{12... | collective-permute-start | bytes 294920 | tf_op jit(solution)/shard_map/ppermute | solution.py:391
  107.6 9.0 %collective-permute-start.19 = (bf16[256,192]{1,0:T(8,128)(2,1)S(1)}, bf16[256,192]{1,0:T(8,128)(2,1)S(1)}, u32[]{:S(2)}, u32[]{:S(2)}) collective-permute-start(bf16[256,192]{1,0:T(8,128)(2,1)S(1)} %get-tuple-element.171), channel_id=1, source_target_pairs={{0,6},{2,0},{4,2},{6,4},{1,7},{3,1},{5,3},{7,5},{8,14},{10,8},{12,... | collective-permute-start | bytes 294920 | tf_op jit(solution)/shard_map/ppermute | solution.py:391
  111.5 8.0 %collective-permute-start.21 = (bf16[256,768]{1,0:T(8,128)(2,1)S(1)}, bf16[256,768]{1,0:T(8,128)(2,1)S(1)}, u32[]{:S(2)}, u32[]{:S(2)}) collective-permute-start(bf16[256,768]{1,0:T(8,128)(2,1)S(1)} %bitcast.243), channel_id=1, source_target_pairs={{0,1},{1,0},{2,3},{3,2},{4,5},{5,4},{6,7},{7,6},{8,9},{9,8},{10,11... | collective-permute-start | bytes 1179656 | tf_op jit(solution)/shard_map/ppermute | solution.py:391
  126.8 9.0 %collective-permute-start.26 = (bf16[2,256,768]{2,1,0:T(8,128)(2,1)S(1)}, bf16[2,256,768]{2,1,0:T(8,128)(2,1)S(1)}, u32[]{:S(2)}, u32[]{:S(2)}) collective-permute-start(bf16[2,256,768]{2,1,0:T(8,128)(2,1)S(1)} %get-tuple-element.84), channel_id=1, source_target_pairs={{0,1},{1,0},{2,3},{3,2},{4,5},{5,4},{6,7},{7,6},{8,9},{9,8},{10,11... | collective-permute-start | bytes 2359304 | tf_op jit(solution)/shard_map/ppermute | solution.py:391
  133.1 33.5 %collective-permute-start.31 = (bf16[2,2,192,768]{3,2,1,0:T(8,128)(2,1)}, bf16[2,2,192,768]{3,2,1,0:T(8,128)(2,1)}, u32[]{:S(2)}, u32[]{:S(2)}) collective-permute-start(bf16[2,2,192,768]{3,2,1,0:T(8,128)(2,1)} %get-tuple-element.99), channel_id=1, source_target_pairs={{0,8},{8,0},{1,9},{9,1},{2,10},{10,2},{3,11},{11,3},{4,12},{12,4},... | collective-permute-start | bytes 3538952 | tf_op jit(solution)/shard_map/ppermute | solution.py:391
  140.5 8.5 %collective-permute-start.27 = (bf16[256,192]{1,0:T(8,128)(2,1)}, bf16[256,192]{1,0:T(8,128)(2,1)S(1)}, u32[]{:S(2)}, u32[]{:S(2)}) collective-permute-start(bf16[256,192]{1,0:T(8,128)(2,1)} %get-tuple-element.88), channel_id=1, source_target_pairs={{0,2},{2,4},{4,6},{6,0},{1,3},{3,5},{5,7},{7,1},{8,10},{10,12},{12... | collective-permute-start | bytes 294920 | tf_op jit(solution)/shard_map/ppermute | solution.py:391
  143.4 10.1 %collective-permute-start.28 = (bf16[256,192]{1,0:T(8,128)(2,1)S(1)}, bf16[256,192]{1,0:T(8,128)(2,1)S(1)}, u32[]{:S(2)}, u32[]{:S(2)}) collective-permute-start(bf16[256,192]{1,0:T(8,128)(2,1)S(1)} %get-tuple-element.89), channel_id=1, source_target_pairs={{0,4},{2,6},{4,0},{6,2},{1,5},{3,7},{5,1},{7,3},{8,12},{10,14},{12... | collective-permute-start | bytes 294920 | tf_op jit(solution)/shard_map/ppermute | solution.py:391
  144.6 8.9 %collective-permute-start.29 = (bf16[256,192]{1,0:T(8,128)(2,1)S(1)}, bf16[256,192]{1,0:T(8,128)(2,1)S(1)}, u32[]{:S(2)}, u32[]{:S(2)}) collective-permute-start(bf16[256,192]{1,0:T(8,128)(2,1)S(1)} %get-tuple-element.90), channel_id=1, source_target_pairs={{0,6},{2,0},{4,2},{6,4},{1,7},{3,1},{5,3},{7,5},{8,14},{10,8},{12,... | collective-permute-start | bytes 294920 | tf_op jit(solution)/shard_map/ppermute | solution.py:391
  145.7 28.3 %collective-permute-start.30 = (bf16[2,2,192,768]{3,2,1,0:T(8,128)(2,1)}, bf16[2,2,192,768]{3,2,1,0:T(8,128)(2,1)S(1)}, u32[]{:S(2)}, u32[]{:S(2)}) collective-permute-start(bf16[2,2,192,768]{3,2,1,0:T(8,128)(2,1)} %copy-done.24), channel_id=1, source_target_pairs={{0,16},{16,0},{1,17},{17,1},{2,18},{18,2},{3,19},{19,3},{4,20},{20... | collective-permute-start | bytes 3538952 | tf_op jit(solution)/shard_map/ppermute | solution.py:391
  166.6 17.8 %collective-permute-start.32 = (bf16[1024,384]{1,0:T(8,128)(2,1)S(1)}, bf16[1024,384]{1,0:T(8,128)(2,1)S(1)}, u32[]{:S(2)}, u32[]{:S(2)}) collective-permute-start(bf16[1024,384]{1,0:T(8,128)(2,1)S(1)} %get-tuple-element.104), channel_id=1, source_target_pairs={{0,1},{1,0},{2,3},{3,2},{4,5},{5,4},{6,7},{7,6},{8,9},{9,8},{10,11... | collective-permute-start | bytes 2359304 | tf_op jit(solution)/shard_map/ppermute | solution.py:391
  174.3 14.2 %collective-permute-start.34 = (bf16[2,192,768]{2,1,0:T(8,128)(2,1)S(1)}, bf16[2,192,768]{2,1,0:T(8,128)(2,1)S(1)}, u32[]{:S(2)}, u32[]{:S(2)}) collective-permute-start(bf16[2,192,768]{2,1,0:T(8,128)(2,1)S(1)} %fusion.1), channel_id=1, source_target_pairs={{0,16},{16,0},{1,17},{17,1},{2,18},{18,2},{3,19},{19,3},{4,20},{20... | collective-permute-start | bytes 1769480 | tf_op jit(solution)/shard_map/ppermute | solution.py:391
  176.2 13.6 %collective-permute-start.33 = (bf16[2,192,768]{2,1,0:T(8,128)(2,1)S(1)}, bf16[2,192,768]{2,1,0:T(8,128)(2,1)S(1)}, u32[]{:S(2)}, u32[]{:S(2)}) collective-permute-start(bf16[2,192,768]{2,1,0:T(8,128)(2,1)S(1)} %fusion), channel_id=1, source_target_pairs={{0,8},{8,0},{1,9},{9,1},{2,10},{10,2},{3,11},{11,3},{4,12},{12,4},... | collective-permute-start | bytes 1769480 | tf_op jit(solution)/shard_map/ppermute | solution.py:391
  192.4 12.8 %collective-permute-start.47 = (bf16[192,768]{1,0:T(8,128)(2,1)}, bf16[192,768]{1,0:T(8,128)(2,1)}, u32[]{:S(2)}, u32[]{:S(2)}) collective-permute-start(bf16[192,768]{1,0:T(8,128)(2,1)} %get-tuple-element.150), channel_id=1, source_target_pairs={{0,2},{2,4},{4,6},{6,0},{1,3},{3,5},{5,7},{7,1},{8,10},{10,12},{12... | collective-permute-start | bytes 884744 | tf_op jit(solution)/shard_map/ppermute | solution.py:391
  194.5 20.4 %collective-permute-start.48 = (bf16[192,768]{1,0:T(8,128)(2,1)}, bf16[192,768]{1,0:T(8,128)(2,1)}, u32[]{:S(2)}, u32[]{:S(2)}) collective-permute-start(bf16[192,768]{1,0:T(8,128)(2,1)} %get-tuple-element.152), channel_id=1, source_target_pairs={{0,4},{2,6},{4,0},{6,2},{1,5},{3,7},{5,1},{7,3},{8,12},{10,14},{12... | collective-permute-start | bytes 884744 | tf_op jit(solution)/shard_map/ppermute | solution.py:391
  195.9 27.6 %collective-permute-start.49 = (bf16[192,768]{1,0:T(8,128)(2,1)}, bf16[192,768]{1,0:T(8,128)(2,1)}, u32[]{:S(2)}, u32[]{:S(2)}) collective-permute-start(bf16[192,768]{1,0:T(8,128)(2,1)} %get-tuple-element.151), channel_id=1, source_target_pairs={{0,6},{2,0},{4,2},{6,4},{1,7},{3,1},{5,3},{7,5},{8,14},{10,8},{12,... | collective-permute-start | bytes 884744 | tf_op jit(solution)/shard_map/ppermute | solution.py:391
  203.8 24.1 %collective-permute-start.36 = (bf16[16,32,1344]{2,1,0:T(8,128)(2,1)S(1)}, bf16[16,32,1344]{2,1,0:T(8,128)(2,1)S(1)}, u32[]{:S(2)}, u32[]{:S(2)}) collective-permute-start(bf16[16,32,1344]{2,1,0:T(8,128)(2,1)S(1)} %get-tuple-element.119), channel_id=1, source_target_pairs={{0,1},{1,0},{2,3},{3,2},{4,5},{5,4},{6,7},{7,6},{8,9},{9,8},{10,11... | collective-permute-start | bytes 4128776 | tf_op jit(solution)/shard_map/ppermute | solution.py:391
  203.9 47.0 %collective-permute-start.43 = (bf16[256,768]{1,0:T(8,128)(2,1)S(1)}, bf16[256,768]{1,0:T(8,128)(2,1)S(1)}, u32[]{:S(2)}, u32[]{:S(2)}) collective-permute-start(bf16[256,768]{1,0:T(8,128)(2,1)S(1)} %copy-done.13), channel_id=1, source_target_pairs={{2,0},{4,2},{6,4},{3,1},{5,3},{7,5},{10,8},{12,10},{14,12},{11,9},... | collective-permute-start | bytes 1179656 | tf_op jit(solution)/shard_map/ppermute | solution.py:446
  205.2 49.8 %collective-permute-start.35 = (bf16[256,768]{1,0:T(8,128)(2,1)S(1)}, bf16[256,768]{1,0:T(8,128)(2,1)S(1)}, u32[]{:S(2)}, u32[]{:S(2)}) collective-permute-start(bf16[256,768]{1,0:T(8,128)(2,1)S(1)} %get-tuple-element.110), channel_id=1, source_target_pairs={{0,2},{2,4},{4,6},{1,3},{3,5},{5,7},{8,10},{10,12},{12,14},{9,11},... | collective-permute-start | bytes 1179656 | tf_op jit(solution)/shard_map/ppermute | solution.py:445
  214.9 14.7 %collective-permute-start.41 = (bf16[256,768]{1,0:T(8,128)(2,1)S(1)}, bf16[256,768]{1,0:T(8,128)(2,1)S(1)}, u32[]{:S(2)}, u32[]{:S(2)}) collective-permute-start(bf16[256,768]{1,0:T(8,128)(2,1)S(1)} %broadcast_select_fusion.2), channel_id=1, source_target_pairs={{0,2},{6,4},{1,3},{7,5},{8,10},{14,12},{9,11},{15,13},{16,18},{22,... | collective-permute-start | bytes 1179656 | tf_op jit(solution)/shard_map/ppermute | solution.py:442
  228.4 10.5 %collective-permute-start.39 = (bf16[2,2,32,1344]{3,2,1,0:T(8,128)(2,1)S(1)}, bf16[2,2,32,1344]{3,2,1,0:T(8,128)(2,1)S(1)}, u32[]{:S(2)}, u32[]{:S(2)}) collective-permute-start(bf16[2,2,32,1344]{3,2,1,0:T(8,128)(2,1)S(1)} %dynamic-slice_bitcast_fusion), channel_id=1, source_target_pairs={{0,8},{8,0},{1,9},{9,1},{2,10},{10,2},{3,11},{11,3},{4,12},{12,4},... | collective-permute-start | bytes 1032200 | tf_op jit(solution)/shard_map/ppermute | solution.py:391
  229.7 21.2 %collective-permute-start.42 = (bf16[256,768]{1,0:T(8,128)(2,1)S(1)}, bf16[256,768]{1,0:T(8,128)(2,1)S(1)}, u32[]{:S(2)}, u32[]{:S(2)}) collective-permute-start(bf16[256,768]{1,0:T(8,128)(2,1)S(1)} %add_convert_fusion.1), channel_id=1, source_target_pairs={{0,4},{2,6},{4,0},{6,2},{1,5},{3,7},{5,1},{7,3},{8,12},{10,14},{12... | collective-permute-start | bytes 1179656 | tf_op jit(solution)/shard_map/ppermute | solution.py:391
  231.9 11.0 %collective-permute-start.37 = (bf16[2,2,32,1344]{3,2,1,0:T(8,128)(2,1)S(1)}, bf16[2,2,32,1344]{3,2,1,0:T(8,128)(2,1)S(1)}, u32[]{:S(2)}, u32[]{:S(2)}) collective-permute-start(bf16[2,2,32,1344]{3,2,1,0:T(8,128)(2,1)S(1)} %dynamic-slice_bitcast_fusion.1), channel_id=1, source_target_pairs={{0,16},{16,0},{1,17},{17,1},{2,18},{18,2},{3,19},{19,3},{4,20},{20... | collective-permute-start | bytes 1032200 | tf_op jit(solution)/shard_map/ppermute | solution.py:391
  239.0 8.3 %collective-permute-start.40 = (bf16[2,32,1344]{2,1,0:T(8,128)(2,1)S(1)}, bf16[2,32,1344]{2,1,0:T(8,128)(2,1)S(1)}, u32[]{:S(2)}, u32[]{:S(2)}) collective-permute-start(bf16[2,32,1344]{2,1,0:T(8,128)(2,1)S(1)} %fusion.5), channel_id=1, source_target_pairs={{0,16},{16,0},{1,17},{17,1},{2,18},{18,2},{3,19},{19,3},{4,20},{20... | collective-permute-start | bytes 516104 | tf_op jit(solution)/shard_map/ppermute | solution.py:391
  243.0 7.9 %collective-permute-start.38 = (bf16[2,32,1344]{2,1,0:T(8,128)(2,1)S(1)}, bf16[2,32,1344]{2,1,0:T(8,128)(2,1)S(1)}, u32[]{:S(2)}, u32[]{:S(2)}) collective-permute-start(bf16[2,32,1344]{2,1,0:T(8,128)(2,1)S(1)} %fusion.4), channel_id=1, source_target_pairs={{0,8},{8,0},{1,9},{9,1},{2,10},{10,2},{3,11},{11,3},{4,12},{12,4},... | collective-permute-start | bytes 516104 | tf_op jit(solution)/shard_map/ppermute | solution.py:391
  251.1 7.3 %collective-permute-start.44 = (bf16[32,1344]{1,0:T(8,128)(2,1)S(1)}, bf16[32,1344]{1,0:T(8,128)(2,1)S(1)}, u32[]{:S(2)}, u32[]{:S(2)}) collective-permute-start(bf16[32,1344]{1,0:T(8,128)(2,1)S(1)} %get-tuple-element.177), channel_id=1, source_target_pairs={{0,2},{2,4},{4,6},{6,0},{1,3},{3,5},{5,7},{7,1},{8,10},{10,12},{12... | collective-permute-start | bytes 258056 | tf_op jit(solution)/shard_map/ppermute | solution.py:391
  251.2 9.2 %collective-permute-start.45 = (bf16[32,1344]{1,0:T(8,128)(2,1)S(1)}, bf16[32,1344]{1,0:T(8,128)(2,1)S(1)}, u32[]{:S(2)}, u32[]{:S(2)}) collective-permute-start(bf16[32,1344]{1,0:T(8,128)(2,1)S(1)} %get-tuple-element.176), channel_id=1, source_target_pairs={{0,4},{2,6},{4,0},{6,2},{1,5},{3,7},{5,1},{7,3},{8,12},{10,14},{12... | collective-permute-start | bytes 258056 | tf_op jit(solution)/shard_map/ppermute | solution.py:391
  253.3 7.1 %collective-permute-start.46 = (bf16[32,1344]{1,0:T(8,128)(2,1)S(1)}, bf16[32,1344]{1,0:T(8,128)(2,1)S(1)}, u32[]{:S(2)}, u32[]{:S(2)}) collective-permute-start(bf16[32,1344]{1,0:T(8,128)(2,1)S(1)} %get-tuple-element.175), channel_id=1, source_target_pairs={{0,6},{2,0},{4,2},{6,4},{1,7},{3,1},{5,3},{7,5},{8,14},{10,8},{12,... | collective-permute-start | bytes 258056 | tf_op jit(solution)/shard_map/ppermute | solution.py:391
  (59 other events, 247.3 us)
where the time goes:
time: 266 us; the launch traced here: 263 us
  starting transfers between devices  86.2 us (32%)
  waiting for transfers between devices  71.1 us (27%)
  Pallas kernels  60.7 us (23%)
  local copies, waits for them, and re-layouts  26.1 us (10%)
  other arithmetic  16.1 us (6%)
  between operations  3.38 us (1%)
    ppermute x48, waiting for transfers between devices, shift(): lax.ppermute(array, axis, [(i, (i + hop) % size) for i in range(size)])  70.6 us
    ppermute x48, starting transfers between devices, shift(): lax.ppermute(array, axis, [(i, (i + hop) % size) for i in range(size)])  66.6 us
    pallas_call x11, Pallas kernels, kernel_call(): pl.pallas_call(body, out_shape=tuple((jax.ShapeDtypeStruct(shape, dtype)...  33.8 us
    pallas_call x2, Pallas kernels, attend_back(): pl.pallas_call(functools.partial(attend_back_kernel, first), out_shape=tu...  16.6 us
    unnamed x117, local copies, waits for them, and re-layouts  15.7 us
    pallas_call x1, Pallas kernels, attend(): pl.pallas_call(attend_kernel, out_shape=(jax.ShapeDtypeStruct((rows, GW),...  10.3 us
    ppermute x1, starting transfers between devices, z_reduce(): up = lax.ppermute(sent[0], 'z', [(0, 1), (1, 2), (2, 3)])  9.68 us
    ppermute x1, starting transfers between devices, z_reduce(): edge = lax.ppermute(edge, 'z', [(0, 1), (NZ - 1, NZ - 2)])  8.55 us
  transfers between devices with their start and end apart: 51, of which 22 were waited for; matrix products, arithmetic and copies ran while one was open for 8% of the time, Pallas kernels for 20%

commit v1 on v0

--- a/solution.py
+++ b/solution.py
@@ -401,16 +401,21 @@
     return jnp.stack([first, second], axis=axis)
 
 
-def z_pieces(block):
-    return [block] + [shift(block, "z", NZ, j) for j in range(1, NZ)]
+def hops(send, order):
+    got = {hop: send(hop) for hop in order}
+    return [got[hop] for hop in range(1, NZ)]
+
+
+def z_pieces(block, order):
+    return [block] + hops(lambda hop: shift(block, "z", NZ, hop), order)
 
 
 def z_order(pieces, z):
     return jnp.stack([lax.select_n((z - a) % NZ, *pieces) for a in range(NZ)])
 
 
-def z_exchange(array, z):
-    return [pick(array, z)] + [shift(pick(array, (z + j) % NZ), "z", NZ, j) for j in range(1, NZ)]
+def z_exchange(array, z, order):
+    return [pick(array, z)] + hops(lambda hop: shift(pick(array, (z + hop) % NZ), "z", NZ, hop), order)
 
 
 def xy_gather(line, y, x):
@@ -524,7 +529,9 @@
 }
 
 
-WEIGHT = {'branch': 3, 'feed': 10, 'feed_weights': 3, 'middle': 3, 'inward': 3, 'owners': 3, 'finish': 10, 'deliver': 3, 'weave': 3}
+WEIGHT = {
+    "project": 1, "branch": 3, "feed": 10, "feed_weights": 3, "middle": 3, "inward": 3, "owners": 3, "finish": 10, "deliver": 3, "weave": 3,
+}
 
 
 def kernel_call(body, place, arrays, in_specs, outs, out_specs, grid, scratch, flops, name, more=()):
@@ -1098,16 +1105,15 @@
             at = pl.ds(pl.multiple_of(lax.rem(z - r + NZ, NZ) * CHUNK, CHUNK), CHUNK)
             for h in range(GROUP):
                 do_s[h, at] = ref[:, HEAD_DIM * h : HEAD_DIM * (h + 1)]
-        ones = jnp.ones((8, HEAD_DIM), jnp.float32)
+        ones = jnp.ones((8, HEAD_DIM), jnp.bfloat16)
         for h in range(GROUP):
             lanes = slice(HEAD_DIM * h, HEAD_DIM * (h + 1))
             q_s[h] = q_ref[:, lanes]
             if first:
                 both = do_s[h].astype(jnp.float32) * from_ref[:, lanes]
-                delta_ref[h : h + 1] = lax.dot_general(
-                    ones, both, (((1,), (1,)), ((), ())), precision=lax.Precision.HIGHEST,
-                    preferred_element_type=jnp.float32,
-                )[0:1]
+                high = both.astype(jnp.bfloat16)
+                rest = (both - high.astype(jnp.float32)).astype(jnp.bfloat16)
+                delta_ref[h : h + 1] = (dot_nt(ones, high) + dot_nt(ones, rest))[0:1]
         dqt_ref[...] = jnp.zeros(dqt_ref.shape, jnp.float32) if first else old_ref[...]
         if first:
             delta_ref[GROUP:] = jnp.zeros((8 - GROUP, rows), jnp.float32)
@@ -1220,17 +1226,17 @@
         [jnp.broadcast_to(out_weight[None], (NZ, own_rows, width)), wz], axis=2
     )
     group1 = jnp.concatenate([group1, jnp.broadcast_to(extra[None], (NZ, 8, span))], axis=1)
-    pieces1 = z_exchange(group1, z)
+    pieces1 = z_exchange(group1, z, (2, 3, 1))
 
     up_sets = up_weight.reshape(own_rows, pairs, 2, units).transpose(2, 0, 1, 3)
     up_sets = up_sets.reshape(2, own_rows, half)
     up_chip = in_order(pick(up_sets, c), swap(pick(up_sets, 1 - c), "c"), c, 0)
     up_chip = up_chip.reshape(2 * own_rows, half)
     group2 = jnp.concatenate([up_chip[:, :width], up_chip[:, width:], down_weight], axis=0)
-    pieces2 = z_pieces(group2)
+    pieces2 = z_pieces(group2, (3, 1, 2))
 
     own, pieces2[1], pieces2[3] = meet(tokens[0], pieces2[1], pieces2[3])
-    line_pieces = z_pieces(own)
+    line_pieces = z_pieces(own, (2, 1, 3))
     group1 = z_order(pieces1, z)
     own_seg = group1[:, own_rows, cuts[-1] : cuts[-1] + rows].astype(wide)
     seg = in_order(own_seg, swap(own_seg, "c"), c, 1).reshape(keys // CHUNK, CHUNK)
@@ -1265,7 +1271,7 @@
     line, n1, q, kv = project(place, line_pieces, vec, wz)
     kv_theirs = swap(kv, "c")
     att_wide, att_low, lse = attend(active, may, place, q, kv, kv_theirs, own_seg, seg)
-    att = z_exchange(att_low.reshape(NZ, rows, GW), z)
+    att = z_exchange(att_low.reshape(NZ, rows, GW), z, (2, 1, 3))
     group2 = [in_order(own_half, after(other, att_low), at, axis) for own_half, other, at, axis in group2]
     group2 = jnp.concatenate(group2, axis=2)
 
@@ -1285,7 +1291,7 @@
     output, grad_hidden, grad_branch, *grad_att, mid = middle(
         place, m_part, out_part, sums, hidden, go, vec, wo
     )
-    dout = [grad_att[0]] + [shift(grad_att[j], "z", NZ, j) for j in range(1, NZ)]
+    dout = [grad_att[0]] + hops(lambda hop: shift(grad_att[hop], "z", NZ, hop), (3, 1, 2))
     a, b = add_up(a_kept, a_sent, "y"), add_up(b_kept, b_sent, "x")
 
     dq_part, delta, dkv_theirs = attend_back(
@@ -1297,7 +1303,6 @@
         False, active, may, place, q, dout, kv, lse, own_seg, seg, delta, dq_part
     )
     dqkv, m1_own, *m1_sent, cols, dqkv_sum = inward(place, dq, dkv_mine, swap(dkv_theirs, "c"), line, wz)
-    a, b, m1_sent[0] = meet(a, b, m1_sent[0])
     group2 = jnp.concatenate([a, b], axis=0)
     m1_up, m1_far, m1_down = z_reduce(m1_sent, z)
 
@@ -1312,7 +1317,7 @@
     a, b, m1_far, m1_down = meet(a, b, m1_far, m1_down)
     grad_tokens = finish(place, m1_own, (m1_up, m1_far, m1_down), own, grad_hidden, vec)
     group1 = jnp.concatenate([a, b], axis=0)
-    pieces = z_exchange(group1.astype(low), z)
+    pieces = z_exchange(group1.astype(low), z, (1, 2, 3))
     arrays = (pick(group1, z), *pieces[1:])
     outs = [((own_rows, 3 * width), wide), ((own_rows, width), wide), ((tall - own_rows, span), wide)]
     grad_qkv, grad_wo, vec_sum = kernel_call(
@@ -1323,7 +1328,7 @@
 
     group2_low = group2.astype(low)
     sent = [pick(group2_low, (z + j) % NZ) for j in range(1, NZ)]
-    group2 = sum((piece.astype(wide) for piece in [shift(p, "z", NZ, j) for j, p in enumerate(sent, 1)]), pick(group2, z))
+    group2 = sum((piece.astype(wide) for piece in hops(lambda hop: shift(sent[hop - 1], "z", NZ, hop), (2, 3, 1))), pick(group2, z))
     grad_down = group2[units:]
     up_rows = jnp.concatenate([group2[: 2 * own_rows], group2[2 * own_rows : units]], axis=1)
     up_rows = up_rows.reshape(2, own_rows, half)

time: 266 us -> 263 us (0.989)
  Pallas kernels: 60.7 us -> 68.2 us
  local copies, waits for them, and re-layouts: 26.1 us -> 21.4 us
    ppermute x1, waiting for transfers between devices: 0.47 us -> 6.07 us  [z_reduce(): edge = lax.ppermute(edge, 'z', [(0, 1), (NZ - 1, NZ - 2)])]
    pallas_call x2, Pallas kernels: 16.6 us -> 22 us  [attend_back(): pl.pallas_call(functools.partial(attend_back_kernel, first), out_shape=tu...]
    ppermute x48, waiting for transfers between devices: 70.6 us -> 65.6 us  [shift(): lax.ppermute(array, axis, [(i, (i + hop) % size) for i in range(size)])]
    unnamed x117 -> x122, local copies, waits for them, and re-layouts: 15.7 us -> 11.9 us
  transfers between devices with their start and end apart: 51 -> 51, of which waited for: 22 -> 21; matrix products, arithmetic and copies ran while one was open for 8% -> 7% of each run, Pallas kernels for 20% -> 23%
where the time goes in v1:
time: 263 us; the launch traced here: 262 us
  starting transfers between devices  83.8 us (32%)
  waiting for transfers between devices  71.6 us (27%)
  Pallas kernels  68.2 us (26%)
  local copies, waits for them, and re-layouts  21.4 us (8%)
  other arithmetic  13.9 us (5%)
  between operations  3.45 us (1%)
    ppermute x48, waiting for transfers between devices, shift(): lax.ppermute(array, axis, [(i, (i + hop) % size) for i in range(size)])  65.6 us
    ppermute x48, starting transfers between devices, shift(): lax.ppermute(array, axis, [(i, (i + hop) % size) for i in range(size)])  65.4 us
    pallas_call x11, Pallas kernels, kernel_call(): pl.pallas_call(body, out_shape=tuple((jax.ShapeDtypeStruct(shape, dtype)...  34.1 us
    pallas_call x2, Pallas kernels, attend_back(): pl.pallas_call(functools.partial(attend_back_kernel, first), out_shape=tu...  22 us
    pallas_call x1, Pallas kernels, attend(): pl.pallas_call(attend_kernel, out_shape=(jax.ShapeDtypeStruct((rows, GW),...  12.1 us
    unnamed x122, local copies, waits for them, and re-layouts  11.9 us
    ppermute x1, starting transfers between devices, z_reduce(): up = lax.ppermute(sent[0], 'z', [(0, 1), (1, 2), (2, 3)])  9.21 us
    ppermute x1, starting transfers between devices, z_reduce(): edge = lax.ppermute(edge, 'z', [(0, 1), (NZ - 1, NZ - 2)])  7.94 us
  transfers between devices with their start and end apart: 51, of which 21 were waited for; matrix products, arithmetic and copies ran while one was open for 7% of the time, Pallas kernels for 23%

profile of v1, /device:TPU:0, one launch (start us, length us, event | category | flops | bytes accessed | tf_op | source)
XLA Modules:
  0.0 262.4 jit_solution(12834030813605512419)
XLA Ops:
  4.5 3.1 %collective-permute-start = (bf16[32,1344]{1,0:T(8,128)(2,1)S(1)}, bf16[32,1344]{1,0:T(8,128)(2,1)S(1)}, u32[]{:S(2)}, u32[]{:S(2)}) collective-permute-start(bf16[32,1344]{1,0:T(8,128)(2,1)S(1)} %get-tuple-element.178), channel_id=1, source_target_pairs={{0,2},{2,4},{4,6},{6,0},{1,3},{3,5},{5,7},{7,1},{8,10},{10,12},{12... | collective-permute-start | bytes 258056 | tf_op jit(solution)/shard_map/ppermute | solution.py:391
  7.6 2.6 collective-permute-start.1
  10.2 1.3 collective-permute-start.2
  13.4 2.8 %collective-permute-done.1 = bf16[32,1344]{1,0:T(8,128)(2,1)S(1)} collective-permute-done((bf16[32,1344]{1,0:T(8,128)(2,1)S(1)}, bf16[32,1344]{1,0:T(8,128)(2,1)S(1)}, u32[]{:S(2)}, u32[]{:S(2)}) %collective-permute-start.1) | collective-permute-done | bytes 86048 | tf_op jit(solution)/shard_map/ppermute | solution.py:391
  16.5 1.6 collective-permute-start.11
  18.1 1.6 collective-permute-start.13
  20.4 2.2 collective-permute-start.5
  22.6 1.6 collective-permute-start.6
  26.3 9.9 %collective-permute-done.12 = bf16[2,2,32,1344]{3,2,1,0:T(8,128)(2,1)S(1)} collective-permute-done((bf16[2,2,32,1344]{3,2,1,0:T(8,128)(2,1)S(1)}, bf16[2,2,32,1344]{3,2,1,0:T(8,128)(2,1)S(1)}, u32[]{:S(2)}, u32[]{:S(2)}) %collective-permute-start.12) | collective-permute-done | bytes 344096 | tf_op jit(solution)/shard_map/ppermute | solution.py:391
  36.8 9.5 %collective-permute-done.14 = bf16[2,2,32,1344]{3,2,1,0:T(8,128)(2,1)S(1)} collective-permute-done((bf16[2,2,32,1344]{3,2,1,0:T(8,128)(2,1)S(1)}, bf16[2,2,32,1344]{3,2,1,0:T(8,128)(2,1)S(1)}, u32[]{:S(2)}, u32[]{:S(2)}) %collective-permute-start.14) | collective-permute-done | bytes 344096 | tf_op jit(solution)/shard_map/ppermute | solution.py:391
  48.0 2.1 collective-permute-start.7
  51.2 2.5 collective-permute-start.9
  53.8 1.4 select_bitcast_fusion.16
  55.2 1.4 select_bitcast_fusion.17
  58.1 1.8 select_bitcast_fusion.1
  62.0 1.4 fusion.30
  64.7 13.6 %collective-permute-done.8.t2_ref = bf16[256,768]{1,0:T(8,128)(2,1)S(1)} collective-permute-done((bf16[256,768]{1,0:T(8,128)(2,1)S(1)}, bf16[256,768]{1,0:T(8,128)(2,1)S(1)}, u32[]{:S(2)}, u32[]{:S(2)}) %collective-permute-start.8) | collective-permute-done | bytes 393248 | tf_op jit(solution)/shard_map/ppermute | solution.py:391
  78.3 4.2 %project.1 = (bf16[1024,768]{1,0:T(8,128)(2,1)S(1)}, bf16[1024,768]{1,0:T(8,128)(2,1)S(1)}, bf16[1024,192]{1,0:T(8,128)(2,1)S(1)}, bf16[1024,384]{1,0:T(8,128)(2,1)S(1)}) custom-call(s32[4]{0:T(128)S(1)} %pad_add_fusion.1.place_ref.refs_2_, bf16[256,768]{1,0:T(8,128)(2,1)S(1)} %bitcast.237, bf16[256,768]{1,0:T(8,128)(2,1)S(1)} %collective-permute-done.7.t1_ref, ...), custom_call_target="tpu_custom_call" | custom-call | flops 3623878656 | bytes 2506752 | tf_op jit(solution)/shard_map/project/pallas_call | solution.py:540
  86.1 12.1 %attend.1 = (f32[1024,192]{1,0:T(8,128)S(1)}, bf16[1024,192]{1,0:T(8,128)(2,1)S(1)}, f32[8,1024]{1,0:T(8,128)S(1)}) custom-call(s32[4,8]{1,0:T(4,128)S(1)} %convert_element_type.157.act_ref.refs_0_, s32[8,16]{1,0:T(8,128)S(1)} %fusion.24.may_ref.refs_1_, s32[4]{0:T(128)S(1)} %pad_add_fusion.1.place_ref.refs_2_, ...), custom_call_target="tpu_custom_call" | custom-call | flops 19327352832 | bytes 6291456 | tf_op jit(solution)/shard_map/attend/pallas_call | solution.py:1057
  98.3 9.0 %collective-permute-start.17 = (bf16[256,192]{1,0:T(8,128)(2,1)S(1)}, bf16[256,192]{1,0:T(8,128)(2,1)S(1)}, u32[]{:S(2)}, u32[]{:S(2)}) collective-permute-start(bf16[256,192]{1,0:T(8,128)(2,1)S(1)} %get-tuple-element.167), channel_id=1, source_target_pairs={{0,2},{2,4},{4,6},{6,0},{1,3},{3,5},{5,7},{7,1},{8,10},{10,12},{12... | collective-permute-start | bytes 294920 | tf_op jit(solution)/shard_map/ppermute | solution.py:391
  107.3 1.9 collective-permute-start.18
  113.0 5.1 %collective-permute-done.18.a2_ref = bf16[256,192]{1,0:T(8,128)(2,1)S(1)} collective-permute-done((bf16[256,192]{1,0:T(8,128)(2,1)S(1)}, bf16[256,192]{1,0:T(8,128)(2,1)S(1)}, u32[]{:S(2)}, u32[]{:S(2)}) %collective-permute-start.18) | collective-permute-done | bytes 98336 | tf_op jit(solution)/shard_map/ppermute | solution.py:391
  121.2 7.0 %feed.1 = (bf16[512,1536]{1,0:T(8,128)(2,1)S(1)}, bf16[512,1536]{1,0:T(8,128)(2,1)S(1)}, f32[256,768]{1,0:T(8,128)S(1)}, f32[256,768]{1,0:T(8,128)S(1)}, bf16[2,...) custom-call(s32[4]{0:T(128)S(1)} %pad_add_fusion.1.place_ref.refs_2_, bf16[256,768]{1,0:T(8,128)(2,1)S(1)} %get-tuple-element.77.na_ref, ...), custom_call_target="tpu_custom_call" | custom-call | flops 96636764160 | bytes 110161920 | tf_op jit(solution)/shard_map/feed/pallas_call | solution.py:540
  128.4 6.1 %feed_weights.1 = (bf16[2,2,192,768]{3,2,1,0:T(8,128)(2,1)S(1)}, bf16[2,2,192,768]{3,2,1,0:T(8,128)(2,1)S(1)}, bf16[2,2,192,768]{3,2,1,0:T(8,128)(2,1)S(1)}, bf16[2,2,192,768]{3,2,1,0:T(8,128)(2,1)}) custom-call(s32[4]{0:T(128)S(1)} %pad_add_fusion.1.place_ref.refs_2_, bf16[256,768]{1,0:T(8,128)(2,1)S(1)} %get-tuple-element.77.na_ref, ...), custom_call_target="tpu_custom_call" | custom-call | flops 7247757312 | bytes 14155776 | tf_op jit(solution)/shard_map/feed_weights/pallas_call | solution.py:540
  134.8 2.5 middle.1
  139.4 3.0 %collective-permute-start.27 = (bf16[256,192]{1,0:T(8,128)(2,1)}, bf16[256,192]{1,0:T(8,128)(2,1)}, u32[]{:S(2)}, u32[]{:S(2)}) collective-permute-start(bf16[256,192]{1,0:T(8,128)(2,1)} %get-tuple-element.85), channel_id=1, source_target_pairs={{0,2},{2,4},{4,6},{6,0},{1,3},{3,5},{5,7},{7,1},{8,10},{10,12},{12... | collective-permute-start | bytes 294920 | tf_op jit(solution)/shard_map/ppermute | solution.py:391
  146.0 1.9 collective-permute-done.27.refs_5_
  147.9 5.0 %collective-permute-done.28.refs_6_ = bf16[256,192]{1,0:T(8,128)(2,1)} collective-permute-done((bf16[256,192]{1,0:T(8,128)(2,1)}, bf16[256,192]{1,0:T(8,128)(2,1)}, u32[]{:S(2)}, u32[]{:S(2)}) %collective-permute-start.28) | collective-permute-done | bytes 98336 | tf_op jit(solution)/shard_map/ppermute | solution.py:391
  159.3 9.2 %attend_back_first.1 = (f32[3,64,1024]{2,1,0:T(8,128)S(1)}, f32[8,1024]{1,0:T(8,128)S(1)}, bf16[1024,384]{1,0:T(8,128)(2,1)S(1)}) custom-call(s32[4,8]{1,0:T(4,128)S(1)} %copy-done.25, s32[8,16]{1,0:T(8,128)S(1)} %copy-done.23, s32[4]{0:T(128)S(1)} %pad_add_fusion.1.place_ref.refs_2_, bf16[1024,192]{1,0:T(8,128)(2,1)S(1)} %copy-done.36, ...), custom_call_target="tpu_custom_call" | custom-call | flops 11274289152 | bytes 6291456 | tf_op jit(solution)/shard_map/attend_back_first/pallas_call | solution.py:1173
  169.8 1.5 convert_add_fusion
  175.7 12.8 %attend_back_last.1 = (bf16[1024,192]{1,0:T(8,128)(2,1)S(1)}, bf16[1024,384]{1,0:T(8,128)(2,1)S(1)}) custom-call(s32[4,8]{1,0:T(4,128)S(1)} %copy-done.26, s32[8,16]{1,0:T(8,128)S(1)} %copy-done.23, s32[4]{0:T(128)S(1)} %pad_add_fusion.1.place_ref.refs_2_, bf16[1024,192]{1,0:T(8,128)(2,1)S(1)} %copy-done.37, bf16[256,192]{1,0:T(8,128)(2,1)S(1)} %copy-done.39, ...), custom_call_target="tpu_custom_call" | custom-call | flops 11274289152 | bytes 6291456 | tf_op jit(solution)/shard_map/attend_back_last/pallas_call | solution.py:1173
  189.7 3.4 %collective-permute-start.47 = (bf16[192,768]{1,0:T(8,128)(2,1)S(1)}, bf16[192,768]{1,0:T(8,128)(2,1)S(1)}, u32[]{:S(2)}, u32[]{:S(2)}) collective-permute-start(bf16[192,768]{1,0:T(8,128)(2,1)S(1)} %get-tuple-element.144), channel_id=1, source_target_pairs={{0,2},{2,4},{4,6},{6,0},{1,3},{3,5},{5,7},{7,1},{8,10},{10,12},{12... | collective-permute-start | bytes 884744 | tf_op jit(solution)/shard_map/ppermute | solution.py:391
  195.7 4.0 %inward.1 = (bf16[1024,576]{1,0:T(8,128)(2,1)S(1)}, f32[256,768]{1,0:T(8,128)S(1)}, bf16[256,768]{1,0:T(8,128)(2,1)S(1)}, bf16[256,768]{1,0:T(8,128)(2,1)S(1)}, ...) custom-call(s32[4]{0:T(128)S(1)} %pad_add_fusion.1.place_ref.refs_2_, ...), custom_call_target="tpu_custom_call" | custom-call | flops 10871635968 | bytes 13271040 | tf_op jit(solution)/shard_map/inward/pallas_call | solution.py:540
  199.8 3.2 %owners.1 = (bf16[16,32,1344]{2,1,0:T(8,128)(2,1)S(1)}, bf16[16,32,1344]{2,1,0:T(8,128)(2,1)S(1)}) custom-call(s32[4]{0:T(128)S(1)} %pad_add_fusion.1.place_ref.refs_2_, bf16[256,192]{1,0:T(8,128)(2,1)S(1)} %copy-done.5, bf16[256,192]{1,0:T(8,128)(2,1)S(1)} %copy-done.13, bf16[256,192]{1,0:T(8,128)(2,1)S(1)} %copy-done.15, bf16[256,192]{1,0:T(8,128)(2,1)S(1)} %copy-done.17, ...), custom_call_target="tpu_custom_call" | custom-call | flops 3145728 | bytes 10838016 | tf_op jit(solution)/shard_map/owners/pallas_call | solution.py:540
  204.4 9.2 %collective-permute-start.33 = (bf16[256,768]{1,0:T(8,128)(2,1)S(1)}, bf16[256,768]{1,0:T(8,128)(2,1)S(1)}, u32[]{:S(2)}, u32[]{:S(2)}) collective-permute-start(bf16[256,768]{1,0:T(8,128)(2,1)S(1)} %get-tuple-element.104), channel_id=1, source_target_pairs={{0,2},{2,4},{4,6},{1,3},{3,5},{5,7},{8,10},{10,12},{12,14},{9,11},... | collective-permute-start | bytes 1179656 | tf_op jit(solution)/shard_map/ppermute | solution.py:450
  213.6 7.9 %collective-permute-start.39 = (bf16[256,768]{1,0:T(8,128)(2,1)S(1)}, bf16[256,768]{1,0:T(8,128)(2,1)S(1)}, u32[]{:S(2)}, u32[]{:S(2)}) collective-permute-start(bf16[256,768]{1,0:T(8,128)(2,1)S(1)} %broadcast_select_fusion.2), channel_id=1, source_target_pairs={{0,2},{6,4},{1,3},{7,5},{8,10},{14,12},{9,11},{15,13},{16,18},{22,... | collective-permute-start | bytes 1179656 | tf_op jit(solution)/shard_map/ppermute | solution.py:447
  221.9 6.1 %collective-permute-done.39 = bf16[256,768]{1,0:T(8,128)(2,1)S(1)} collective-permute-done((bf16[256,768]{1,0:T(8,128)(2,1)S(1)}, bf16[256,768]{1,0:T(8,128)(2,1)S(1)}, u32[]{:S(2)}, u32[]{:S(2)}) %collective-permute-start.39) | collective-permute-done | bytes 393248 | tf_op jit(solution)/shard_map/ppermute | solution.py:447
  228.6 2.2 collective-permute-start.37
  231.6 2.5 collective-permute-start.40
  234.1 1.5 weave.1
  235.6 1.5 collective-permute-start.35
  237.2 2.0 collective-permute-start.38
  239.2 5.0 %collective-permute-done.35 = bf16[2,2,32,1344]{3,2,1,0:T(8,128)(2,1)S(1)} collective-permute-done((bf16[2,2,32,1344]{3,2,1,0:T(8,128)(2,1)S(1)}, bf16[2,2,32,1344]{3,2,1,0:T(8,128)(2,1)S(1)}, u32[]{:S(2)}, u32[]{:S(2)}) %collective-permute-start.35) | collective-permute-done | bytes 344096 | tf_op jit(solution)/shard_map/ppermute | solution.py:391
  246.2 3.7 %collective-permute-done.36 = bf16[2,32,1344]{2,1,0:T(8,128)(2,1)S(1)} collective-permute-done((bf16[2,32,1344]{2,1,0:T(8,128)(2,1)S(1)}, bf16[2,32,1344]{2,1,0:T(8,128)(2,1)S(1)}, u32[]{:S(2)}, u32[]{:S(2)}) %collective-permute-start.36) | collective-permute-done | bytes 172064 | tf_op jit(solution)/shard_map/ppermute | solution.py:391
  251.1 2.6 %collective-permute-start.43 = (bf16[32,1344]{1,0:T(8,128)(2,1)S(1)}, bf16[32,1344]{1,0:T(8,128)(2,1)S(1)}, u32[]{:S(2)}, u32[]{:S(2)}) collective-permute-start(bf16[32,1344]{1,0:T(8,128)(2,1)S(1)} %get-tuple-element.170), channel_id=1, source_target_pairs={{0,4},{2,6},{4,0},{6,2},{1,5},{3,7},{5,1},{7,3},{8,12},{10,14},{12... | collective-permute-start | bytes 258056 | tf_op jit(solution)/shard_map/ppermute | solution.py:391
  254.3 2.1 finish.1
  256.6 2.2 collective-permute-done.43.p2_ref
  259.3 1.3 deliver.1
  (298 shorter events, 56.8 us)
Async XLA Ops:
  4.5 8.9 %collective-permute-start = (bf16[32,1344]{1,0:T(8,128)(2,1)S(1)}, bf16[32,1344]{1,0:T(8,128)(2,1)S(1)}, u32[]{:S(2)}, u32[]{:S(2)}) collective-permute-start(bf16[32,1344]{1,0:T(8,128)(2,1)S(1)} %get-tuple-element.178), channel_id=1, source_target_pairs={{0,2},{2,4},{4,6},{6,0},{1,3},{3,5},{5,7},{7,1},{8,10},{10,12},{12... | collective-permute-start | bytes 258056 | tf_op jit(solution)/shard_map/ppermute | solution.py:391
  7.6 8.6 %collective-permute-start.1 = (bf16[32,1344]{1,0:T(8,128)(2,1)S(1)}, bf16[32,1344]{1,0:T(8,128)(2,1)S(1)}, u32[]{:S(2)}, u32[]{:S(2)}) collective-permute-start(bf16[32,1344]{1,0:T(8,128)(2,1)S(1)} %get-tuple-element.177), channel_id=1, source_target_pairs={{0,4},{2,6},{4,0},{6,2},{1,5},{3,7},{5,1},{7,3},{8,12},{10,14},{12... | collective-permute-start | bytes 258056 | tf_op jit(solution)/shard_map/ppermute | solution.py:391
  10.2 6.2 %collective-permute-start.2 = (bf16[32,1344]{1,0:T(8,128)(2,1)S(1)}, bf16[32,1344]{1,0:T(8,128)(2,1)S(1)}, u32[]{:S(2)}, u32[]{:S(2)}) collective-permute-start(bf16[32,1344]{1,0:T(8,128)(2,1)S(1)} %get-tuple-element.176), channel_id=1, source_target_pairs={{0,6},{2,0},{4,2},{6,4},{1,7},{3,1},{5,3},{7,5},{8,14},{10,8},{12,... | collective-permute-start | bytes 258056 | tf_op jit(solution)/shard_map/ppermute | solution.py:391
  16.5 8.5 %collective-permute-start.11 = (bf16[2,32,1344]{2,1,0:T(8,128)(2,1)S(1)}, bf16[2,32,1344]{2,1,0:T(8,128)(2,1)S(1)}, u32[]{:S(2)}, u32[]{:S(2)}) collective-permute-start(bf16[2,32,1344]{2,1,0:T(8,128)(2,1)S(1)} %pad_maximum_fusion.11), channel_id=1, source_target_pairs={{0,8},{8,0},{1,9},{9,1},{2,10},{10,2},{3,11},{11,3},{4,12},{12,4},... | collective-permute-start | bytes 516104 | tf_op jit(solution)/shard_map/ppermute | solution.py:391
  18.1 7.0 %collective-permute-start.13 = (bf16[2,32,1344]{2,1,0:T(8,128)(2,1)S(1)}, bf16[2,32,1344]{2,1,0:T(8,128)(2,1)S(1)}, u32[]{:S(2)}, u32[]{:S(2)}) collective-permute-start(bf16[2,32,1344]{2,1,0:T(8,128)(2,1)S(1)} %pad_maximum_fusion.12), channel_id=1, source_target_pairs={{0,16},{16,0},{1,17},{17,1},{2,18},{18,2},{3,19},{19,3},{4,20},{20... | collective-permute-start | bytes 516104 | tf_op jit(solution)/shard_map/ppermute | solution.py:391
  20.4 27.5 %collective-permute-start.5 = (bf16[192,768]{1,0:T(8,128)(2,1)}, bf16[192,768]{1,0:T(8,128)(2,1)}, u32[]{:S(2)}, u32[]{:S(2)}) collective-permute-start(bf16[192,768]{1,0:T(8,128)(2,1)} %pad_maximum_fusion.9), channel_id=1, source_target_pairs={{0,2},{2,4},{4,6},{6,0},{1,3},{3,5},{5,7},{7,1},{8,10},{10,12},{12... | collective-permute-start | bytes 884744 | tf_op jit(solution)/shard_map/ppermute | solution.py:391
  22.6 25.3 %collective-permute-start.6 = (bf16[192,768]{1,0:T(8,128)(2,1)}, bf16[192,768]{1,0:T(8,128)(2,1)}, u32[]{:S(2)}, u32[]{:S(2)}) collective-permute-start(bf16[192,768]{1,0:T(8,128)(2,1)} %pad_maximum_fusion.9), channel_id=1, source_target_pairs={{0,6},{2,0},{4,2},{6,4},{1,7},{3,1},{5,3},{7,5},{8,14},{10,8},{12,... | collective-permute-start | bytes 884744 | tf_op jit(solution)/shard_map/ppermute | solution.py:391
  24.3 29.5 %collective-permute-start.10 = (bf16[192,768]{1,0:T(8,128)(2,1)}, bf16[192,768]{1,0:T(8,128)(2,1)}, u32[]{:S(2)}, u32[]{:S(2)}) collective-permute-start(bf16[192,768]{1,0:T(8,128)(2,1)} %pad_maximum_fusion.9), channel_id=1, source_target_pairs={{0,4},{2,6},{4,0},{6,2},{1,5},{3,7},{5,1},{7,3},{8,12},{10,14},{12... | collective-permute-start | bytes 884744 | tf_op jit(solution)/shard_map/ppermute | solution.py:391
  25.1 22.2 %collective-permute-start.3 = (f32[4,256]{1,0:T(4,128)S(1)}, f32[4,256]{1,0:T(4,128)S(1)}, u32[]{:S(2)}, u32[]{:S(2)}) collective-permute-start(f32[4,256]{1,0:T(4,128)S(1)} %bitcast.240), channel_id=1, source_target_pairs={{0,1},{1,0},{2,3},{3,2},{4,5},{5,4},{6,7},{7,6},{8,9},{9,8},{10,11... | collective-permute-start | bytes 12296 | tf_op jit(solution)/shard_map/ppermute | solution.py:391
  25.3 10.9 %collective-permute-start.12 = (bf16[2,2,32,1344]{3,2,1,0:T(8,128)(2,1)S(1)}, bf16[2,2,32,1344]{3,2,1,0:T(8,128)(2,1)S(1)}, u32[]{:S(2)}, u32[]{:S(2)}) collective-permute-start(bf16[2,2,32,1344]{3,2,1,0:T(8,128)(2,1)S(1)} %pad_maximum_fusion.7), channel_id=1, source_target_pairs={{0,16},{16,0},{1,17},{17,1},{2,18},{18,2},{3,19},{19,3},{4,20},{20... | collective-permute-start | bytes 1032200 | tf_op jit(solution)/shard_map/ppermute | solution.py:391
  36.2 10.1 %collective-permute-start.14 = (bf16[2,2,32,1344]{3,2,1,0:T(8,128)(2,1)S(1)}, bf16[2,2,32,1344]{3,2,1,0:T(8,128)(2,1)S(1)}, u32[]{:S(2)}, u32[]{:S(2)}) collective-permute-start(bf16[2,2,32,1344]{3,2,1,0:T(8,128)(2,1)S(1)} %pad_maximum_fusion.8), channel_id=1, source_target_pairs={{0,8},{8,0},{1,9},{9,1},{2,10},{10,2},{3,11},{11,3},{4,12},{12,4},... | collective-permute-start | bytes 1032200 | tf_op jit(solution)/shard_map/ppermute | solution.py:391
  47.3 10.6 %collective-permute-start.15 = (bf16[2,2,4,32,1344]{4,3,2,1,0:T(8,128)(2,1)S(1)}, bf16[2,2,4,32,1344]{4,3,2,1,0:T(8,128)(2,1)}, u32[]{:S(2)}, u32[]{:S(2)}) collective-permute-start(bf16[2,2,4,32,1344]{4,3,2,1,0:T(8,128)(2,1)S(1)} %maximum_maximum_fusion.1), channel_id=1, source_target_pairs={{0,1},{1,0},{2,3},{3,2},{4,5},{5,4},{6,7},{7,6},{8,9},{9,8},{10,11... | collective-permute-start | bytes 4128776 | tf_op jit(solution)/shard_map/ppermute | solution.py:391
  48.0 16.7 %collective-permute-start.7 = (bf16[256,768]{1,0:T(8,128)(2,1)S(1)}, bf16[256,768]{1,0:T(8,128)(2,1)S(1)}, u32[]{:S(2)}, u32[]{:S(2)}) collective-permute-start(bf16[256,768]{1,0:T(8,128)(2,1)S(1)} %bitcast.234), channel_id=1, source_target_pairs={{0,2},{2,4},{4,6},{6,0},{1,3},{3,5},{5,7},{7,1},{8,10},{10,12},{12... | collective-permute-start | bytes 1179656 | tf_op jit(solution)/shard_map/ppermute | solution.py:391
  50.1 28.3 %collective-permute-start.8 = (bf16[256,768]{1,0:T(8,128)(2,1)S(1)}, bf16[256,768]{1,0:T(8,128)(2,1)S(1)}, u32[]{:S(2)}, u32[]{:S(2)}) collective-permute-start(bf16[256,768]{1,0:T(8,128)(2,1)S(1)} %bitcast.235), channel_id=1, source_target_pairs={{0,4},{2,6},{4,0},{6,2},{1,5},{3,7},{5,1},{7,3},{8,12},{10,14},{12... | collective-permute-start | bytes 1179656 | tf_op jit(solution)/shard_map/ppermute | solution.py:391
  51.2 27.1 %collective-permute-start.9 = (bf16[256,768]{1,0:T(8,128)(2,1)S(1)}, bf16[256,768]{1,0:T(8,128)(2,1)S(1)}, u32[]{:S(2)}, u32[]{:S(2)}) collective-permute-start(bf16[256,768]{1,0:T(8,128)(2,1)S(1)} %bitcast.236), channel_id=1, source_target_pairs={{0,6},{2,0},{4,2},{6,4},{1,7},{3,1},{5,3},{7,5},{8,14},{10,8},{12,... | collective-permute-start | bytes 1179656 | tf_op jit(solution)/shard_map/ppermute | solution.py:391
  63.4 20.4 %collective-permute-start.22 = (bf16[2,192,768]{2,1,0:T(8,128)(2,1)S(1)}, bf16[2,192,768]{2,1,0:T(8,128)(2,1)S(1)}, u32[]{:S(2)}, u32[]{:S(2)}) collective-permute-start(bf16[2,192,768]{2,1,0:T(8,128)(2,1)S(1)} %get-tuple-element.149), channel_id=1, source_target_pairs={{0,8},{8,0},{1,9},{9,1},{2,10},{10,2},{3,11},{11,3},{4,12},{12,4},... | collective-permute-start | bytes 1769480 | tf_op jit(solution)/shard_map/ppermute | solution.py:391
  64.0 19.8 %collective-permute-start.24 = (bf16[2,192,768]{2,1,0:T(8,128)(2,1)S(1)}, bf16[2,192,768]{2,1,0:T(8,128)(2,1)S(1)}, u32[]{:S(2)}, u32[]{:S(2)}) collective-permute-start(bf16[2,192,768]{2,1,0:T(8,128)(2,1)S(1)} %get-tuple-element.150), channel_id=1, source_target_pairs={{0,16},{16,0},{1,17},{17,1},{2,18},{18,2},{3,19},{19,3},{4,20},{20... | collective-permute-start | bytes 1769480 | tf_op jit(solution)/shard_map/ppermute | solution.py:391
  84.1 35.5 %collective-permute-start.23 = (bf16[2,2,192,768]{3,2,1,0:T(8,128)(2,1)S(1)}, bf16[2,2,192,768]{3,2,1,0:T(8,128)(2,1)S(1)}, u32[]{:S(2)}, u32[]{:S(2)}) collective-permute-start(bf16[2,2,192,768]{3,2,1,0:T(8,128)(2,1)S(1)} %pad_maximum_fusion.3), channel_id=1, source_target_pairs={{0,16},{16,0},{1,17},{17,1},{2,18},{18,2},{3,19},{19,3},{4,20},{20... | collective-permute-start | bytes 3538952 | tf_op jit(solution)/shard_map/ppermute | solution.py:391
  84.8 35.0 %collective-permute-start.25 = (bf16[2,2,192,768]{3,2,1,0:T(8,128)(2,1)S(1)}, bf16[2,2,192,768]{3,2,1,0:T(8,128)(2,1)S(1)}, u32[]{:S(2)}, u32[]{:S(2)}) collective-permute-start(bf16[2,2,192,768]{3,2,1,0:T(8,128)(2,1)S(1)} %pad_maximum_fusion.4), channel_id=1, source_target_pairs={{0,8},{8,0},{1,9},{9,1},{2,10},{10,2},{3,11},{11,3},{4,12},{12,4},... | collective-permute-start | bytes 3538952 | tf_op jit(solution)/shard_map/ppermute | solution.py:391
  98.3 14.7 %collective-permute-start.17 = (bf16[256,192]{1,0:T(8,128)(2,1)S(1)}, bf16[256,192]{1,0:T(8,128)(2,1)S(1)}, u32[]{:S(2)}, u32[]{:S(2)}) collective-permute-start(bf16[256,192]{1,0:T(8,128)(2,1)S(1)} %get-tuple-element.167), channel_id=1, source_target_pairs={{0,2},{2,4},{4,6},{6,0},{1,3},{3,5},{5,7},{7,1},{8,10},{10,12},{12... | collective-permute-start | bytes 294920 | tf_op jit(solution)/shard_map/ppermute | solution.py:391
  107.3 10.8 %collective-permute-start.18 = (bf16[256,192]{1,0:T(8,128)(2,1)S(1)}, bf16[256,192]{1,0:T(8,128)(2,1)S(1)}, u32[]{:S(2)}, u32[]{:S(2)}) collective-permute-start(bf16[256,192]{1,0:T(8,128)(2,1)S(1)} %get-tuple-element.166), channel_id=1, source_target_pairs={{0,4},{2,6},{4,0},{6,2},{1,5},{3,7},{5,1},{7,3},{8,12},{10,14},{12... | collective-permute-start | bytes 294920 | tf_op jit(solution)/shard_map/ppermute | solution.py:391
  109.1 8.9 %collective-permute-start.19 = (bf16[256,192]{1,0:T(8,128)(2,1)S(1)}, bf16[256,192]{1,0:T(8,128)(2,1)S(1)}, u32[]{:S(2)}, u32[]{:S(2)}) collective-permute-start(bf16[256,192]{1,0:T(8,128)(2,1)S(1)} %get-tuple-element.165), channel_id=1, source_target_pairs={{0,6},{2,0},{4,2},{6,4},{1,7},{3,1},{5,3},{7,5},{8,14},{10,8},{12,... | collective-permute-start | bytes 294920 | tf_op jit(solution)/shard_map/ppermute | solution.py:391
  112.9 7.9 %collective-permute-start.21 = (bf16[256,768]{1,0:T(8,128)(2,1)S(1)}, bf16[256,768]{1,0:T(8,128)(2,1)S(1)}, u32[]{:S(2)}, u32[]{:S(2)}) collective-permute-start(bf16[256,768]{1,0:T(8,128)(2,1)S(1)} %bitcast.245), channel_id=1, source_target_pairs={{0,1},{1,0},{2,3},{3,2},{4,5},{5,4},{6,7},{7,6},{8,9},{9,8},{10,11... | collective-permute-start | bytes 1179656 | tf_op jit(solution)/shard_map/ppermute | solution.py:391
  128.2 6.6 %collective-permute-start.26 = (bf16[2,256,768]{2,1,0:T(8,128)(2,1)S(1)}, bf16[2,256,768]{2,1,0:T(8,128)(2,1)S(1)}, u32[]{:S(2)}, u32[]{:S(2)}) collective-permute-start(bf16[2,256,768]{2,1,0:T(8,128)(2,1)S(1)} %get-tuple-element.81), channel_id=1, source_target_pairs={{0,1},{1,0},{2,3},{3,2},{4,5},{5,4},{6,7},{7,6},{8,9},{9,8},{10,11... | collective-permute-start | bytes 2359304 | tf_op jit(solution)/shard_map/ppermute | solution.py:391
  134.5 35.3 %collective-permute-start.31 = (bf16[2,2,192,768]{3,2,1,0:T(8,128)(2,1)}, bf16[2,2,192,768]{3,2,1,0:T(8,128)(2,1)}, u32[]{:S(2)}, u32[]{:S(2)}) collective-permute-start(bf16[2,2,192,768]{3,2,1,0:T(8,128)(2,1)} %get-tuple-element.96), channel_id=1, source_target_pairs={{0,8},{8,0},{1,9},{9,1},{2,10},{10,2},{3,11},{11,3},{4,12},{12,4},... | collective-permute-start | bytes 3538952 | tf_op jit(solution)/shard_map/ppermute | solution.py:391
  139.4 8.5 %collective-permute-start.27 = (bf16[256,192]{1,0:T(8,128)(2,1)}, bf16[256,192]{1,0:T(8,128)(2,1)}, u32[]{:S(2)}, u32[]{:S(2)}) collective-permute-start(bf16[256,192]{1,0:T(8,128)(2,1)} %get-tuple-element.85), channel_id=1, source_target_pairs={{0,2},{2,4},{4,6},{6,0},{1,3},{3,5},{5,7},{7,1},{8,10},{10,12},{12... | collective-permute-start | bytes 294920 | tf_op jit(solution)/shard_map/ppermute | solution.py:391
  142.4 10.5 %collective-permute-start.28 = (bf16[256,192]{1,0:T(8,128)(2,1)}, bf16[256,192]{1,0:T(8,128)(2,1)}, u32[]{:S(2)}, u32[]{:S(2)}) collective-permute-start(bf16[256,192]{1,0:T(8,128)(2,1)} %get-tuple-element.86), channel_id=1, source_target_pairs={{0,4},{2,6},{4,0},{6,2},{1,5},{3,7},{5,1},{7,3},{8,12},{10,14},{12... | collective-permute-start | bytes 294920 | tf_op jit(solution)/shard_map/ppermute | solution.py:391
  143.5 9.5 %collective-permute-start.29 = (bf16[256,192]{1,0:T(8,128)(2,1)}, bf16[256,192]{1,0:T(8,128)(2,1)}, u32[]{:S(2)}, u32[]{:S(2)}) collective-permute-start(bf16[256,192]{1,0:T(8,128)(2,1)} %get-tuple-element.87), channel_id=1, source_target_pairs={{0,6},{2,0},{4,2},{6,4},{1,7},{3,1},{5,3},{7,5},{8,14},{10,8},{12,... | collective-permute-start | bytes 294920 | tf_op jit(solution)/shard_map/ppermute | solution.py:391
  144.7 27.9 %collective-permute-start.30 = (bf16[2,2,192,768]{3,2,1,0:T(8,128)(2,1)}, bf16[2,2,192,768]{3,2,1,0:T(8,128)(2,1)S(1)}, u32[]{:S(2)}, u32[]{:S(2)}) collective-permute-start(bf16[2,2,192,768]{3,2,1,0:T(8,128)(2,1)} %copy-done.27), channel_id=1, source_target_pairs={{0,16},{16,0},{1,17},{17,1},{2,18},{18,2},{3,19},{19,3},{4,20},{20... | collective-permute-start | bytes 3538952 | tf_op jit(solution)/shard_map/ppermute | solution.py:391
  168.5 27.1 %collective-permute-start.32 = (bf16[1024,384]{1,0:T(8,128)(2,1)S(1)}, bf16[1024,384]{1,0:T(8,128)(2,1)S(1)}, u32[]{:S(2)}, u32[]{:S(2)}) collective-permute-start(bf16[1024,384]{1,0:T(8,128)(2,1)S(1)} %get-tuple-element.101), channel_id=1, source_target_pairs={{0,1},{1,0},{2,3},{3,2},{4,5},{5,4},{6,7},{7,6},{8,9},{9,8},{10,11... | collective-permute-start | bytes 2359304 | tf_op jit(solution)/shard_map/ppermute | solution.py:391
  173.0 15.6 %collective-permute-start.46 = (bf16[2,192,768]{2,1,0:T(8,128)(2,1)S(1)}, bf16[2,192,768]{2,1,0:T(8,128)(2,1)S(1)}, u32[]{:S(2)}, u32[]{:S(2)}) collective-permute-start(bf16[2,192,768]{2,1,0:T(8,128)(2,1)S(1)} %fusion.2), channel_id=1, source_target_pairs={{0,16},{16,0},{1,17},{17,1},{2,18},{18,2},{3,19},{19,3},{4,20},{20... | collective-permute-start | bytes 1769480 | tf_op jit(solution)/shard_map/ppermute | solution.py:391
  174.4 15.0 %collective-permute-start.45 = (bf16[2,192,768]{2,1,0:T(8,128)(2,1)S(1)}, bf16[2,192,768]{2,1,0:T(8,128)(2,1)S(1)}, u32[]{:S(2)}, u32[]{:S(2)}) collective-permute-start(bf16[2,192,768]{2,1,0:T(8,128)(2,1)S(1)} %fusion.1), channel_id=1, source_target_pairs={{0,8},{8,0},{1,9},{9,1},{2,10},{10,2},{3,11},{11,3},{4,12},{12,4},... | collective-permute-start | bytes 1769480 | tf_op jit(solution)/shard_map/ppermute | solution.py:391
  189.7 14.6 %collective-permute-start.47 = (bf16[192,768]{1,0:T(8,128)(2,1)S(1)}, bf16[192,768]{1,0:T(8,128)(2,1)S(1)}, u32[]{:S(2)}, u32[]{:S(2)}) collective-permute-start(bf16[192,768]{1,0:T(8,128)(2,1)S(1)} %get-tuple-element.144), channel_id=1, source_target_pairs={{0,2},{2,4},{4,6},{6,0},{1,3},{3,5},{5,7},{7,1},{8,10},{10,12},{12... | collective-permute-start | bytes 884744 | tf_op jit(solution)/shard_map/ppermute | solution.py:391
  193.2 20.4 %collective-permute-start.48 = (bf16[192,768]{1,0:T(8,128)(2,1)S(1)}, bf16[192,768]{1,0:T(8,128)(2,1)S(1)}, u32[]{:S(2)}, u32[]{:S(2)}) collective-permute-start(bf16[192,768]{1,0:T(8,128)(2,1)S(1)} %get-tuple-element.146), channel_id=1, source_target_pairs={{0,4},{2,6},{4,0},{6,2},{1,5},{3,7},{5,1},{7,3},{8,12},{10,14},{12... | collective-permute-start | bytes 884744 | tf_op jit(solution)/shard_map/ppermute | solution.py:391
  194.5 27.1 %collective-permute-start.49 = (bf16[192,768]{1,0:T(8,128)(2,1)S(1)}, bf16[192,768]{1,0:T(8,128)(2,1)S(1)}, u32[]{:S(2)}, u32[]{:S(2)}) collective-permute-start(bf16[192,768]{1,0:T(8,128)(2,1)S(1)} %get-tuple-element.145), channel_id=1, source_target_pairs={{0,6},{2,0},{4,2},{6,4},{1,7},{3,1},{5,3},{7,5},{8,14},{10,8},{12,... | collective-permute-start | bytes 884744 | tf_op jit(solution)/shard_map/ppermute | solution.py:391
  202.9 25.2 %collective-permute-start.34 = (bf16[16,32,1344]{2,1,0:T(8,128)(2,1)S(1)}, bf16[16,32,1344]{2,1,0:T(8,128)(2,1)S(1)}, u32[]{:S(2)}, u32[]{:S(2)}) collective-permute-start(bf16[16,32,1344]{2,1,0:T(8,128)(2,1)S(1)} %get-tuple-element.113), channel_id=1, source_target_pairs={{0,1},{1,0},{2,3},{3,2},{4,5},{5,4},{6,7},{7,6},{8,9},{9,8},{10,11... | collective-permute-start | bytes 4128776 | tf_op jit(solution)/shard_map/ppermute | solution.py:391
  203.0 46.9 %collective-permute-start.41 = (bf16[256,768]{1,0:T(8,128)(2,1)S(1)}, bf16[256,768]{1,0:T(8,128)(2,1)S(1)}, u32[]{:S(2)}, u32[]{:S(2)}) collective-permute-start(bf16[256,768]{1,0:T(8,128)(2,1)S(1)} %get-tuple-element.115), channel_id=1, source_target_pairs={{2,0},{4,2},{6,4},{3,1},{5,3},{7,5},{10,8},{12,10},{14,12},{11,9},... | collective-permute-start | bytes 1179656 | tf_op jit(solution)/shard_map/ppermute | solution.py:451
  204.4 49.9 %collective-permute-start.33 = (bf16[256,768]{1,0:T(8,128)(2,1)S(1)}, bf16[256,768]{1,0:T(8,128)(2,1)S(1)}, u32[]{:S(2)}, u32[]{:S(2)}) collective-permute-start(bf16[256,768]{1,0:T(8,128)(2,1)S(1)} %get-tuple-element.104), channel_id=1, source_target_pairs={{0,2},{2,4},{4,6},{1,3},{3,5},{5,7},{8,10},{10,12},{12,14},{9,11},... | collective-permute-start | bytes 1179656 | tf_op jit(solution)/shard_map/ppermute | solution.py:450
  213.6 14.4 %collective-permute-start.39 = (bf16[256,768]{1,0:T(8,128)(2,1)S(1)}, bf16[256,768]{1,0:T(8,128)(2,1)S(1)}, u32[]{:S(2)}, u32[]{:S(2)}) collective-permute-start(bf16[256,768]{1,0:T(8,128)(2,1)S(1)} %broadcast_select_fusion.2), channel_id=1, source_target_pairs={{0,2},{6,4},{1,3},{7,5},{8,10},{14,12},{9,11},{15,13},{16,18},{22,... | collective-permute-start | bytes 1179656 | tf_op jit(solution)/shard_map/ppermute | solution.py:447
  221.9 12.3 %collective-permute-start.50 = (bf16[24,1536]{1,0:T(8,128)(2,1)S(1)}, bf16[24,1536]{1,0:T(8,128)(2,1)S(1)}, u32[]{:S(2)}, u32[]{:S(2)}) collective-permute-start(bf16[24,1536]{1,0:T(8,128)(2,1)S(1)} %fusion.18), channel_id=1, source_target_pairs={{0,1},{1,0},{2,3},{3,2},{4,5},{5,4},{6,7},{7,6},{8,9},{9,8},{10,11... | collective-permute-start | bytes 221192 | tf_op jit(solution)/shard_map/ppermute | solution.py:391
  228.6 8.4 %collective-permute-start.37 = (bf16[2,2,32,1344]{3,2,1,0:T(8,128)(2,1)S(1)}, bf16[2,2,32,1344]{3,2,1,0:T(8,128)(2,1)S(1)}, u32[]{:S(2)}, u32[]{:S(2)}) collective-permute-start(bf16[2,2,32,1344]{3,2,1,0:T(8,128)(2,1)S(1)} %dynamic-slice_bitcast_fusion), channel_id=1, source_target_pairs={{0,8},{8,0},{1,9},{9,1},{2,10},{10,2},{3,11},{11,3},{4,12},{12,4},... | collective-permute-start | bytes 1032200 | tf_op jit(solution)/shard_map/ppermute | solution.py:391
  231.6 18.3 %collective-permute-start.40 = (bf16[256,768]{1,0:T(8,128)(2,1)S(1)}, bf16[256,768]{1,0:T(8,128)(2,1)S(1)}, u32[]{:S(2)}, u32[]{:S(2)}) collective-permute-start(bf16[256,768]{1,0:T(8,128)(2,1)S(1)} %add_convert_fusion.1), channel_id=1, source_target_pairs={{0,4},{2,6},{4,0},{6,2},{1,5},{3,7},{5,1},{7,3},{8,12},{10,14},{12... | collective-permute-start | bytes 1179656 | tf_op jit(solution)/shard_map/ppermute | solution.py:391
  235.6 8.6 %collective-permute-start.35 = (bf16[2,2,32,1344]{3,2,1,0:T(8,128)(2,1)S(1)}, bf16[2,2,32,1344]{3,2,1,0:T(8,128)(2,1)S(1)}, u32[]{:S(2)}, u32[]{:S(2)}) collective-permute-start(bf16[2,2,32,1344]{3,2,1,0:T(8,128)(2,1)S(1)} %dynamic-slice_bitcast_fusion.1), channel_id=1, source_target_pairs={{0,16},{16,0},{1,17},{17,1},{2,18},{18,2},{3,19},{19,3},{4,20},{20... | collective-permute-start | bytes 1032200 | tf_op jit(solution)/shard_map/ppermute | solution.py:391
  237.2 8.9 %collective-permute-start.38 = (bf16[2,32,1344]{2,1,0:T(8,128)(2,1)S(1)}, bf16[2,32,1344]{2,1,0:T(8,128)(2,1)S(1)}, u32[]{:S(2)}, u32[]{:S(2)}) collective-permute-start(bf16[2,32,1344]{2,1,0:T(8,128)(2,1)S(1)} %fusion.9), channel_id=1, source_target_pairs={{0,16},{16,0},{1,17},{17,1},{2,18},{18,2},{3,19},{19,3},{4,20},{20... | collective-permute-start | bytes 516104 | tf_op jit(solution)/shard_map/ppermute | solution.py:391
  244.3 5.6 %collective-permute-start.36 = (bf16[2,32,1344]{2,1,0:T(8,128)(2,1)S(1)}, bf16[2,32,1344]{2,1,0:T(8,128)(2,1)S(1)}, u32[]{:S(2)}, u32[]{:S(2)}) collective-permute-start(bf16[2,32,1344]{2,1,0:T(8,128)(2,1)S(1)} %fusion.8), channel_id=1, source_target_pairs={{0,8},{8,0},{1,9},{9,1},{2,10},{10,2},{3,11},{11,3},{4,12},{12,4},... | collective-permute-start | bytes 516104 | tf_op jit(solution)/shard_map/ppermute | solution.py:391
  250.1 6.5 %collective-permute-start.42 = (bf16[32,1344]{1,0:T(8,128)(2,1)S(1)}, bf16[32,1344]{1,0:T(8,128)(2,1)S(1)}, u32[]{:S(2)}, u32[]{:S(2)}) collective-permute-start(bf16[32,1344]{1,0:T(8,128)(2,1)S(1)} %get-tuple-element.171), channel_id=1, source_target_pairs={{0,2},{2,4},{4,6},{6,0},{1,3},{3,5},{5,7},{7,1},{8,10},{10,12},{12... | collective-permute-start | bytes 258056 | tf_op jit(solution)/shard_map/ppermute | solution.py:391
  251.1 7.7 %collective-permute-start.43 = (bf16[32,1344]{1,0:T(8,128)(2,1)S(1)}, bf16[32,1344]{1,0:T(8,128)(2,1)S(1)}, u32[]{:S(2)}, u32[]{:S(2)}) collective-permute-start(bf16[32,1344]{1,0:T(8,128)(2,1)S(1)} %get-tuple-element.170), channel_id=1, source_target_pairs={{0,4},{2,6},{4,0},{6,2},{1,5},{3,7},{5,1},{7,3},{8,12},{10,14},{12... | collective-permute-start | bytes 258056 | tf_op jit(solution)/shard_map/ppermute | solution.py:391
  253.8 5.5 %collective-permute-start.44 = (bf16[32,1344]{1,0:T(8,128)(2,1)S(1)}, bf16[32,1344]{1,0:T(8,128)(2,1)S(1)}, u32[]{:S(2)}, u32[]{:S(2)}) collective-permute-start(bf16[32,1344]{1,0:T(8,128)(2,1)S(1)} %get-tuple-element.169), channel_id=1, source_target_pairs={{0,6},{2,0},{4,2},{6,4},{1,7},{3,1},{5,3},{7,5},{8,14},{10,8},{12,... | collective-permute-start | bytes 258056 | tf_op jit(solution)/shard_map/ppermute | solution.py:391
  (62 other events, 431.2 us)

commit v2 on v1

--- a/solution.py
+++ b/solution.py
@@ -1011,9 +1011,10 @@
             for a in range(chunks // 2):
                 rows = slice(a * CHUNK, (a + 1) * CHUNK)
                 at = pl.ds(pl.multiple_of((2 * a + core) * CHUNK, CHUNK), CHUNK)
+                turned = jnp.transpose(ref[rows, :])
                 for h in range(GROUP):
                     k_s[h, at] = ref[rows, HEAD_DIM * h : HEAD_DIM * (h + 1)]
-                    vt_s[h, :, at] = jnp.transpose(ref[rows, GW + HEAD_DIM * h : GW + HEAD_DIM * (h + 1)])
+                    vt_s[h, :, at] = turned[GW + HEAD_DIM * h : GW + HEAD_DIM * (h + 1)]
         for j in range(chunks):
             col_s[j * CHUNK : (j + 1) * CHUNK] = column_of(kseg_ref[j : j + 1])
 
@@ -1123,7 +1124,8 @@
     here = pl.ds(pl.multiple_of(step * CHUNK, CHUNK), CHUNK)
     k_heads = [kv_ref[here, HEAD_DIM * h : HEAD_DIM * (h + 1)] for h in range(GROUP)]
     v_heads = [kv_ref[here, GW + HEAD_DIM * h : GW + HEAD_DIM * (h + 1)] for h in range(GROUP)]
-    k_turned = [jnp.transpose(k) for k in k_heads]
+    turned = jnp.transpose(kv_ref[here, :])
+    k_turned = [turned[HEAD_DIM * h : HEAD_DIM * (h + 1)] for h in range(GROUP)]
     k_column = column_of(kseg_ref[pl.ds(j, 1)])
 
     count = list_live([act_ref[i, j] for i in range(rows // CHUNK)], list_s)

time: 263 us -> 261 us (level)
  waiting for transfers between devices: 71.6 us -> 75.8 us
  starting transfers between devices: 83.8 us -> 80.5 us
  Pallas kernels: 68.2 us -> 65.1 us
    ppermute x48, waiting for transfers between devices: 65.6 us -> 69.7 us  [shift(): lax.ppermute(array, axis, [(i, (i + hop) % size) for i in range(size)])]
    ppermute x48, starting transfers between devices: 65.4 us -> 62.1 us  [shift(): lax.ppermute(array, axis, [(i, (i + hop) % size) for i in range(size)])]
  transfers between devices with their start and end apart: 51 -> 51, of which waited for: 21 -> 23; matrix products, arithmetic and copies ran while one was open for 7% -> 7% of each run, Pallas kernels for 23% -> 22%
where the time goes in v2:
time: 261 us; the launch traced here: 260 us
  starting transfers between devices  80.5 us (31%)
  waiting for transfers between devices  75.8 us (29%)
  Pallas kernels  65.1 us (25%)
  local copies, waits for them, and re-layouts  21.4 us (8%)
  other arithmetic  13.9 us (5%)
  between operations  3.46 us (1%)
    ppermute x48, waiting for transfers between devices, shift(): lax.ppermute(array, axis, [(i, (i + hop) % size) for i in range(size)])  69.7 us
    ppermute x48, starting transfers between devices, shift(): lax.ppermute(array, axis, [(i, (i + hop) % size) for i in range(size)])  62.1 us
    pallas_call x11, Pallas kernels, kernel_call(): pl.pallas_call(body, out_shape=tuple((jax.ShapeDtypeStruct(shape, dtype)...  34.1 us
    pallas_call x2, Pallas kernels, attend_back(): pl.pallas_call(functools.partial(attend_back_kernel, first), out_shape=tu...  20.1 us
    unnamed x122, local copies, waits for them, and re-layouts  11.9 us
    pallas_call x1, Pallas kernels, attend(): pl.pallas_call(attend_kernel, out_shape=(jax.ShapeDtypeStruct((rows, GW),...  10.9 us
    ppermute x1, starting transfers between devices, z_reduce(): up = lax.ppermute(sent[0], 'z', [(0, 1), (1, 2), (2, 3)])  9.14 us
    ppermute x1, starting transfers between devices, z_reduce(): edge = lax.ppermute(edge, 'z', [(0, 1), (NZ - 1, NZ - 2)])  8.01 us
  transfers between devices with their start and end apart: 51, of which 23 were waited for; matrix products, arithmetic and copies ran while one was open for 7% of the time, Pallas kernels for 22%

profile of v2, /device:TPU:0, one launch (start us, length us, event | category | flops | bytes accessed | tf_op | source)
XLA Modules:
  0.0 260.2 jit_solution(1274419194575664736)
XLA Ops:
  4.5 3.1 %collective-permute-start = (bf16[32,1344]{1,0:T(8,128)(2,1)S(1)}, bf16[32,1344]{1,0:T(8,128)(2,1)S(1)}, u32[]{:S(2)}, u32[]{:S(2)}) collective-permute-start(bf16[32,1344]{1,0:T(8,128)(2,1)S(1)} %get-tuple-element.178), channel_id=1, source_target_pairs={{0,2},{2,4},{4,6},{6,0},{1,3},{3,5},{5,7},{7,1},{8,10},{10,12},{12... | collective-permute-start | bytes 258056 | tf_op jit(solution)/shard_map/ppermute | solution.py:391
  7.6 2.6 collective-permute-start.1
  13.4 2.8 %collective-permute-done.1 = bf16[32,1344]{1,0:T(8,128)(2,1)S(1)} collective-permute-done((bf16[32,1344]{1,0:T(8,128)(2,1)S(1)}, bf16[32,1344]{1,0:T(8,128)(2,1)S(1)}, u32[]{:S(2)}, u32[]{:S(2)}) %collective-permute-start.1) | collective-permute-done | bytes 86048 | tf_op jit(solution)/shard_map/ppermute | solution.py:391
  16.5 1.6 collective-permute-start.11
  18.1 1.6 collective-permute-start.13
  20.4 2.2 collective-permute-start.5
  22.6 1.6 collective-permute-start.6
  26.3 9.9 %collective-permute-done.12 = bf16[2,2,32,1344]{3,2,1,0:T(8,128)(2,1)S(1)} collective-permute-done((bf16[2,2,32,1344]{3,2,1,0:T(8,128)(2,1)S(1)}, bf16[2,2,32,1344]{3,2,1,0:T(8,128)(2,1)S(1)}, u32[]{:S(2)}, u32[]{:S(2)}) %collective-permute-start.12) | collective-permute-done | bytes 344096 | tf_op jit(solution)/shard_map/ppermute | solution.py:391
  36.8 9.5 %collective-permute-done.14 = bf16[2,2,32,1344]{3,2,1,0:T(8,128)(2,1)S(1)} collective-permute-done((bf16[2,2,32,1344]{3,2,1,0:T(8,128)(2,1)S(1)}, bf16[2,2,32,1344]{3,2,1,0:T(8,128)(2,1)S(1)}, u32[]{:S(2)}, u32[]{:S(2)}) %collective-permute-start.14) | collective-permute-done | bytes 344096 | tf_op jit(solution)/shard_map/ppermute | solution.py:391
  48.0 2.1 collective-permute-start.7
  51.2 2.5 collective-permute-start.9
  53.8 1.4 select_bitcast_fusion.16
  55.2 1.4 select_bitcast_fusion.17
  58.1 1.8 select_bitcast_fusion.1
  62.0 1.4 fusion.30
  64.7 13.6 %collective-permute-done.8.t2_ref = bf16[256,768]{1,0:T(8,128)(2,1)S(1)} collective-permute-done((bf16[256,768]{1,0:T(8,128)(2,1)S(1)}, bf16[256,768]{1,0:T(8,128)(2,1)S(1)}, u32[]{:S(2)}, u32[]{:S(2)}) %collective-permute-start.8) | collective-permute-done | bytes 393248 | tf_op jit(solution)/shard_map/ppermute | solution.py:391
  78.3 4.2 %project.1 = (bf16[1024,768]{1,0:T(8,128)(2,1)S(1)}, bf16[1024,768]{1,0:T(8,128)(2,1)S(1)}, bf16[1024,192]{1,0:T(8,128)(2,1)S(1)}, bf16[1024,384]{1,0:T(8,128)(2,1)S(1)}) custom-call(s32[4]{0:T(128)S(1)} %pad_add_fusion.1.place_ref.refs_2_, bf16[256,768]{1,0:T(8,128)(2,1)S(1)} %bitcast.237, bf16[256,768]{1,0:T(8,128)(2,1)S(1)} %collective-permute-done.7.t1_ref, ...), custom_call_target="tpu_custom_call" | custom-call | flops 3623878656 | bytes 2506752 | tf_op jit(solution)/shard_map/project/pallas_call | solution.py:540
  86.1 10.9 %attend.1 = (f32[1024,192]{1,0:T(8,128)S(1)}, bf16[1024,192]{1,0:T(8,128)(2,1)S(1)}, f32[8,1024]{1,0:T(8,128)S(1)}) custom-call(s32[4,8]{1,0:T(4,128)S(1)} %convert_element_type.157.act_ref.refs_0_, s32[8,16]{1,0:T(8,128)S(1)} %fusion.24.may_ref.refs_1_, s32[4]{0:T(128)S(1)} %pad_add_fusion.1.place_ref.refs_2_, ...), custom_call_target="tpu_custom_call" | custom-call | flops 19327352832 | bytes 6291456 | tf_op jit(solution)/shard_map/attend/pallas_call | solution.py:1058
  97.1 9.0 %collective-permute-start.17 = (bf16[256,192]{1,0:T(8,128)(2,1)S(1)}, bf16[256,192]{1,0:T(8,128)(2,1)S(1)}, u32[]{:S(2)}, u32[]{:S(2)}) collective-permute-start(bf16[256,192]{1,0:T(8,128)(2,1)S(1)} %get-tuple-element.167), channel_id=1, source_target_pairs={{0,2},{2,4},{4,6},{6,0},{1,3},{3,5},{5,7},{7,1},{8,10},{10,12},{12... | collective-permute-start | bytes 294920 | tf_op jit(solution)/shard_map/ppermute | solution.py:391
  106.0 1.9 collective-permute-start.18
  111.9 5.5 %collective-permute-done.18.a2_ref = bf16[256,192]{1,0:T(8,128)(2,1)S(1)} collective-permute-done((bf16[256,192]{1,0:T(8,128)(2,1)S(1)}, bf16[256,192]{1,0:T(8,128)(2,1)S(1)}, u32[]{:S(2)}, u32[]{:S(2)}) %collective-permute-start.18) | collective-permute-done | bytes 98336 | tf_op jit(solution)/shard_map/ppermute | solution.py:391
  120.5 7.0 %feed.1 = (bf16[512,1536]{1,0:T(8,128)(2,1)S(1)}, bf16[512,1536]{1,0:T(8,128)(2,1)S(1)}, f32[256,768]{1,0:T(8,128)S(1)}, f32[256,768]{1,0:T(8,128)S(1)}, bf16[2,...) custom-call(s32[4]{0:T(128)S(1)} %pad_add_fusion.1.place_ref.refs_2_, bf16[256,768]{1,0:T(8,128)(2,1)S(1)} %get-tuple-element.77.na_ref, ...), custom_call_target="tpu_custom_call" | custom-call | flops 96636764160 | bytes 110161920 | tf_op jit(solution)/shard_map/feed/pallas_call | solution.py:540
  127.7 6.1 %feed_weights.1 = (bf16[2,2,192,768]{3,2,1,0:T(8,128)(2,1)S(1)}, bf16[2,2,192,768]{3,2,1,0:T(8,128)(2,1)S(1)}, bf16[2,2,192,768]{3,2,1,0:T(8,128)(2,1)S(1)}, bf16[2,2,192,768]{3,2,1,0:T(8,128)(2,1)}) custom-call(s32[4]{0:T(128)S(1)} %pad_add_fusion.1.place_ref.refs_2_, bf16[256,768]{1,0:T(8,128)(2,1)S(1)} %get-tuple-element.77.na_ref, ...), custom_call_target="tpu_custom_call" | custom-call | flops 7247757312 | bytes 14155776 | tf_op jit(solution)/shard_map/feed_weights/pallas_call | solution.py:540
  133.8 2.5 middle.1
  138.4 3.4 %collective-permute-start.27 = (bf16[256,192]{1,0:T(8,128)(2,1)}, bf16[256,192]{1,0:T(8,128)(2,1)}, u32[]{:S(2)}, u32[]{:S(2)}) collective-permute-start(bf16[256,192]{1,0:T(8,128)(2,1)} %get-tuple-element.85), channel_id=1, source_target_pairs={{0,2},{2,4},{4,6},{6,0},{1,3},{3,5},{5,7},{7,1},{8,10},{10,12},{12... | collective-permute-start | bytes 294920 | tf_op jit(solution)/shard_map/ppermute | solution.py:391
  141.7 1.4 collective-permute-start.28
  145.1 2.1 collective-permute-done.27.refs_5_
  147.2 5.2 %collective-permute-done.28.refs_6_ = bf16[256,192]{1,0:T(8,128)(2,1)} collective-permute-done((bf16[256,192]{1,0:T(8,128)(2,1)}, bf16[256,192]{1,0:T(8,128)(2,1)}, u32[]{:S(2)}, u32[]{:S(2)}) %collective-permute-start.28) | collective-permute-done | bytes 98336 | tf_op jit(solution)/shard_map/ppermute | solution.py:391
  158.8 11.4 %attend_back_first.1 = (f32[3,64,1024]{2,1,0:T(8,128)S(1)}, f32[8,1024]{1,0:T(8,128)S(1)}, bf16[1024,384]{1,0:T(8,128)(2,1)S(1)}) custom-call(s32[4,8]{1,0:T(4,128)S(1)} %copy-done.25, s32[8,16]{1,0:T(8,128)S(1)} %copy-done.23, s32[4]{0:T(128)S(1)} %pad_add_fusion.1.place_ref.refs_2_, bf16[1024,192]{1,0:T(8,128)(2,1)S(1)} %copy-done.36, ...), custom_call_target="tpu_custom_call" | custom-call | flops 11274289152 | bytes 6291456 | tf_op jit(solution)/shard_map/attend_back_first/pallas_call | solution.py:1175
  170.3 1.5 convert_add_fusion
  174.9 8.7 %attend_back_last.1 = (bf16[1024,192]{1,0:T(8,128)(2,1)S(1)}, bf16[1024,384]{1,0:T(8,128)(2,1)S(1)}) custom-call(s32[4,8]{1,0:T(4,128)S(1)} %copy-done.26, s32[8,16]{1,0:T(8,128)S(1)} %copy-done.23, s32[4]{0:T(128)S(1)} %pad_add_fusion.1.place_ref.refs_2_, bf16[1024,192]{1,0:T(8,128)(2,1)S(1)} %copy-done.37, bf16[256,192]{1,0:T(8,128)(2,1)S(1)} %copy-done.39, ...), custom_call_target="tpu_custom_call" | custom-call | flops 11274289152 | bytes 6291456 | tf_op jit(solution)/shard_map/attend_back_last/pallas_call | solution.py:1175
  183.6 4.3 %collective-permute-done.46 = bf16[2,192,768]{2,1,0:T(8,128)(2,1)S(1)} collective-permute-done((bf16[2,192,768]{2,1,0:T(8,128)(2,1)S(1)}, bf16[2,192,768]{2,1,0:T(8,128)(2,1)S(1)}, u32[]{:S(2)}, u32[]{:S(2)}) %collective-permute-start.46) | collective-permute-done | bytes 589856 | tf_op jit(solution)/shard_map/ppermute | solution.py:391
  189.1 3.4 %collective-permute-start.47 = (bf16[192,768]{1,0:T(8,128)(2,1)S(1)}, bf16[192,768]{1,0:T(8,128)(2,1)S(1)}, u32[]{:S(2)}, u32[]{:S(2)}) collective-permute-start(bf16[192,768]{1,0:T(8,128)(2,1)S(1)} %get-tuple-element.144), channel_id=1, source_target_pairs={{0,2},{2,4},{4,6},{6,0},{1,3},{3,5},{5,7},{7,1},{8,10},{10,12},{12... | collective-permute-start | bytes 884744 | tf_op jit(solution)/shard_map/ppermute | solution.py:391
  193.6 1.5 collective-permute-start.49
  195.1 4.0 %inward.1 = (bf16[1024,576]{1,0:T(8,128)(2,1)S(1)}, f32[256,768]{1,0:T(8,128)S(1)}, bf16[256,768]{1,0:T(8,128)(2,1)S(1)}, bf16[256,768]{1,0:T(8,128)(2,1)S(1)}, ...) custom-call(s32[4]{0:T(128)S(1)} %pad_add_fusion.1.place_ref.refs_2_, ...), custom_call_target="tpu_custom_call" | custom-call | flops 10871635968 | bytes 13271040 | tf_op jit(solution)/shard_map/inward/pallas_call | solution.py:540
  199.2 3.2 %owners.1 = (bf16[16,32,1344]{2,1,0:T(8,128)(2,1)S(1)}, bf16[16,32,1344]{2,1,0:T(8,128)(2,1)S(1)}) custom-call(s32[4]{0:T(128)S(1)} %pad_add_fusion.1.place_ref.refs_2_, bf16[256,192]{1,0:T(8,128)(2,1)S(1)} %copy-done.5, bf16[256,192]{1,0:T(8,128)(2,1)S(1)} %copy-done.13, bf16[256,192]{1,0:T(8,128)(2,1)S(1)} %copy-done.15, bf16[256,192]{1,0:T(8,128)(2,1)S(1)} %copy-done.17, ...), custom_call_target="tpu_custom_call" | custom-call | flops 3145728 | bytes 10838016 | tf_op jit(solution)/shard_map/owners/pallas_call | solution.py:540
  203.8 9.1 %collective-permute-start.33 = (bf16[256,768]{1,0:T(8,128)(2,1)S(1)}, bf16[256,768]{1,0:T(8,128)(2,1)S(1)}, u32[]{:S(2)}, u32[]{:S(2)}) collective-permute-start(bf16[256,768]{1,0:T(8,128)(2,1)S(1)} %get-tuple-element.104), channel_id=1, source_target_pairs={{0,2},{2,4},{4,6},{1,3},{3,5},{5,7},{8,10},{10,12},{12,14},{9,11},... | collective-permute-start | bytes 1179656 | tf_op jit(solution)/shard_map/ppermute | solution.py:450
  212.9 8.0 %collective-permute-start.39 = (bf16[256,768]{1,0:T(8,128)(2,1)S(1)}, bf16[256,768]{1,0:T(8,128)(2,1)S(1)}, u32[]{:S(2)}, u32[]{:S(2)}) collective-permute-start(bf16[256,768]{1,0:T(8,128)(2,1)S(1)} %broadcast_select_fusion.2), channel_id=1, source_target_pairs={{0,2},{6,4},{1,3},{7,5},{8,10},{14,12},{9,11},{15,13},{16,18},{22,... | collective-permute-start | bytes 1179656 | tf_op jit(solution)/shard_map/ppermute | solution.py:447
  221.3 6.1 %collective-permute-done.39 = bf16[256,768]{1,0:T(8,128)(2,1)S(1)} collective-permute-done((bf16[256,768]{1,0:T(8,128)(2,1)S(1)}, bf16[256,768]{1,0:T(8,128)(2,1)S(1)}, u32[]{:S(2)}, u32[]{:S(2)}) %collective-permute-start.39) | collective-permute-done | bytes 393248 | tf_op jit(solution)/shard_map/ppermute | solution.py:447
  229.5 2.2 collective-permute-start.40
  231.7 1.5 weave.1
  233.2 2.1 collective-permute-start.35
  235.7 1.9 collective-permute-start.38
  237.6 5.1 %collective-permute-done.35 = bf16[2,2,32,1344]{3,2,1,0:T(8,128)(2,1)S(1)} collective-permute-done((bf16[2,2,32,1344]{3,2,1,0:T(8,128)(2,1)S(1)}, bf16[2,2,32,1344]{3,2,1,0:T(8,128)(2,1)S(1)}, u32[]{:S(2)}, u32[]{:S(2)}) %collective-permute-start.35) | collective-permute-done | bytes 344096 | tf_op jit(solution)/shard_map/ppermute | solution.py:391
  244.7 3.7 %collective-permute-done.36 = bf16[2,32,1344]{2,1,0:T(8,128)(2,1)S(1)} collective-permute-done((bf16[2,32,1344]{2,1,0:T(8,128)(2,1)S(1)}, bf16[2,32,1344]{2,1,0:T(8,128)(2,1)S(1)}, u32[]{:S(2)}, u32[]{:S(2)}) %collective-permute-start.36) | collective-permute-done | bytes 172064 | tf_op jit(solution)/shard_map/ppermute | solution.py:391
  249.2 2.6 %collective-permute-start.43 = (bf16[32,1344]{1,0:T(8,128)(2,1)S(1)}, bf16[32,1344]{1,0:T(8,128)(2,1)S(1)}, u32[]{:S(2)}, u32[]{:S(2)}) collective-permute-start(bf16[32,1344]{1,0:T(8,128)(2,1)S(1)} %get-tuple-element.170), channel_id=1, source_target_pairs={{0,4},{2,6},{4,0},{6,2},{1,5},{3,7},{5,1},{7,3},{8,12},{10,14},{12... | collective-permute-start | bytes 258056 | tf_op jit(solution)/shard_map/ppermute | solution.py:391
  252.6 2.1 finish.1
  255.1 1.9 collective-permute-done.43.p2_ref
  (298 shorter events, 54.3 us)
Async XLA Ops:
  4.5 8.9 %collective-permute-start = (bf16[32,1344]{1,0:T(8,128)(2,1)S(1)}, bf16[32,1344]{1,0:T(8,128)(2,1)S(1)}, u32[]{:S(2)}, u32[]{:S(2)}) collective-permute-start(bf16[32,1344]{1,0:T(8,128)(2,1)S(1)} %get-tuple-element.178), channel_id=1, source_target_pairs={{0,2},{2,4},{4,6},{6,0},{1,3},{3,5},{5,7},{7,1},{8,10},{10,12},{12... | collective-permute-start | bytes 258056 | tf_op jit(solution)/shard_map/ppermute | solution.py:391
  7.6 8.6 %collective-permute-start.1 = (bf16[32,1344]{1,0:T(8,128)(2,1)S(1)}, bf16[32,1344]{1,0:T(8,128)(2,1)S(1)}, u32[]{:S(2)}, u32[]{:S(2)}) collective-permute-start(bf16[32,1344]{1,0:T(8,128)(2,1)S(1)} %get-tuple-element.177), channel_id=1, source_target_pairs={{0,4},{2,6},{4,0},{6,2},{1,5},{3,7},{5,1},{7,3},{8,12},{10,14},{12... | collective-permute-start | bytes 258056 | tf_op jit(solution)/shard_map/ppermute | solution.py:391
  10.2 6.2 %collective-permute-start.2 = (bf16[32,1344]{1,0:T(8,128)(2,1)S(1)}, bf16[32,1344]{1,0:T(8,128)(2,1)S(1)}, u32[]{:S(2)}, u32[]{:S(2)}) collective-permute-start(bf16[32,1344]{1,0:T(8,128)(2,1)S(1)} %get-tuple-element.176), channel_id=1, source_target_pairs={{0,6},{2,0},{4,2},{6,4},{1,7},{3,1},{5,3},{7,5},{8,14},{10,8},{12,... | collective-permute-start | bytes 258056 | tf_op jit(solution)/shard_map/ppermute | solution.py:391
  16.5 8.5 %collective-permute-start.11 = (bf16[2,32,1344]{2,1,0:T(8,128)(2,1)S(1)}, bf16[2,32,1344]{2,1,0:T(8,128)(2,1)S(1)}, u32[]{:S(2)}, u32[]{:S(2)}) collective-permute-start(bf16[2,32,1344]{2,1,0:T(8,128)(2,1)S(1)} %pad_maximum_fusion.11), channel_id=1, source_target_pairs={{0,8},{8,0},{1,9},{9,1},{2,10},{10,2},{3,11},{11,3},{4,12},{12,4},... | collective-permute-start | bytes 516104 | tf_op jit(solution)/shard_map/ppermute | solution.py:391
  18.1 7.0 %collective-permute-start.13 = (bf16[2,32,1344]{2,1,0:T(8,128)(2,1)S(1)}, bf16[2,32,1344]{2,1,0:T(8,128)(2,1)S(1)}, u32[]{:S(2)}, u32[]{:S(2)}) collective-permute-start(bf16[2,32,1344]{2,1,0:T(8,128)(2,1)S(1)} %pad_maximum_fusion.12), channel_id=1, source_target_pairs={{0,16},{16,0},{1,17},{17,1},{2,18},{18,2},{3,19},{19,3},{4,20},{20... | collective-permute-start | bytes 516104 | tf_op jit(solution)/shard_map/ppermute | solution.py:391
  20.4 27.5 %collective-permute-start.5 = (bf16[192,768]{1,0:T(8,128)(2,1)}, bf16[192,768]{1,0:T(8,128)(2,1)}, u32[]{:S(2)}, u32[]{:S(2)}) collective-permute-start(bf16[192,768]{1,0:T(8,128)(2,1)} %pad_maximum_fusion.9), channel_id=1, source_target_pairs={{0,2},{2,4},{4,6},{6,0},{1,3},{3,5},{5,7},{7,1},{8,10},{10,12},{12... | collective-permute-start | bytes 884744 | tf_op jit(solution)/shard_map/ppermute | solution.py:391
  22.6 25.3 %collective-permute-start.6 = (bf16[192,768]{1,0:T(8,128)(2,1)}, bf16[192,768]{1,0:T(8,128)(2,1)}, u32[]{:S(2)}, u32[]{:S(2)}) collective-permute-start(bf16[192,768]{1,0:T(8,128)(2,1)} %pad_maximum_fusion.9), channel_id=1, source_target_pairs={{0,6},{2,0},{4,2},{6,4},{1,7},{3,1},{5,3},{7,5},{8,14},{10,8},{12,... | collective-permute-start | bytes 884744 | tf_op jit(solution)/shard_map/ppermute | solution.py:391
  24.3 29.5 %collective-permute-start.10 = (bf16[192,768]{1,0:T(8,128)(2,1)}, bf16[192,768]{1,0:T(8,128)(2,1)}, u32[]{:S(2)}, u32[]{:S(2)}) collective-permute-start(bf16[192,768]{1,0:T(8,128)(2,1)} %pad_maximum_fusion.9), channel_id=1, source_target_pairs={{0,4},{2,6},{4,0},{6,2},{1,5},{3,7},{5,1},{7,3},{8,12},{10,14},{12... | collective-permute-start | bytes 884744 | tf_op jit(solution)/shard_map/ppermute | solution.py:391
  25.1 22.2 %collective-permute-start.3 = (f32[4,256]{1,0:T(4,128)S(1)}, f32[4,256]{1,0:T(4,128)S(1)}, u32[]{:S(2)}, u32[]{:S(2)}) collective-permute-start(f32[4,256]{1,0:T(4,128)S(1)} %bitcast.240), channel_id=1, source_target_pairs={{0,1},{1,0},{2,3},{3,2},{4,5},{5,4},{6,7},{7,6},{8,9},{9,8},{10,11... | collective-permute-start | bytes 12296 | tf_op jit(solution)/shard_map/ppermute | solution.py:391
  25.3 10.9 %collective-permute-start.12 = (bf16[2,2,32,1344]{3,2,1,0:T(8,128)(2,1)S(1)}, bf16[2,2,32,1344]{3,2,1,0:T(8,128)(2,1)S(1)}, u32[]{:S(2)}, u32[]{:S(2)}) collective-permute-start(bf16[2,2,32,1344]{3,2,1,0:T(8,128)(2,1)S(1)} %pad_maximum_fusion.7), channel_id=1, source_target_pairs={{0,16},{16,0},{1,17},{17,1},{2,18},{18,2},{3,19},{19,3},{4,20},{20... | collective-permute-start | bytes 1032200 | tf_op jit(solution)/shard_map/ppermute | solution.py:391
  36.2 10.1 %collective-permute-start.14 = (bf16[2,2,32,1344]{3,2,1,0:T(8,128)(2,1)S(1)}, bf16[2,2,32,1344]{3,2,1,0:T(8,128)(2,1)S(1)}, u32[]{:S(2)}, u32[]{:S(2)}) collective-permute-start(bf16[2,2,32,1344]{3,2,1,0:T(8,128)(2,1)S(1)} %pad_maximum_fusion.8), channel_id=1, source_target_pairs={{0,8},{8,0},{1,9},{9,1},{2,10},{10,2},{3,11},{11,3},{4,12},{12,4},... | collective-permute-start | bytes 1032200 | tf_op jit(solution)/shard_map/ppermute | solution.py:391
  47.3 10.6 %collective-permute-start.15 = (bf16[2,2,4,32,1344]{4,3,2,1,0:T(8,128)(2,1)S(1)}, bf16[2,2,4,32,1344]{4,3,2,1,0:T(8,128)(2,1)}, u32[]{:S(2)}, u32[]{:S(2)}) collective-permute-start(bf16[2,2,4,32,1344]{4,3,2,1,0:T(8,128)(2,1)S(1)} %maximum_maximum_fusion.1), channel_id=1, source_target_pairs={{0,1},{1,0},{2,3},{3,2},{4,5},{5,4},{6,7},{7,6},{8,9},{9,8},{10,11... | collective-permute-start | bytes 4128776 | tf_op jit(solution)/shard_map/ppermute | solution.py:391
  48.0 16.7 %collective-permute-start.7 = (bf16[256,768]{1,0:T(8,128)(2,1)S(1)}, bf16[256,768]{1,0:T(8,128)(2,1)S(1)}, u32[]{:S(2)}, u32[]{:S(2)}) collective-permute-start(bf16[256,768]{1,0:T(8,128)(2,1)S(1)} %bitcast.234), channel_id=1, source_target_pairs={{0,2},{2,4},{4,6},{6,0},{1,3},{3,5},{5,7},{7,1},{8,10},{10,12},{12... | collective-permute-start | bytes 1179656 | tf_op jit(solution)/shard_map/ppermute | solution.py:391
  50.1 28.3 %collective-permute-start.8 = (bf16[256,768]{1,0:T(8,128)(2,1)S(1)}, bf16[256,768]{1,0:T(8,128)(2,1)S(1)}, u32[]{:S(2)}, u32[]{:S(2)}) collective-permute-start(bf16[256,768]{1,0:T(8,128)(2,1)S(1)} %bitcast.235), channel_id=1, source_target_pairs={{0,4},{2,6},{4,0},{6,2},{1,5},{3,7},{5,1},{7,3},{8,12},{10,14},{12... | collective-permute-start | bytes 1179656 | tf_op jit(solution)/shard_map/ppermute | solution.py:391
  51.2 27.1 %collective-permute-start.9 = (bf16[256,768]{1,0:T(8,128)(2,1)S(1)}, bf16[256,768]{1,0:T(8,128)(2,1)S(1)}, u32[]{:S(2)}, u32[]{:S(2)}) collective-permute-start(bf16[256,768]{1,0:T(8,128)(2,1)S(1)} %bitcast.236), channel_id=1, source_target_pairs={{0,6},{2,0},{4,2},{6,4},{1,7},{3,1},{5,3},{7,5},{8,14},{10,8},{12,... | collective-permute-start | bytes 1179656 | tf_op jit(solution)/shard_map/ppermute | solution.py:391
  63.4 20.4 %collective-permute-start.22 = (bf16[2,192,768]{2,1,0:T(8,128)(2,1)S(1)}, bf16[2,192,768]{2,1,0:T(8,128)(2,1)S(1)}, u32[]{:S(2)}, u32[]{:S(2)}) collective-permute-start(bf16[2,192,768]{2,1,0:T(8,128)(2,1)S(1)} %get-tuple-element.149), channel_id=1, source_target_pairs={{0,8},{8,0},{1,9},{9,1},{2,10},{10,2},{3,11},{11,3},{4,12},{12,4},... | collective-permute-start | bytes 1769480 | tf_op jit(solution)/shard_map/ppermute | solution.py:391
  64.0 19.8 %collective-permute-start.24 = (bf16[2,192,768]{2,1,0:T(8,128)(2,1)S(1)}, bf16[2,192,768]{2,1,0:T(8,128)(2,1)S(1)}, u32[]{:S(2)}, u32[]{:S(2)}) collective-permute-start(bf16[2,192,768]{2,1,0:T(8,128)(2,1)S(1)} %get-tuple-element.150), channel_id=1, source_target_pairs={{0,16},{16,0},{1,17},{17,1},{2,18},{18,2},{3,19},{19,3},{4,20},{20... | collective-permute-start | bytes 1769480 | tf_op jit(solution)/shard_map/ppermute | solution.py:391
  84.1 34.8 %collective-permute-start.23 = (bf16[2,2,192,768]{3,2,1,0:T(8,128)(2,1)S(1)}, bf16[2,2,192,768]{3,2,1,0:T(8,128)(2,1)S(1)}, u32[]{:S(2)}, u32[]{:S(2)}) collective-permute-start(bf16[2,2,192,768]{3,2,1,0:T(8,128)(2,1)S(1)} %pad_maximum_fusion.3), channel_id=1, source_target_pairs={{0,16},{16,0},{1,17},{17,1},{2,18},{18,2},{3,19},{19,3},{4,20},{20... | collective-permute-start | bytes 3538952 | tf_op jit(solution)/shard_map/ppermute | solution.py:391
  84.8 34.3 %collective-permute-start.25 = (bf16[2,2,192,768]{3,2,1,0:T(8,128)(2,1)S(1)}, bf16[2,2,192,768]{3,2,1,0:T(8,128)(2,1)S(1)}, u32[]{:S(2)}, u32[]{:S(2)}) collective-permute-start(bf16[2,2,192,768]{3,2,1,0:T(8,128)(2,1)S(1)} %pad_maximum_fusion.4), channel_id=1, source_target_pairs={{0,8},{8,0},{1,9},{9,1},{2,10},{10,2},{3,11},{11,3},{4,12},{12,4},... | collective-permute-start | bytes 3538952 | tf_op jit(solution)/shard_map/ppermute | solution.py:391
  97.1 14.5 %collective-permute-start.17 = (bf16[256,192]{1,0:T(8,128)(2,1)S(1)}, bf16[256,192]{1,0:T(8,128)(2,1)S(1)}, u32[]{:S(2)}, u32[]{:S(2)}) collective-permute-start(bf16[256,192]{1,0:T(8,128)(2,1)S(1)} %get-tuple-element.167), channel_id=1, source_target_pairs={{0,2},{2,4},{4,6},{6,0},{1,3},{3,5},{5,7},{7,1},{8,10},{10,12},{12... | collective-permute-start | bytes 294920 | tf_op jit(solution)/shard_map/ppermute | solution.py:391
  106.0 11.3 %collective-permute-start.18 = (bf16[256,192]{1,0:T(8,128)(2,1)S(1)}, bf16[256,192]{1,0:T(8,128)(2,1)S(1)}, u32[]{:S(2)}, u32[]{:S(2)}) collective-permute-start(bf16[256,192]{1,0:T(8,128)(2,1)S(1)} %get-tuple-element.166), channel_id=1, source_target_pairs={{0,4},{2,6},{4,0},{6,2},{1,5},{3,7},{5,1},{7,3},{8,12},{10,14},{12... | collective-permute-start | bytes 294920 | tf_op jit(solution)/shard_map/ppermute | solution.py:391
  107.9 9.4 %collective-permute-start.19 = (bf16[256,192]{1,0:T(8,128)(2,1)S(1)}, bf16[256,192]{1,0:T(8,128)(2,1)S(1)}, u32[]{:S(2)}, u32[]{:S(2)}) collective-permute-start(bf16[256,192]{1,0:T(8,128)(2,1)S(1)} %get-tuple-element.165), channel_id=1, source_target_pairs={{0,6},{2,0},{4,2},{6,4},{1,7},{3,1},{5,3},{7,5},{8,14},{10,8},{12,... | collective-permute-start | bytes 294920 | tf_op jit(solution)/shard_map/ppermute | solution.py:391
  111.6 8.6 %collective-permute-start.21 = (bf16[256,768]{1,0:T(8,128)(2,1)S(1)}, bf16[256,768]{1,0:T(8,128)(2,1)S(1)}, u32[]{:S(2)}, u32[]{:S(2)}) collective-permute-start(bf16[256,768]{1,0:T(8,128)(2,1)S(1)} %bitcast.245), channel_id=1, source_target_pairs={{0,1},{1,0},{2,3},{3,2},{4,5},{5,4},{6,7},{7,6},{8,9},{9,8},{10,11... | collective-permute-start | bytes 1179656 | tf_op jit(solution)/shard_map/ppermute | solution.py:391
  127.5 6.3 %collective-permute-start.26 = (bf16[2,256,768]{2,1,0:T(8,128)(2,1)S(1)}, bf16[2,256,768]{2,1,0:T(8,128)(2,1)S(1)}, u32[]{:S(2)}, u32[]{:S(2)}) collective-permute-start(bf16[2,256,768]{2,1,0:T(8,128)(2,1)S(1)} %get-tuple-element.81), channel_id=1, source_target_pairs={{0,1},{1,0},{2,3},{3,2},{4,5},{5,4},{6,7},{7,6},{8,9},{9,8},{10,11... | collective-permute-start | bytes 2359304 | tf_op jit(solution)/shard_map/ppermute | solution.py:391
  133.8 36.5 %collective-permute-start.31 = (bf16[2,2,192,768]{3,2,1,0:T(8,128)(2,1)}, bf16[2,2,192,768]{3,2,1,0:T(8,128)(2,1)}, u32[]{:S(2)}, u32[]{:S(2)}) collective-permute-start(bf16[2,2,192,768]{3,2,1,0:T(8,128)(2,1)} %get-tuple-element.96), channel_id=1, source_target_pairs={{0,8},{8,0},{1,9},{9,1},{2,10},{10,2},{3,11},{11,3},{4,12},{12,4},... | collective-permute-start | bytes 3538952 | tf_op jit(solution)/shard_map/ppermute | solution.py:391
  138.4 8.8 %collective-permute-start.27 = (bf16[256,192]{1,0:T(8,128)(2,1)}, bf16[256,192]{1,0:T(8,128)(2,1)}, u32[]{:S(2)}, u32[]{:S(2)}) collective-permute-start(bf16[256,192]{1,0:T(8,128)(2,1)} %get-tuple-element.85), channel_id=1, source_target_pairs={{0,2},{2,4},{4,6},{6,0},{1,3},{3,5},{5,7},{7,1},{8,10},{10,12},{12... | collective-permute-start | bytes 294920 | tf_op jit(solution)/shard_map/ppermute | solution.py:391
  141.7 10.7 %collective-permute-start.28 = (bf16[256,192]{1,0:T(8,128)(2,1)}, bf16[256,192]{1,0:T(8,128)(2,1)}, u32[]{:S(2)}, u32[]{:S(2)}) collective-permute-start(bf16[256,192]{1,0:T(8,128)(2,1)} %get-tuple-element.86), channel_id=1, source_target_pairs={{0,4},{2,6},{4,0},{6,2},{1,5},{3,7},{5,1},{7,3},{8,12},{10,14},{12... | collective-permute-start | bytes 294920 | tf_op jit(solution)/shard_map/ppermute | solution.py:391
  143.1 9.3 %collective-permute-start.29 = (bf16[256,192]{1,0:T(8,128)(2,1)}, bf16[256,192]{1,0:T(8,128)(2,1)}, u32[]{:S(2)}, u32[]{:S(2)}) collective-permute-start(bf16[256,192]{1,0:T(8,128)(2,1)} %get-tuple-element.87), channel_id=1, source_target_pairs={{0,6},{2,0},{4,2},{6,4},{1,7},{3,1},{5,3},{7,5},{8,14},{10,8},{12,... | collective-permute-start | bytes 294920 | tf_op jit(solution)/shard_map/ppermute | solution.py:391
  144.1 27.9 %collective-permute-start.30 = (bf16[2,2,192,768]{3,2,1,0:T(8,128)(2,1)}, bf16[2,2,192,768]{3,2,1,0:T(8,128)(2,1)S(1)}, u32[]{:S(2)}, u32[]{:S(2)}) collective-permute-start(bf16[2,2,192,768]{3,2,1,0:T(8,128)(2,1)} %copy-done.27), channel_id=1, source_target_pairs={{0,16},{16,0},{1,17},{17,1},{2,18},{18,2},{3,19},{19,3},{4,20},{20... | collective-permute-start | bytes 3538952 | tf_op jit(solution)/shard_map/ppermute | solution.py:391
  170.2 24.8 %collective-permute-start.32 = (bf16[1024,384]{1,0:T(8,128)(2,1)S(1)}, bf16[1024,384]{1,0:T(8,128)(2,1)S(1)}, u32[]{:S(2)}, u32[]{:S(2)}) collective-permute-start(bf16[1024,384]{1,0:T(8,128)(2,1)S(1)} %get-tuple-element.101), channel_id=1, source_target_pairs={{0,1},{1,0},{2,3},{3,2},{4,5},{5,4},{6,7},{7,6},{8,9},{9,8},{10,11... | collective-permute-start | bytes 2359304 | tf_op jit(solution)/shard_map/ppermute | solution.py:391
  172.3 15.6 %collective-permute-start.46 = (bf16[2,192,768]{2,1,0:T(8,128)(2,1)S(1)}, bf16[2,192,768]{2,1,0:T(8,128)(2,1)S(1)}, u32[]{:S(2)}, u32[]{:S(2)}) collective-permute-start(bf16[2,192,768]{2,1,0:T(8,128)(2,1)S(1)} %fusion.2), channel_id=1, source_target_pairs={{0,16},{16,0},{1,17},{17,1},{2,18},{18,2},{3,19},{19,3},{4,20},{20... | collective-permute-start | bytes 1769480 | tf_op jit(solution)/shard_map/ppermute | solution.py:391
  173.8 15.0 %collective-permute-start.45 = (bf16[2,192,768]{2,1,0:T(8,128)(2,1)S(1)}, bf16[2,192,768]{2,1,0:T(8,128)(2,1)S(1)}, u32[]{:S(2)}, u32[]{:S(2)}) collective-permute-start(bf16[2,192,768]{2,1,0:T(8,128)(2,1)S(1)} %fusion.1), channel_id=1, source_target_pairs={{0,8},{8,0},{1,9},{9,1},{2,10},{10,2},{3,11},{11,3},{4,12},{12,4},... | collective-permute-start | bytes 1769480 | tf_op jit(solution)/shard_map/ppermute | solution.py:391
  189.1 14.6 %collective-permute-start.47 = (bf16[192,768]{1,0:T(8,128)(2,1)S(1)}, bf16[192,768]{1,0:T(8,128)(2,1)S(1)}, u32[]{:S(2)}, u32[]{:S(2)}) collective-permute-start(bf16[192,768]{1,0:T(8,128)(2,1)S(1)} %get-tuple-element.144), channel_id=1, source_target_pairs={{0,2},{2,4},{4,6},{6,0},{1,3},{3,5},{5,7},{7,1},{8,10},{10,12},{12... | collective-permute-start | bytes 884744 | tf_op jit(solution)/shard_map/ppermute | solution.py:391
  192.6 20.4 %collective-permute-start.48 = (bf16[192,768]{1,0:T(8,128)(2,1)S(1)}, bf16[192,768]{1,0:T(8,128)(2,1)S(1)}, u32[]{:S(2)}, u32[]{:S(2)}) collective-permute-start(bf16[192,768]{1,0:T(8,128)(2,1)S(1)} %get-tuple-element.146), channel_id=1, source_target_pairs={{0,4},{2,6},{4,0},{6,2},{1,5},{3,7},{5,1},{7,3},{8,12},{10,14},{12... | collective-permute-start | bytes 884744 | tf_op jit(solution)/shard_map/ppermute | solution.py:391
  193.6 27.4 %collective-permute-start.49 = (bf16[192,768]{1,0:T(8,128)(2,1)S(1)}, bf16[192,768]{1,0:T(8,128)(2,1)S(1)}, u32[]{:S(2)}, u32[]{:S(2)}) collective-permute-start(bf16[192,768]{1,0:T(8,128)(2,1)S(1)} %get-tuple-element.145), channel_id=1, source_target_pairs={{0,6},{2,0},{4,2},{6,4},{1,7},{3,1},{5,3},{7,5},{8,14},{10,8},{12,... | collective-permute-start | bytes 884744 | tf_op jit(solution)/shard_map/ppermute | solution.py:391
  202.3 25.2 %collective-permute-start.34 = (bf16[16,32,1344]{2,1,0:T(8,128)(2,1)S(1)}, bf16[16,32,1344]{2,1,0:T(8,128)(2,1)S(1)}, u32[]{:S(2)}, u32[]{:S(2)}) collective-permute-start(bf16[16,32,1344]{2,1,0:T(8,128)(2,1)S(1)} %get-tuple-element.113), channel_id=1, source_target_pairs={{0,1},{1,0},{2,3},{3,2},{4,5},{5,4},{6,7},{7,6},{8,9},{9,8},{10,11... | collective-permute-start | bytes 4128776 | tf_op jit(solution)/shard_map/ppermute | solution.py:391
  202.4 46.0 %collective-permute-start.41 = (bf16[256,768]{1,0:T(8,128)(2,1)S(1)}, bf16[256,768]{1,0:T(8,128)(2,1)S(1)}, u32[]{:S(2)}, u32[]{:S(2)}) collective-permute-start(bf16[256,768]{1,0:T(8,128)(2,1)S(1)} %get-tuple-element.115), channel_id=1, source_target_pairs={{2,0},{4,2},{6,4},{3,1},{5,3},{7,5},{10,8},{12,10},{14,12},{11,9},... | collective-permute-start | bytes 1179656 | tf_op jit(solution)/shard_map/ppermute | solution.py:451
  203.8 48.7 %collective-permute-start.33 = (bf16[256,768]{1,0:T(8,128)(2,1)S(1)}, bf16[256,768]{1,0:T(8,128)(2,1)S(1)}, u32[]{:S(2)}, u32[]{:S(2)}) collective-permute-start(bf16[256,768]{1,0:T(8,128)(2,1)S(1)} %get-tuple-element.104), channel_id=1, source_target_pairs={{0,2},{2,4},{4,6},{1,3},{3,5},{5,7},{8,10},{10,12},{12,14},{9,11},... | collective-permute-start | bytes 1179656 | tf_op jit(solution)/shard_map/ppermute | solution.py:450
  212.9 14.5 %collective-permute-start.39 = (bf16[256,768]{1,0:T(8,128)(2,1)S(1)}, bf16[256,768]{1,0:T(8,128)(2,1)S(1)}, u32[]{:S(2)}, u32[]{:S(2)}) collective-permute-start(bf16[256,768]{1,0:T(8,128)(2,1)S(1)} %broadcast_select_fusion.2), channel_id=1, source_target_pairs={{0,2},{6,4},{1,3},{7,5},{8,10},{14,12},{9,11},{15,13},{16,18},{22,... | collective-permute-start | bytes 1179656 | tf_op jit(solution)/shard_map/ppermute | solution.py:447
  221.3 10.4 %collective-permute-start.50 = (bf16[24,1536]{1,0:T(8,128)(2,1)S(1)}, bf16[24,1536]{1,0:T(8,128)(2,1)S(1)}, u32[]{:S(2)}, u32[]{:S(2)}) collective-permute-start(bf16[24,1536]{1,0:T(8,128)(2,1)S(1)} %fusion.18), channel_id=1, source_target_pairs={{0,1},{1,0},{2,3},{3,2},{4,5},{5,4},{6,7},{7,6},{8,9},{9,8},{10,11... | collective-permute-start | bytes 221192 | tf_op jit(solution)/shard_map/ppermute | solution.py:391
  228.1 7.5 %collective-permute-start.37 = (bf16[2,2,32,1344]{3,2,1,0:T(8,128)(2,1)S(1)}, bf16[2,2,32,1344]{3,2,1,0:T(8,128)(2,1)S(1)}, u32[]{:S(2)}, u32[]{:S(2)}) collective-permute-start(bf16[2,2,32,1344]{3,2,1,0:T(8,128)(2,1)S(1)} %dynamic-slice_bitcast_fusion), channel_id=1, source_target_pairs={{0,8},{8,0},{1,9},{9,1},{2,10},{10,2},{3,11},{11,3},{4,12},{12,4},... | collective-permute-start | bytes 1032200 | tf_op jit(solution)/shard_map/ppermute | solution.py:391
  229.5 19.0 %collective-permute-start.40 = (bf16[256,768]{1,0:T(8,128)(2,1)S(1)}, bf16[256,768]{1,0:T(8,128)(2,1)S(1)}, u32[]{:S(2)}, u32[]{:S(2)}) collective-permute-start(bf16[256,768]{1,0:T(8,128)(2,1)S(1)} %add_convert_fusion.1), channel_id=1, source_target_pairs={{0,4},{2,6},{4,0},{6,2},{1,5},{3,7},{5,1},{7,3},{8,12},{10,14},{12... | collective-permute-start | bytes 1179656 | tf_op jit(solution)/shard_map/ppermute | solution.py:391
  233.2 9.5 %collective-permute-start.35 = (bf16[2,2,32,1344]{3,2,1,0:T(8,128)(2,1)S(1)}, bf16[2,2,32,1344]{3,2,1,0:T(8,128)(2,1)S(1)}, u32[]{:S(2)}, u32[]{:S(2)}) collective-permute-start(bf16[2,2,32,1344]{3,2,1,0:T(8,128)(2,1)S(1)} %dynamic-slice_bitcast_fusion.1), channel_id=1, source_target_pairs={{0,16},{16,0},{1,17},{17,1},{2,18},{18,2},{3,19},{19,3},{4,20},{20... | collective-permute-start | bytes 1032200 | tf_op jit(solution)/shard_map/ppermute | solution.py:391
  235.7 8.9 %collective-permute-start.38 = (bf16[2,32,1344]{2,1,0:T(8,128)(2,1)S(1)}, bf16[2,32,1344]{2,1,0:T(8,128)(2,1)S(1)}, u32[]{:S(2)}, u32[]{:S(2)}) collective-permute-start(bf16[2,32,1344]{2,1,0:T(8,128)(2,1)S(1)} %fusion.9), channel_id=1, source_target_pairs={{0,16},{16,0},{1,17},{17,1},{2,18},{18,2},{3,19},{19,3},{4,20},{20... | collective-permute-start | bytes 516104 | tf_op jit(solution)/shard_map/ppermute | solution.py:391
  242.8 5.6 %collective-permute-start.36 = (bf16[2,32,1344]{2,1,0:T(8,128)(2,1)S(1)}, bf16[2,32,1344]{2,1,0:T(8,128)(2,1)S(1)}, u32[]{:S(2)}, u32[]{:S(2)}) collective-permute-start(bf16[2,32,1344]{2,1,0:T(8,128)(2,1)S(1)} %fusion.8), channel_id=1, source_target_pairs={{0,8},{8,0},{1,9},{9,1},{2,10},{10,2},{3,11},{11,3},{4,12},{12,4},... | collective-permute-start | bytes 516104 | tf_op jit(solution)/shard_map/ppermute | solution.py:391
  248.6 6.5 %collective-permute-start.42 = (bf16[32,1344]{1,0:T(8,128)(2,1)S(1)}, bf16[32,1344]{1,0:T(8,128)(2,1)S(1)}, u32[]{:S(2)}, u32[]{:S(2)}) collective-permute-start(bf16[32,1344]{1,0:T(8,128)(2,1)S(1)} %get-tuple-element.171), channel_id=1, source_target_pairs={{0,2},{2,4},{4,6},{6,0},{1,3},{3,5},{5,7},{7,1},{8,10},{10,12},{12... | collective-permute-start | bytes 258056 | tf_op jit(solution)/shard_map/ppermute | solution.py:391
  249.2 7.9 %collective-permute-start.43 = (bf16[32,1344]{1,0:T(8,128)(2,1)S(1)}, bf16[32,1344]{1,0:T(8,128)(2,1)S(1)}, u32[]{:S(2)}, u32[]{:S(2)}) collective-permute-start(bf16[32,1344]{1,0:T(8,128)(2,1)S(1)} %get-tuple-element.170), channel_id=1, source_target_pairs={{0,4},{2,6},{4,0},{6,2},{1,5},{3,7},{5,1},{7,3},{8,12},{10,14},{12... | collective-permute-start | bytes 258056 | tf_op jit(solution)/shard_map/ppermute | solution.py:391
  251.8 5.3 %collective-permute-start.44 = (bf16[32,1344]{1,0:T(8,128)(2,1)S(1)}, bf16[32,1344]{1,0:T(8,128)(2,1)S(1)}, u32[]{:S(2)}, u32[]{:S(2)}) collective-permute-start(bf16[32,1344]{1,0:T(8,128)(2,1)S(1)} %get-tuple-element.169), channel_id=1, source_target_pairs={{0,6},{2,0},{4,2},{6,4},{1,7},{3,1},{5,3},{7,5},{8,14},{10,8},{12,... | collective-permute-start | bytes 258056 | tf_op jit(solution)/shard_map/ppermute | solution.py:391
  (62 other events, 428.2 us)
